TPU v7x, 32 devices: a whole 2x2x4 slice. The times are simulated.
32 devices in a mesh: img: 4 (over z), ty: 4 (over y, core), tx: 2 (over x).
Axes of the slice: x: 2, y: 2, z: 4, core: 2. Of those that a mesh axis runs over, the one named last changes fastest.
Arguments:
- block_in: float32 [4, 64, 16, 1152], P('img', 'ty', 'tx'), may hold values from -6 to 6
- bucket: int32 [4], P('img'), may hold values from 0 to 31
- tile_anchor: int32 [4, 4, 2, 2], P('img', 'ty', 'tx'), may hold values from 0 to 255
- cond_table: float32 [32, 1152], replicated, may hold values from -6 to 6
- mod_weight: bfloat16 [1152, 6912], P(None, ('ty', 'tx')), may hold values from -0.1875 to 0.1875
- mod_bias: float32 [6912], P(('ty', 'tx')), may hold values from -3 to 3
- qkv_weight: bfloat16 [1152, 3456], replicated, may hold values from -0.1875 to 0.1875
- query_gain: float32 [72], replicated, may hold values from 0.5 to 1.5
- key_gain: float32 [72], replicated, may hold values from 0.5 to 1.5
- out_weight: bfloat16 [1152, 1152], replicated, may hold values from -3.5 to 3.5
- gate_up_weight: bfloat16 [1152, 6144], replicated, may hold values from -0.1875 to 0.1875
- down_weight: bfloat16 [3072, 1152], replicated, may hold values from -0.109375 to 0.109375
- cotangent: float32 [4, 64, 16, 1152], P('img', 'ty', 'tx'), may hold values from -6 to 6
Outputs:
- output: float32 [4, 64, 16, 1152], P('img', 'ty', 'tx')
- in_grad: float32 [4, 64, 16, 1152], P('img', 'ty', 'tx')
- table_grad: float32 [32, 1152], P(('ty', 'tx'), 'img')
- modw_grad: float32 [1152, 6912], P('img', ('ty', 'tx'))
- modb_grad: float32 [6912], P(('ty', 'tx'))
- qkv_grad: float32 [1152, 3456], P(('ty', 'tx'), 'img')
- qgain_grad: float32 [72], replicated
- kgain_grad: float32 [72], replicated
- outw_grad: float32 [1152, 1152], P(('ty', 'tx'), 'img')
- gateup_grad: float32 [1152, 6144], P(('ty', 'tx'), 'img')
- down_grad: float32 [3072, 1152], P(('ty', 'tx'), 'img')
All inputs are finite; a program needn't handle non-finite values.
Results may differ from a plain program's by a relative error of at most 0.017.
Values may be sent and summed in bfloat16 or wider, within the bound.
No kernel may reach another device: no remote copies, remote signals or barrier semaphores. Data moves between devices by JAX's collectives and lax.ppermute only.
A program may use at most 256 MiB of HBM per device.

v0:
```python
import math

import jax
import jax.numpy as jnp
from jax import lax
from jax.sharding import PartitionSpec as P

HEADS = 16
HD = 72


EPS = 1e-06
PRECISE = lax.Precision.HIGHEST


def normed(value):
    return value * lax.rsqrt(jnp.mean(value * value, axis=-1, keepdims=True) + EPS)


def norm_back(value, upstream):
    inverse = lax.rsqrt(jnp.mean(value * value, axis=-1, keepdims=True) + EPS)
    unit_value = value * inverse
    return inverse * (
        upstream - unit_value * jnp.mean(upstream * unit_value, axis=-1, keepdims=True)
    )


def rotate(value, tables, turning):
    row_cos, row_sin, col_cos, col_sin = tables
    quarter = value.shape[-1] // 4
    first = value[..., :quarter]
    second = value[..., quarter : 2 * quarter]
    third = value[..., 2 * quarter : 3 * quarter]
    fourth = value[..., 3 * quarter :]
    row_turn = turning * row_sin
    col_turn = turning * col_sin
    return jnp.concatenate(
        [
            first * row_cos - second * row_turn,
            second * row_cos + first * row_turn,
            third * col_cos - fourth * col_turn,
            fourth * col_cos + third * col_turn,
        ],
        axis=-1,
    )


def silu_slope(value):
    sigma = jax.nn.sigmoid(value)
    return sigma * (1.0 + value * (1.0 - sigma))


def product(left, right):
    return jnp.einsum("ik,kj->ij", left, right, preferred_element_type=jnp.float32)


def product_rt(left, right):
    return jnp.einsum("ik,jk->ij", left, right, preferred_element_type=jnp.float32)


def product_lt(left, right):
    return jnp.einsum("ki,kj->ij", left, right, preferred_element_type=jnp.float32)


def on_device(
    block_in,
    bucket,
    tile_anchor,
    cond_table,
    mod_weight,
    mod_bias,
    qkv_weight,
    query_gain,
    key_gain,
    out_weight,
    gate_up_weight,
    down_weight,
    cotangent,
):
    images, tile_rows, tile_cols, model_width = block_in.shape
    tokens = tile_rows * tile_cols
    all_rows = images * tokens
    head_count = HEADS
    head_size = HD
    score_scale = head_size ** (-0.5)
    hidden_units = down_weight.shape[0]
    onehot = (bucket[:, None] == jnp.arange(cond_table.shape[0], dtype=jnp.int32)[None, :]).astype(
        jnp.float32
    )
    condition = jnp.dot(onehot, cond_table, precision=PRECISE)
    cond_act = jax.nn.silu(condition).astype(jnp.bfloat16)
    mod_part = product(cond_act, mod_weight) + mod_bias[None, :]
    modulation = lax.all_gather(mod_part, ("ty", "tx"), axis=1, tiled=True)
    pieces = [
        modulation[:, None, index * model_width : (index + 1) * model_width] for index in range(6)
    ]
    shift_in, scale_in, gate_in, shift_mid, scale_mid, gate_mid = pieces
    places = jnp.arange(tokens, dtype=jnp.int32)
    row_pos = (tile_anchor[:, 0, 0, 0][:, None] + places[None, :] // tile_cols).astype(jnp.float32)
    col_pos = (tile_anchor[:, 0, 0, 1][:, None] + places[None, :] % tile_cols).astype(jnp.float32)
    quarter = head_size // 4
    frequency = jnp.exp(-math.log(10000.0) * jnp.arange(quarter, dtype=jnp.float32) / quarter)
    row_angle = row_pos[:, :, None, None] * frequency
    col_angle = col_pos[:, :, None, None] * frequency
    tables = (jnp.cos(row_angle), jnp.sin(row_angle), jnp.cos(col_angle), jnp.sin(col_angle))
    inputs = block_in.reshape(images, tokens, model_width)
    normed_in = normed(inputs)
    hidden_in = (
        (normed_in * (1.0 + scale_in) + shift_in)
        .astype(jnp.bfloat16)
        .reshape(all_rows, model_width)
    )
    qkv = product(hidden_in, qkv_weight).reshape(images, tokens, 3 * model_width)
    query_raw = qkv[..., :model_width].reshape(images, tokens, head_count, head_size)
    key_raw = qkv[..., model_width : 2 * model_width].reshape(images, tokens, head_count, head_size)
    query_unit = normed(query_raw)
    key_unit = normed(key_raw)
    query_low = rotate(query_unit * query_gain, tables, 1.0).astype(jnp.bfloat16)
    key_low = rotate(key_unit * key_gain, tables, 1.0).astype(jnp.bfloat16)
    value_low = qkv[..., 2 * model_width :].astype(jnp.bfloat16)
    keys_all, values_all = (
        lax.all_gather(
            key_low.reshape(images, tokens, model_width), ("ty", "tx"), axis=1, tiled=True
        ),
        lax.all_gather(value_low, ("ty", "tx"), axis=1, tiled=True),
    )
    key_heads = keys_all.reshape(images, -1, head_count, head_size)
    value_heads = values_all.reshape(images, -1, head_count, head_size)

    def attend(items):
        query_img, key_img, value_img = items
        scores = (
            jnp.einsum("qhd,khd->hqk", query_img, key_img, preferred_element_type=jnp.float32)
            * score_scale
        )
        row_max = jnp.max(scores, axis=-1, keepdims=True)
        expo = jnp.exp(scores - row_max)
        row_sum = jnp.sum(expo, axis=-1, keepdims=True)
        mixed = jnp.einsum(
            "hqk,khd->qhd",
            (expo / row_sum).astype(jnp.bfloat16),
            value_img,
            preferred_element_type=jnp.float32,
        )
        return (mixed, (row_max + jnp.log(row_sum))[:, :, 0])

    mixed_full, log_total = lax.map(attend, (query_low, key_heads, value_heads))
    attended = mixed_full.reshape(all_rows, model_width).astype(jnp.bfloat16)
    attn_out = product(attended, out_weight).reshape(images, tokens, model_width)
    middle = inputs + gate_in * attn_out
    normed_mid = normed(middle)
    hidden_mid = (
        (normed_mid * (1.0 + scale_mid) + shift_mid)
        .astype(jnp.bfloat16)
        .reshape(all_rows, model_width)
    )

    def feed(hidden_value):
        gate_up = product(hidden_value, gate_up_weight)
        return (gate_up[:, :hidden_units], gate_up[:, hidden_units:])

    gate_pre, up_pre = feed(hidden_mid)
    activ = (jax.nn.silu(gate_pre) * up_pre).astype(jnp.bfloat16)
    mlp_out = product(activ, down_weight).reshape(images, tokens, model_width)
    output = middle + gate_mid * mlp_out
    upstream = cotangent.reshape(images, tokens, model_width)
    gmid_grad = jnp.sum(upstream * mlp_out, axis=1)
    mlp_grad = (gate_mid * upstream).astype(jnp.bfloat16).reshape(all_rows, model_width)
    down_grad = product_lt(activ, mlp_grad)
    activ_grad = product_rt(mlp_grad, down_weight)
    gate_pre, up_pre = feed(hidden_mid)
    gu_grad = jnp.concatenate(
        [activ_grad * up_pre * silu_slope(gate_pre), activ_grad * jax.nn.silu(gate_pre)], axis=1
    ).astype(jnp.bfloat16)
    gateup_grad = product_lt(hidden_mid, gu_grad)
    mid_grad = product_rt(gu_grad, gate_up_weight).reshape(images, tokens, model_width)
    smid_grad = jnp.sum(mid_grad, axis=1)
    cmid_grad = jnp.sum(mid_grad * normed_mid, axis=1)
    middle_grad = upstream + norm_back(middle, mid_grad * (1.0 + scale_mid))
    gin_grad = jnp.sum(middle_grad * attn_out, axis=1)
    attn_grad = (gate_in * middle_grad).astype(jnp.bfloat16).reshape(all_rows, model_width)
    outw_grad = product_lt(attended, attn_grad)
    attended_grad = (
        product_rt(attn_grad, out_weight)
        .astype(jnp.bfloat16)
        .reshape(images, tokens, head_count, head_size)
    )
    row_delta = jnp.swapaxes(jnp.sum(attended_grad.astype(jnp.float32) * mixed_full, axis=-1), 1, 2)

    def score_parts(query_img, key_img, value_img, grad_img, total_img, delta_img):
        scores = (
            jnp.einsum("qhd,khd->hqk", query_img, key_img, preferred_element_type=jnp.float32)
            * score_scale
        )
        probs = jnp.exp(scores - total_img[:, :, None])
        prob_grad = jnp.einsum(
            "qhd,khd->hqk", grad_img, value_img, preferred_element_type=jnp.float32
        )
        score_grad = (probs * (prob_grad - delta_img[:, :, None])).astype(jnp.bfloat16)
        return (probs.astype(jnp.bfloat16), score_grad)

    def grads_all(items):
        query_img, key_img, value_img, grad_img, total_img, delta_img = items
        probs_low, score_grad = score_parts(
            query_img, key_img, value_img, grad_img, total_img, delta_img
        )
        query_part = (
            jnp.einsum("hqk,khd->qhd", score_grad, key_img, preferred_element_type=jnp.float32)
            * score_scale
        )
        key_part = (
            jnp.einsum("hqk,qhd->khd", score_grad, query_img, preferred_element_type=jnp.float32)
            * score_scale
        )
        value_part = jnp.einsum(
            "hqk,qhd->khd", probs_low, grad_img, preferred_element_type=jnp.float32
        )
        return (query_part, key_part.reshape(-1, model_width), value_part.reshape(-1, model_width))

    query_grad, key_full, value_full = lax.map(
        grads_all, (query_low, key_heads, value_heads, attended_grad, log_total, row_delta)
    )
    key_grad, value_grad = (
        lax.psum_scatter(
            key_full.astype(jnp.bfloat16), ("ty", "tx"), scatter_dimension=1, tiled=True
        ).astype(jnp.float32),
        lax.psum_scatter(
            value_full.astype(jnp.bfloat16), ("ty", "tx"), scatter_dimension=1, tiled=True
        ).astype(jnp.float32),
    )
    query_turned = rotate(query_grad, tables, -1.0)
    key_turned = rotate(key_grad.reshape(images, tokens, head_count, head_size), tables, -1.0)
    qgain_part = jnp.sum(query_turned * query_unit, axis=(0, 1, 2))
    kgain_part = jnp.sum(key_turned * key_unit, axis=(0, 1, 2))
    query_back = norm_back(query_raw, query_turned * query_gain).reshape(
        images, tokens, model_width
    )
    key_back = norm_back(key_raw, key_turned * key_gain).reshape(images, tokens, model_width)
    qkv_back = jnp.concatenate([query_back, key_back, value_grad], axis=-1).astype(jnp.bfloat16)
    qkv_back = qkv_back.reshape(all_rows, 3 * model_width)
    qkv_part = product_lt(hidden_in, qkv_back)
    in_back = product_rt(qkv_back, qkv_weight).reshape(images, tokens, model_width)
    sin_grad = jnp.sum(in_back, axis=1)
    cin_grad = jnp.sum(in_back * normed_in, axis=1)
    in_grad = middle_grad + norm_back(inputs, in_back * (1.0 + scale_in))
    mod_grad = jnp.concatenate(
        [sin_grad, cin_grad, gin_grad, smid_grad, cmid_grad, gmid_grad], axis=1
    )
    mod_cols = lax.psum_scatter(mod_grad, ("ty", "tx"), scatter_dimension=1, tiled=True)
    modw_part = jnp.dot(cond_act.astype(jnp.float32).T, mod_cols, precision=PRECISE)
    modb_part = jnp.sum(mod_cols, axis=0)
    act_grad = jnp.dot(mod_cols, mod_weight.astype(jnp.float32).T, precision=PRECISE)
    cond_grad = act_grad * silu_slope(condition)
    table_part = jnp.dot(onehot.T, cond_grad, precision=PRECISE)
    qkv_share, outw_share, gateup_share, down_share, table_share = (
        lax.psum_scatter(
            qkv_part.astype(jnp.bfloat16), ("ty", "tx"), scatter_dimension=0, tiled=True
        ).astype(jnp.float32),
        lax.psum_scatter(
            outw_grad.astype(jnp.bfloat16), ("ty", "tx"), scatter_dimension=0, tiled=True
        ).astype(jnp.float32),
        lax.psum_scatter(
            gateup_grad.astype(jnp.bfloat16), ("ty", "tx"), scatter_dimension=0, tiled=True
        ).astype(jnp.float32),
        lax.psum_scatter(
            down_grad.astype(jnp.bfloat16), ("ty", "tx"), scatter_dimension=0, tiled=True
        ).astype(jnp.float32),
        lax.psum_scatter(
            table_part.astype(jnp.bfloat16), ("ty", "tx"), scatter_dimension=0, tiled=True
        ).astype(jnp.float32),
    )
    qkv_total, outw_total, gateup_total, down_total, table_total = (
        lax.psum_scatter(
            qkv_share.astype(jnp.bfloat16), "img", scatter_dimension=1, tiled=True
        ).astype(jnp.float32),
        lax.psum_scatter(
            outw_share.astype(jnp.bfloat16), "img", scatter_dimension=1, tiled=True
        ).astype(jnp.float32),
        lax.psum_scatter(
            gateup_share.astype(jnp.bfloat16), "img", scatter_dimension=1, tiled=True
        ).astype(jnp.float32),
        lax.psum_scatter(
            down_share.astype(jnp.bfloat16), "img", scatter_dimension=1, tiled=True
        ).astype(jnp.float32),
        lax.psum_scatter(
            table_share.astype(jnp.bfloat16), "img", scatter_dimension=1, tiled=True
        ).astype(jnp.float32),
    )
    modw_total = lax.psum_scatter(
        modw_part.astype(jnp.bfloat16), "img", scatter_dimension=0, tiled=True
    ).astype(jnp.float32)
    modb_total = lax.psum(modb_part, "img")
    qgain_total, kgain_total = lax.psum((qgain_part, kgain_part), ("img", "ty", "tx"))
    return (
        output.reshape(block_in.shape),
        in_grad.reshape(block_in.shape),
        table_total,
        modw_total,
        modb_total,
        qkv_total,
        qgain_total,
        kgain_total,
        outw_total,
        gateup_total,
        down_total,
    )


def solution(mesh):
    return jax.shard_map(
        on_device,
        mesh=mesh,
        in_specs=(
            P("img", "ty", "tx", None),
            P("img"),
            P("img", "ty", "tx", None),
            P(),
            P(None, ("ty", "tx")),
            P(("ty", "tx")),
            P(),
            P(),
            P(),
            P(),
            P(),
            P(),
            P("img", "ty", "tx", None),
        ),
        out_specs=(
            P("img", "ty", "tx", None),
            P("img", "ty", "tx", None),
            P(("ty", "tx"), "img"),
            P("img", ("ty", "tx")),
            P(("ty", "tx")),
            P(("ty", "tx"), "img"),
            P(),
            P(),
            P(("ty", "tx"), "img"),
            P(("ty", "tx"), "img"),
            P(("ty", "tx"), "img"),
        ),
        check_vma=False,
    )
```

profile of v0, /device:TPU:0, one launch (start us, length us, event | category | flops | bytes accessed | tf_op | source)
XLA Modules:
  0.0 885.4 jit_solution(3208872247475456822)
XLA Ops:
  12.4 2.2 convolution_reduce_fusion.2
  15.5 25.7 %all-reduce = f32[6912]{0:T(1024)S(1)} all-reduce(f32[6912]{0:T(1024)S(1)} %add_dynamic-update-slice_fusion), channel_id=2, replica_groups=mesh['img'=4,'ty'=4,'tx'=2] {'ty','tx'}, use_global_device_ids=true, to_apply=%add | all-reduce | flops 6912 | bytes 55296
  43.1 4.7 convolution_bitcast_fusion
  50.2 2.2 copy.71
  60.3 2.1 copy.70
  67.0 21.0 %all-gather.6.cloned.1.call-done = bf16[1,1024,1152]{1,2,0:T(8,128)(2,1)} async-done(((bf16[1,128,1152]{1,2,0:T(8,128)(2,1)}), bf16[1,1024,1152]{1,2,0:T(8,128)(2,1)}) %all-gather.6.cloned.1.call-update) | async-done | bytes 2359312 | tf_op jit(solution)/shard_map/all_gather | solution.py:122
  88.0 3.1 multiply_reduce_fusion
  95.1 24.4 %all-gather.4.cloned.1.call-done = bf16[1,1024,1152]{2,1,0:T(8,128)(2,1)} async-done(((bf16[1,128,1152]{2,1,0:T(8,128)(2,1)}), bf16[1,1024,1152]{2,1,0:T(8,128)(2,1)}) %all-gather.4.cloned.1.call-update) | async-done | bytes 2359312 | tf_op jit(solution)/shard_map/all_gather | solution.py:125
  119.5 4.4 copy.69
  124.0 7.0 fusion.50
  132.4 4.1 fusion.45
  136.5 4.5 multiply_convert_fusion.4
  141.0 12.0 %multiply_reduce_fusion.3 = (f32[1152]{0:T(1024)}, f32[128]{0:T(128)S(1)}, f32[1152]{0:T(1024)}, f32[128,1152]{1,0:T(8,128)}) fusion(f32[128,1152]{1,0:T(8,128)S(1)} %get-tuple-element.128, f32[128]{0:T(128)S(1)} %add_rsqrt_fusion.3, f32[1152]{0:T(1024)S(1)} %get-tuple-element.113, bf16[1152,6144]{1,0:T(8,128)(2,1)} %param.23, ...), kind=kOutput, calls=%fused_computation.48 | convolution fusion | flops 1816114816 | bytes 16923136 | tf_op jit(solution)/shard_map/ik,jk->ij/dot_general | solution.py:58
  153.0 5.9 multiply_reduce_fusion.4
  163.8 5.7 multiply_convert_fusion
  171.5 8.6 copy.85
  180.1 4.1 copy.100
  184.3 5.2 fusion.7
  189.6 2.5 copy.81
  193.0 2.3 copy.80
  196.2 2.1 copy.76
  199.7 3.8 fusion.11
  206.1 20.8 %reduce-scatter.40.cloned.1.call-done = bf16[128,1152]{1,0:T(8,128)(2,1)} async-done(((bf16[1024,1152]{1,0:T(8,128)(2,1)}), bf16[128,1152]{1,0:T(8,128)(2,1)}) %reduce-scatter.40.cloned.1.call-update) | async-done | bytes 294928
  231.7 2.2 copy.77
  235.0 2.5 multiply_reduce_fusion.1
  237.4 35.6 %reduce-scatter.26.cloned.1.call-done = bf16[1,128,1152]{2,1,0:T(8,128)(2,1)} async-done(((bf16[1,1024,1152]{2,1,0:T(8,128)(2,1)}), bf16[1,128,1152]{2,1,0:T(8,128)(2,1)}) %reduce-scatter.26.cloned.1.call-update) | async-done | bytes 294928 | tf_op jit(solution)/shard_map/reduce_scatter | solution.py:227
  273.1 7.2 multiply_reduce_fusion.5
  280.4 2.4 copy.87
  282.9 48.2 %reduce-scatter.42.cloned.1.call-done = f32[864,1]{1,0:T(8,128)} async-done(((f32[6912,1]{1,0:T(8,128)}), f32[864,1]{1,0:T(8,128)}) %reduce-scatter.42.cloned.1.call-update) | async-done | bytes 3472 | tf_op jit(solution)/shard_map/reshape.98
  331.1 2.6 convolution_reduce_fusion
  334.8 2.3 convolution_convert_fusion.3
  337.3 4.9 convolution_convert_fusion.2
  343.1 5.5 convolution_convert_fusion.1
  349.9 8.5 convolution_convert_fusion
  359.2 25.1 %all-reduce.5.cloned.1.call-done = bf16[32,1152]{1,0:T(8,128)(2,1)} async-done(((bf16[32,1152]{1,0:T(8,128)(2,1)}), bf16[32,1152]{1,0:T(8,128)(2,1)}) %all-reduce.5.cloned.1.call-update) | async-done | bytes 73744
  386.0 47.2 %reduce-scatter.32.cloned.1.call-done = bf16[144,1152]{1,0:T(8,128)(2,1)} async-done(((bf16[1152,1152]{1,0:T(8,128)(2,1)}), bf16[144,1152]{1,0:T(8,128)(2,1)}) %reduce-scatter.32.cloned.1.call-update) | async-done | bytes 331792 | tf_op jit(solution)/shard_map/reduce_scatter | solution.py:259
  437.2 65.0 %reduce-scatter.38.cloned.1.call-done = bf16[384,1152]{1,0:T(8,128)(2,1)} async-done(((bf16[3072,1152]{1,0:T(8,128)(2,1)}), bf16[384,1152]{1,0:T(8,128)(2,1)}) %reduce-scatter.38.cloned.1.call-update) | async-done | bytes 884752 | tf_op jit(solution)/shard_map/reduce_scatter | solution.py:265
  502.2 2.2 copy.95
  504.5 71.7 %reduce-scatter.30.cloned.1.call-done = bf16[144,3456]{1,0:T(8,128)(2,1)} async-done(((bf16[1152,3456]{1,0:T(8,128)(2,1)}), bf16[144,3456]{1,0:T(8,128)(2,1)}) %reduce-scatter.30.cloned.1.call-update) | async-done | bytes 995344 | tf_op jit(solution)/shard_map/reduce_scatter | solution.py:256
  576.2 2.6 copy.91
  578.9 101.5 %reduce-scatter.34.cloned.1.call-done = bf16[144,6144]{1,0:T(8,128)(2,1)} async-done(((bf16[1152,6144]{1,0:T(8,128)(2,1)}), bf16[144,6144]{1,0:T(8,128)(2,1)}) %reduce-scatter.34.cloned.1.call-update) | async-done | bytes 1769488 | tf_op jit(solution)/shard_map/reduce_scatter | solution.py:262
  680.6 39.4 %all-reduce.2 = (f32[72]{0:T(128)}, f32[72]{0:T(128)}) all-reduce(f32[72]{0:T(128)S(1)} %reduce_sum.233, f32[72]{0:T(128)S(1)} %reduce_sum.236), channel_id=1, replica_groups=mesh['img'=4,'ty'=4,'tx'=2] {'img','ty','tx'}, use_global_device_ids=true, to_apply=%region_28.29 | all-reduce | flops 144 | bytes 1152 | tf_op jit(solution)/shard_map/psum | solution.py:293
  721.0 11.2 %psum.21 = f32[864]{0:T(1024)} all-reduce(f32[864]{0:T(1024)S(1)} %bitcast_reduce_fusion), channel_id=1, replica_groups=mesh['img'=4,'ty'=4,'tx'=2] {'img'}, use_global_device_ids=true, to_apply=%region_23.24 | all-reduce | flops 864 | bytes 6912 | tf_op jit(solution)/shard_map/psum | solution.py:292
  735.7 34.5 %reduce-scatter.28.cloned.1.call-done = bf16[288,864]{1,0:T(8,128)(2,1)} async-done(((bf16[1152,864]{1,0:T(8,128)(2,1)}), bf16[288,864]{1,0:T(8,128)(2,1)}) %reduce-scatter.28.cloned.1.call-update) | async-done | bytes 497680 | tf_op jit(solution)/shard_map/reduce_scatter | solution.py:289
  770.2 2.1 convert_element_type.204
  772.3 24.7 %reduce-scatter.50.cloned.1.call-done = bf16[288,384]{1,0:T(8,128)(2,1)} async-done(((bf16[1152,384]{1,0:T(8,128)(2,1)}), bf16[288,384]{1,0:T(8,128)(2,1)}) %reduce-scatter.50.cloned.1.call-update) | async-done | bytes 221200
  799.0 37.7 %reduce-scatter.46.cloned.1.call-done = bf16[864,144]{1,0:T(8,128)(2,1)} async-done(((bf16[3456,144]{1,0:T(8,128)(2,1)}), bf16[864,144]{1,0:T(8,128)(2,1)}) %reduce-scatter.46.cloned.1.call-update) | async-done | bytes 248848
  838.7 37.7 %reduce-scatter.36.cloned.1.call-done = bf16[144,1536]{1,0:T(8,128)(2,1)} async-done(((bf16[144,6144]{1,0:T(8,128)(2,1)}), bf16[144,1536]{1,0:T(8,128)(2,1)}) %reduce-scatter.36.cloned.1.call-update) | async-done | bytes 442384 | tf_op jit(solution)/shard_map/reduce_scatter | solution.py:279
  (274 shorter events, 64.9 us)
Async XLA Ops:
  7.2 123.9 %copy-start = (bf16[1152,1152]{1,0:T(8,128)(2,1)S(1)}, bf16[1152,1152]{1,0:T(8,128)(2,1)}, u32[]{:S(2)}) copy-start(bf16[1152,1152]{1,0:T(8,128)(2,1)} %param.22) | copy-start | bytes 7962628
  7.2 35.9 %copy-start.4 = (f32[1,16,8,1152]{3,2,1,0:T(8,128)S(1)}, f32[1,16,8,1152]{3,2,1,0:T(8,128)}, u32[]{:S(2)}) copy-start(f32[1,16,8,1152]{3,2,1,0:T(8,128)} %param.13) | copy-start | bytes 1769476
  7.2 80.8 %all-gather.6.cloned.1.call-start = ((), (), s32[]{:S(2)}) async-start(), calls=%async_computation.14 | async-start | bytes 2654208 | tf_op jit(solution)/shard_map/all_gather | solution.py:122
  58.4 61.1 %all-gather.4.cloned.1.call-start = ((), (), s32[]{:S(2)}) async-start(), calls=%async_computation.13 | async-start | bytes 2654208 | tf_op jit(solution)/shard_map/all_gather | solution.py:125
  60.3 166.7 %reduce-scatter.40.cloned.1.call-start = ((), (), s32[]{:S(2)}) async-start(), calls=%async_computation.22 | async-start | bytes 2654208
  66.9 24.2 %copy-start.22 = (bf16[128,16,18]{0,2,1:T(8,128)(2,1)}, bf16[128,16,18]{0,2,1:T(8,128)(2,1)S(1)}, u32[]{:S(2)}) copy-start(bf16[128,16,18]{0,2,1:T(8,128)(2,1)S(1)} %get-tuple-element.144) | copy-start | bytes 221188
  67.0 24.2 %copy-start.24 = (bf16[128,16,18]{0,2,1:T(8,128)(2,1)}, bf16[128,16,18]{0,2,1:T(8,128)(2,1)S(1)}, u32[]{:S(2)}) copy-start(bf16[128,16,18]{0,2,1:T(8,128)(2,1)S(1)} %get-tuple-element.145) | copy-start | bytes 221188
  67.0 24.2 %copy-start.26 = (bf16[128,16,18]{0,2,1:T(8,128)(2,1)}, bf16[128,16,18]{0,2,1:T(8,128)(2,1)S(1)}, u32[]{:S(2)}) copy-start(bf16[128,16,18]{0,2,1:T(8,128)(2,1)S(1)} %get-tuple-element.158) | copy-start | bytes 221188
  94.5 29.4 %copy-start.61 = (f32[16,128]{1,0:T(8,128)}, f32[16,128]{1,0:T(8,128)S(1)}, u32[]{:S(2)}) copy-start(f32[16,128]{1,0:T(8,128)S(1)} %fusion) | copy-start | bytes 24580
  124.0 7.9 slice-start
  124.0 7.1 copy-start.39
  124.0 7.9 slice-start.1
  124.0 7.9 slice-start.2
  124.0 8.3 slice-start.3
  131.8 21.2 %copy-start.5 = (f32[128,1152]{1,0:T(8,128)}, f32[128,1152]{1,0:T(8,128)S(1)}, u32[]{:S(2)}) copy-start(f32[128,1152]{1,0:T(8,128)S(1)} %get-tuple-element.128) | copy-start | bytes 1769476
  131.8 21.2 %copy-start.62 = (f32[128]{0:T(128)}, f32[128]{0:T(128)S(1)}, u32[]{:S(2)}) copy-start(f32[128]{0:T(128)S(1)} %add_rsqrt_fusion.3) | copy-start | bytes 1540
  140.9 12.1 %copy-start.16 = (bf16[128,3072]{1,0:T(8,128)(2,1)}, bf16[128,3072]{1,0:T(8,128)(2,1)S(1)}, u32[]{:S(2)}) copy-start(bf16[128,3072]{1,0:T(8,128)(2,1)S(1)} %get-tuple-element.129) | copy-start | bytes 2359300
  140.9 12.1 %copy-start.18 = (bf16[128,3072]{1,0:T(8,128)(2,1)}, bf16[128,3072]{1,0:T(8,128)(2,1)S(1)}, u32[]{:S(2)}) copy-start(bf16[128,3072]{1,0:T(8,128)(2,1)S(1)} %get-tuple-element.130) | copy-start | bytes 2359300
  141.0 12.1 %copy-start.14 = (bf16[128,3072]{1,0:T(8,128)(2,1)}, bf16[128,3072]{1,0:T(8,128)(2,1)S(1)}, u32[]{:S(2)}) copy-start(bf16[128,3072]{1,0:T(8,128)(2,1)S(1)} %get-tuple-element.131) | copy-start | bytes 2359300
  184.3 88.8 %reduce-scatter.26.cloned.1.call-start = ((), (), s32[]{:S(2)}) async-start(), calls=%async_computation.15 | async-start | bytes 2654208 | tf_op jit(solution)/shard_map/reduce_scatter | solution.py:227
  192.1 6.9 copy-start.68
  192.1 7.6 copy-start.11
  192.1 138.9 %reduce-scatter.42.cloned.1.call-start = ((), (), s32[]{:S(2)}) async-start(), calls=%async_computation.23 | async-start | bytes 3981312 | tf_op jit(solution)/shard_map/reshape.98
  205.0 25.0 %copy-start.12 = (f32[1,128,1152]{1,2,0:T(8,128)S(1)}, f32[1,128,1152]{1,2,0:T(8,128)}, u32[]{:S(2)}) copy-start(f32[1,128,1152]{1,2,0:T(8,128)} %copy.71) | copy-start | bytes 1769476
  233.9 39.1 %copy-start.65 = (f32[128]{0:T(128)S(1)}, f32[128]{0:T(128)}, u32[]{:S(2)}) copy-start(f32[128]{0:T(128)} %copy-done.64) | copy-start | bytes 1540
  273.0 7.3 copy-start.58
  273.0 7.3 copy-start.56
  273.0 7.3 copy-start.55
  273.0 7.3 copy-start.57
  282.8 50.9 %copy-start.50 = (f32[1152]{0:T(1024)S(1)}, f32[1152]{0:T(1024)}, u32[]{:S(2)}) copy-start(f32[1152]{0:T(1024)} %copy-done.49) | copy-start | bytes 13828
  282.8 52.0 %copy-start.10 = (f32[128,1152]{1,0:T(8,128)S(1)}, f32[128,1152]{1,0:T(8,128)}, u32[]{:S(2)}) copy-start(f32[128,1152]{1,0:T(8,128)} %copy-done.9) | copy-start | bytes 1769476
  282.8 52.0 %copy-start.40 = (f32[1152]{0:T(1024)S(1)}, f32[1152]{0:T(1024)}, u32[]{:S(2)}) copy-start(f32[1152]{0:T(1024)} %get-tuple-element.116) | copy-start | bytes 13828
  282.8 101.4 %all-reduce.5.cloned.1.call-start = ((), (), s32[]{:S(2)}) async-start(), calls=%async_computation.28 | async-start | bytes 147456
  334.5 98.7 %reduce-scatter.32.cloned.1.call-start = ((), (), s32[]{:S(2)}) async-start(), calls=%async_computation.18 | async-start | bytes 2985984 | tf_op jit(solution)/shard_map/reduce_scatter | solution.py:259
  337.2 165.0 %reduce-scatter.38.cloned.1.call-start = ((), (), s32[]{:S(2)}) async-start(), calls=%async_computation.21 | async-start | bytes 7962624 | tf_op jit(solution)/shard_map/reduce_scatter | solution.py:265
  342.2 234.0 %reduce-scatter.30.cloned.1.call-start = ((), (), s32[]{:S(2)}) async-start(), calls=%async_computation.17 | async-start | bytes 8957952 | tf_op jit(solution)/shard_map/reduce_scatter | solution.py:256
  348.6 331.8 %reduce-scatter.34.cloned.1.call-start = ((), (), s32[]{:S(2)}) async-start(), calls=%async_computation.19 | async-start | bytes 15925248 | tf_op jit(solution)/shard_map/reduce_scatter | solution.py:262
  358.4 76.9 %copy-start.21 = (f32[864,1]{1,0:T(8,128)S(1)}, f32[864,1]{1,0:T(8,128)}, u32[]{:S(2)}) copy-start(f32[864,1]{1,0:T(8,128)} %reduce-scatter.42.cloned.1.call-done) | copy-start | bytes 10372
  358.4 77.1 %copy-start.54 = (f32[1152]{0:T(1024)S(1)}, f32[1152]{0:T(1024)}, u32[]{:S(2)}) copy-start(f32[1152]{0:T(1024)} %get-tuple-element.119) | copy-start | bytes 13828
  358.4 373.8 %reduce-scatter.44.cloned.1.call-start = ((), (), s32[]{:S(2)}) async-start(), calls=%async_computation.24 | async-start | bytes 368640
  385.9 348.1 %reduce-scatter.48.cloned.1.call-start = ((), (), s32[]{:S(2)}) async-start(), calls=%async_computation.26 | async-start | bytes 737280
  435.2 335.0 %reduce-scatter.28.cloned.1.call-start = ((), (), s32[]{:S(2)}) async-start(), calls=%async_computation.16 | async-start | bytes 2580480 | tf_op jit(solution)/shard_map/reduce_scatter | solution.py:289
  437.1 359.8 %reduce-scatter.50.cloned.1.call-start = ((), (), s32[]{:S(2)}) async-start(), calls=%async_computation.27 | async-start | bytes 1105920
  504.4 215.6 %copy-start.70 = (f32[128]{0:T(128)S(1)}, f32[128]{0:T(128)}, u32[]{:S(2)}) copy-start(f32[128]{0:T(128)} %get-tuple-element.108) | copy-start | bytes 1540
  504.4 215.6 %copy-start.29 = (f32[128,1152]{1,0:T(8,128)S(1)}, f32[128,1152]{1,0:T(8,128)}, u32[]{:S(2)}) copy-start(f32[128,1152]{1,0:T(8,128)} %get-tuple-element.181) | copy-start | bytes 1769476
  504.4 332.3 %reduce-scatter.46.cloned.1.call-start = ((), (), s32[]{:S(2)}) async-start(), calls=%async_computation.25 | async-start | bytes 2211840
  578.8 297.6 %reduce-scatter.36.cloned.1.call-start = ((), (), s32[]{:S(2)}) async-start(), calls=%async_computation.20 | async-start | bytes 2211840 | tf_op jit(solution)/shard_map/reduce_scatter | solution.py:279
  732.2 146.2 %copy-start.1 = (bf16[1152,1152]{1,0:T(8,128)(2,1)S(1)}, bf16[1152,1152]{1,0:T(8,128)(2,1)}, u32[]{:S(2)}) copy-start(bf16[1152,1152]{1,0:T(8,128)(2,1)} %param.22) | copy-start | bytes 7962628
  (45 other events, 146.8 us)
Sparse Core Ops, SparseCore 0:
  58.5 29.4 all-gather.5
  90.5 28.9 all-gather.3
  184.4 42.5 reduce-scatter.39
  230.5 42.4 reduce-scatter.25
  282.9 48.0 reduce-scatter.41
  334.6 49.5 all-reduce.4
  388.1 44.9 reduce-scatter.31
  436.6 65.5 reduce-scatter.37
  506.1 70.0 reduce-scatter.29
  579.6 100.7 reduce-scatter.33
  683.3 20.0 reduce-scatter.43
  706.1 20.1 reduce-scatter.47
  728.6 41.5 reduce-scatter.27
  773.0 23.8 reduce-scatter.49
  799.3 37.3 reduce-scatter.45
  838.9 37.4 reduce-scatter.35
where the time goes:
time: 892 us; the launch traced here: 885 us
  waiting for transfers between devices  595 us (67%)
  matrix products  93.8 us (11%)
  blocking collectives  76.2 us (9%)
  local copies, waits for them, and re-layouts  70.3 us (8%)
  other arithmetic  31.3 us (4%)
  between operations  17.5 us (2%)
    unnamed x22, waiting for transfers between devices  109 us
    reduce_scatter x1, waiting for transfers between devices, on_device(): lax.psum_scatter(gateup_grad.astype(jnp.bfloat16), ('ty', 'tx'), scatter_...  102 us
    reduce_scatter x1, waiting for transfers between devices, on_device(): lax.psum_scatter(qkv_part.astype(jnp.bfloat16), ('ty', 'tx'), scatter_dim...  71.7 us
    reduce_scatter x1, waiting for transfers between devices, on_device(): lax.psum_scatter(down_grad.astype(jnp.bfloat16), ('ty', 'tx'), scatter_di...  65 us
    another operation x1, waiting for transfers between devices  48.2 us
    reduce_scatter x1, waiting for transfers between devices, on_device(): lax.psum_scatter(outw_grad.astype(jnp.bfloat16), ('ty', 'tx'), scatter_di...  47.2 us
    unnamed x176, local copies, waits for them, and re-layouts  40.9 us
    psum x1, blocking collectives, on_device(): lax.psum((qgain_part, kgain_part), ('img', 'ty', 'tx'))  39.4 us
  transfers between devices with their start and end apart: 16, of which 14 were waited for; matrix products, arithmetic and copies ran while one was open for 10% of the time, Pallas kernels for 0%

commit v1 on v0

--- a/solution.py
+++ b/solution.py
@@ -1,8 +1,11 @@
+import functools
 import math
 
 import jax
 import jax.numpy as jnp
 from jax import lax
+from jax.experimental import pallas as pl
+from jax.experimental.pallas import tpu as pltpu
 from jax.sharding import PartitionSpec as P
 
 HEADS = 16
@@ -306,9 +309,850 @@
     )
 
 
+def sigmoid(value):
+    return 1.0 / (1.0 + jnp.exp(-value))
+
+
+def dot_nn(left, right):
+    return lax.dot_general(
+        left, right, (((1,), (0,)), ((), ())), preferred_element_type=jnp.float32
+    )
+
+
+def dot_nt(left, right):
+    return lax.dot_general(
+        left, right, (((1,), (1,)), ((), ())), preferred_element_type=jnp.float32
+    )
+
+
+def dot_tn(left, right):
+    return lax.dot_general(
+        left, right, (((0,), (0,)), ((), ())), preferred_element_type=jnp.float32
+    )
+
+
+def column_sum(value):
+    return jnp.sum(value, axis=0, keepdims=True)
+
+
+EXTRA = 16
+LANES = 128
+
+
+def open_kernel(
+    scalars, x_ref, table_ref, weight_ref, bias_ref, cot_ref, pay_ref, low_ref, wide_ref
+):
+    tokens, width = x_ref.shape
+    columns = weight_ref.shape[1]
+    x = x_ref[...]
+    pay_ref[0:tokens, :] = normed(x).astype(jnp.bfloat16)
+    low_ref[...] = cot_ref[...].astype(jnp.bfloat16)
+    row = table_ref[pl.ds(scalars[0], 1), :]
+    act = (row * sigmoid(row)).astype(jnp.bfloat16)
+    mod = dot_nn(jnp.broadcast_to(act, (8, width)), weight_ref[...]) + bias_ref[...]
+    wide_ref[...] = jnp.zeros_like(wide_ref)
+    wide_ref[:, 0:columns] = mod
+    full = wide_ref[0:1, :]
+    high = full.astype(jnp.bfloat16).astype(jnp.float32)
+    rest = full - high
+    middle = rest.astype(jnp.bfloat16).astype(jnp.float32)
+    least = rest - middle
+    lane = lax.broadcasted_iota(jnp.int32, (EXTRA, width), 1)
+    line = lax.broadcasted_iota(jnp.int32, (EXTRA, width), 0)
+    quarter = HD // 4
+    anchor = jnp.where(
+        lane < 2 * quarter,
+        scalars[1].astype(jnp.float32),
+        jnp.where(lane < HD, scalars[2].astype(jnp.float32), 0.0),
+    )
+    extra = jnp.where(
+        line == 0,
+        high,
+        jnp.where(
+            line == 1, middle, jnp.where(line == 2, least, jnp.where(line == 3, anchor, 0.0))
+        ),
+    )
+    pay_ref[tokens : tokens + EXTRA, :] = extra.astype(jnp.bfloat16)
+
+
+def partner(value):
+    quarter = HD // 4
+    lane = lax.broadcasted_iota(jnp.int32, value.shape, 1)
+    ahead = pltpu.roll(value, LANES - quarter, 1)
+    behind = pltpu.roll(value, quarter, 1)
+    return jnp.where((lane // quarter) % 2 == 0, ahead, behind)
+
+
+def unit_rate(raw):
+    return lax.rsqrt(jnp.sum(raw * raw, axis=-1, keepdims=True) * (1.0 / HD) + EPS)
+
+
+def wide_gain(gain_ref, scratch):
+    scratch[...] = jnp.zeros_like(scratch)
+    scratch[0:1, 0:HD] = gain_ref[...]
+    return scratch[0:1, :]
+
+
+def attend_kernel(
+    blocks,
+    tile_cols,
+    scalars,
+    *refs,
+):
+    pieces, refs = refs[:10], refs[10:]
+    (
+        weight_ref,
+        qgain_ref,
+        kgain_ref,
+        att_ref,
+        hid_ref,
+        qkv_ref,
+        raw_ref,
+        turn_ref,
+        mod_ref,
+        spread_ref,
+        rows_ref,
+        flat_ref,
+        anchor_ref,
+        gain_ref,
+        vt_ref,
+    ) = refs
+    mine = scalars[0]
+    own, core, xn, yn, d1, d2, cx, cy, cd1, cd2 = pieces
+    width = own.shape[1]
+    tokens = own.shape[0] - EXTRA
+    columns = 6 * width // blocks
+    half = d1.shape[0]
+    everyone = blocks * tokens
+    heads = HEADS // blocks
+    extras = {
+        0: own[tokens:, :],
+        1: xn[tokens:, :],
+        2: core[tokens:, :],
+        3: cx[tokens:, :],
+        4: yn[tokens:, :],
+        5: d2[tokens - half :, :],
+        6: cy[tokens:, :],
+        7: cd2[tokens - half :, :],
+    }
+    for index, extra in extras.items():
+        extra = extra.astype(jnp.float32)
+        place = mine ^ index
+        rows_ref[pl.ds(place, 1), :] = extra[0:1] + extra[1:2] + extra[2:3]
+        anchor_ref[0, pl.ds(place, 1), :] = extra[3:4, 0:LANES]
+    for index in range(blocks):
+        flat_ref[0:1, columns * index : columns * (index + 1)] = rows_ref[
+            index : index + 1, 0:columns
+        ]
+    mod_ref[...] = jnp.zeros_like(mod_ref)
+    for index in range(6):
+        mod_ref[index : index + 1, :] = flat_ref[0:1, width * index : width * (index + 1)]
+    shift_in = mod_ref[0:1, :]
+    scale_in = 1.0 + mod_ref[1:2, :]
+
+    def place_tokens(index, ref, rows, offset):
+        low = ref[0:rows, :].astype(jnp.float32) * scale_in + shift_in
+        start = pl.multiple_of((mine ^ index) * tokens + offset, 16)
+        hid_ref[pl.ds(start, rows), :] = low.astype(jnp.bfloat16)
+
+    for index, ref in ((0, own), (1, xn), (2, core), (3, cx), (4, yn), (6, cy)):
+        place_tokens(index, ref, tokens, 0)
+    for index, first, second in ((5, d1, d2), (7, cd1, cd2)):
+        place_tokens(index, first, half, 0)
+        place_tokens(index, second, tokens - half, half)
+
+    quarter = HD // 4
+    lane = lax.broadcasted_iota(jnp.int32, (tokens, LANES), 1)
+    token = lax.broadcasted_iota(jnp.int32, (tokens, LANES), 0)
+    rate = jnp.where(
+        lane < HD,
+        jnp.exp((lane % quarter).astype(jnp.float32) * (-math.log(10000.0) / quarter)),
+        0.0,
+    )
+    offset = jnp.where(lane < 2 * quarter, token // tile_cols, token % tile_cols)
+    offset = offset.astype(jnp.float32) * rate
+    offset_cos, offset_sin = jnp.cos(offset), jnp.sin(offset)
+    anchor = anchor_ref[0] * rate[0:blocks]
+    anchor_ref[0] = jnp.cos(anchor)
+    anchor_ref[1] = jnp.sin(anchor)
+    sign = jnp.where((lane // quarter) % 2 == 0, -1.0, 1.0)
+
+    spread_ref[...] = jnp.zeros_like(spread_ref)
+    for index in range(3 * heads):
+        spread_ref[:, LANES * index : LANES * index + HD] = weight_ref[
+            :, HD * index : HD * (index + 1)
+        ]
+    query_gain = wide_gain(qgain_ref, gain_ref.at[0])
+    key_gain = wide_gain(kgain_ref, gain_ref.at[1])
+
+    def project(index, carry):
+        rows = pl.ds(pl.multiple_of(index * tokens, tokens), tokens)
+        anchor_cos = anchor_ref[0, pl.ds(index, 1), :]
+        anchor_sin = anchor_ref[1, pl.ds(index, 1), :]
+        turn_cos = anchor_cos * offset_cos - anchor_sin * offset_sin
+        turn_sin = (anchor_sin * offset_cos + anchor_cos * offset_sin) * sign
+        turn_ref[0, rows, :] = turn_cos
+        turn_ref[1, rows, :] = turn_sin
+        product = dot_nn(hid_ref[rows, :], spread_ref[...])
+        for part in range(2 * heads):
+            raw = product[:, LANES * part : LANES * (part + 1)]
+            raw_ref[part, rows, :] = raw
+            unit = raw * unit_rate(raw) * (query_gain if part < heads else key_gain)
+            turned = unit * turn_cos + partner(unit) * turn_sin
+            qkv_ref[part, rows, :] = turned.astype(jnp.bfloat16)
+        for part in range(2 * heads, 3 * heads):
+            qkv_ref[part, rows, :] = product[:, LANES * part : LANES * (part + 1)].astype(
+                jnp.bfloat16
+            )
+        return carry
+
+    lax.fori_loop(0, blocks, project, 0)
+    scale = HD ** (-0.5) * math.log2(math.e)
+    chunk = 2 * tokens
+    for head in range(heads):
+        keys = qkv_ref[heads + head]
+        vt_ref[...] = qkv_ref[2 * heads + head].T
+
+        def attend(index, carry):
+            rows = pl.ds(pl.multiple_of(index * chunk, chunk), chunk)
+            scores = dot_nt(keys, qkv_ref[head, rows, :])
+            expo = jnp.exp2(scores * scale)
+            total = column_sum(expo)
+            mixed = dot_nn(vt_ref[...], expo.astype(jnp.bfloat16)) * (1.0 / total)
+            att_ref[rows, LANES * head : LANES * (head + 1)] = mixed.T.astype(jnp.bfloat16)
+            return carry
+
+        lax.fori_loop(0, everyone // chunk, attend, 0)
+
+
+def middle_kernel(att_ref, weight_ref, x_ref, mod_ref, out_ref, mid_ref, hid_ref):
+    blocks = att_ref.shape[0]
+    heads = HEADS // blocks
+    attended = jnp.concatenate(
+        [
+            att_ref[index, :, LANES * head : LANES * head + HD]
+            for index in range(blocks)
+            for head in range(heads)
+        ],
+        axis=1,
+    )
+    attn_out = dot_nn(attended, weight_ref[...])
+    out_ref[...] = attn_out
+    middle = x_ref[...] + mod_ref[2:3, :] * attn_out
+    mid_ref[...] = middle
+    hid_ref[...] = (normed(middle) * (1.0 + mod_ref[4:5, :]) + mod_ref[3:4, :]).astype(
+        jnp.bfloat16
+    )
+
+
+def mlp_kernel(
+    gate_ref,
+    up_ref,
+    down_ref,
+    outw_ref,
+    hid_ref,
+    mid_ref,
+    attn_ref,
+    cot_ref,
+    mod_ref,
+    output_ref,
+    mgrad_ref,
+    agrad_ref,
+    dgrad_ref,
+    sums_ref,
+    low_ref,
+    mlp_ref,
+    back_ref,
+):
+    step = pl.program_id(0)
+    blocks = dgrad_ref.shape[0]
+    heads = HEADS // blocks
+    gate_mid = mod_ref[5:6, :]
+
+    @pl.when(step == 0)
+    def _():
+        low_ref[...] = (gate_mid * cot_ref[...]).astype(jnp.bfloat16)
+        mlp_ref[...] = jnp.zeros_like(mlp_ref)
+        back_ref[...] = jnp.zeros_like(back_ref)
+
+    hidden = hid_ref[...]
+    gate = dot_nn(hidden, gate_ref[...])
+    up = dot_nn(hidden, up_ref[...])
+    sigma = sigmoid(gate)
+    silu = gate * sigma
+    act = (silu * up).astype(jnp.bfloat16)
+    mlp_ref[...] += dot_nn(act, down_ref[...])
+    act_grad = dot_nt(low_ref[...], down_ref[...])
+    slope = sigma * (1.0 + gate * (1.0 - sigma))
+    gate_grad = (act_grad * up * slope).astype(jnp.bfloat16)
+    up_grad = (act_grad * silu).astype(jnp.bfloat16)
+    back_ref[...] += dot_nt(gate_grad, gate_ref[...]) + dot_nt(up_grad, up_ref[...])
+
+    @pl.when(step == pl.num_programs(0) - 1)
+    def _():
+        middle = mid_ref[...]
+        upstream = cot_ref[...]
+        mlp_out = mlp_ref[...]
+        output_ref[...] = middle + gate_mid * mlp_out
+        back = back_ref[...]
+        inverse = lax.rsqrt(jnp.mean(middle * middle, axis=-1, keepdims=True) + EPS)
+        unit = middle * inverse
+        lifted = back * (1.0 + mod_ref[4:5, :])
+        middle_grad = upstream + inverse * (
+            lifted - unit * jnp.mean(lifted * unit, axis=-1, keepdims=True)
+        )
+        mgrad_ref[...] = middle_grad
+        attn_grad = (mod_ref[2:3, :] * middle_grad).astype(jnp.bfloat16)
+        agrad_ref[...] = attn_grad
+        dgrad_ref[...] = jnp.zeros_like(dgrad_ref)
+        for index in range(blocks):
+            rows = outw_ref[HD * heads * index : HD * heads * (index + 1), :]
+            part = dot_nt(attn_grad, rows).astype(jnp.bfloat16)
+            for head in range(heads):
+                dgrad_ref[index, :, LANES * head : LANES * head + HD] = part[
+                    :, HD * head : HD * (head + 1)
+                ]
+        sums_ref[...] = jnp.zeros_like(sums_ref)
+        sums_ref[2:3, :] = column_sum(middle_grad * attn_ref[...])
+        sums_ref[3:4, :] = column_sum(back)
+        sums_ref[4:5, :] = column_sum(back * unit)
+        sums_ref[5:6, :] = column_sum(upstream * mlp_out)
+
+
+def gather_blocks(pieces, ref, place, tokens):
+    own, core, xn, yn, d1, d2, cx, cy, cd1, cd2 = pieces
+    half = d1.shape[0]
+    for index, piece in ((0, own), (1, xn), (2, core), (3, cx), (4, yn), (6, cy)):
+        ref[pl.ds(place(index), tokens), :] = piece[...]
+    for index, first, second in ((5, d1, d2), (7, cd1, cd2)):
+        ref[pl.ds(place(index), half), :] = first[...]
+        ref[pl.ds(place(index) + half, tokens - half), :] = second[...]
+
+
+def mlp_weights_kernel(scalars, *refs):
+    hid_pieces, cot_pieces, refs = refs[:10], refs[10:20], refs[20:]
+    gate_ref, up_ref, down_ref, mod_ref, gateup_ref, dgrad_ref, all_ref, low_ref, act_ref = refs
+    tokens, width = hid_pieces[0].shape
+    blocks = gateup_ref.shape[0]
+    rows = width // blocks
+    gather_blocks(hid_pieces, all_ref, lambda index: index * tokens, tokens)
+    gather_blocks(cot_pieces, low_ref, lambda index: index * tokens, tokens)
+    gate_mid = mod_ref[5:6, :]
+    units = act_ref.shape[2]
+
+    def chunked(index, carry):
+        span = pl.ds(pl.multiple_of(index * tokens, tokens), tokens)
+        low = (low_ref[span, :].astype(jnp.float32) * gate_mid).astype(jnp.bfloat16)
+        low_ref[span, :] = low
+        hidden = all_ref[span, :]
+        gate = dot_nn(hidden, gate_ref[...])
+        up = dot_nn(hidden, up_ref[...])
+        act_grad = dot_nt(low, down_ref[...])
+        sigma = sigmoid(gate)
+        silu = gate * sigma
+        slope = sigma * (1.0 + gate * (1.0 - sigma))
+        act_ref[0, span, :] = (silu * up).astype(jnp.bfloat16)
+        act_ref[1, span, :] = (act_grad * up * slope).astype(jnp.bfloat16)
+        act_ref[2, span, :] = (act_grad * silu).astype(jnp.bfloat16)
+        return carry
+
+    lax.fori_loop(0, blocks, chunked, 0)
+    down = dot_tn(low_ref[...], act_ref[0]).astype(jnp.bfloat16)
+    dgrad_ref[...] = down.reshape(dgrad_ref.shape)
+    for side in range(2):
+        grad = dot_tn(all_ref[...], act_ref[1 + side]).astype(jnp.bfloat16)
+        gateup_ref[:, side, :, :] = grad.reshape(blocks, rows, units)
+
+
+def attend_back_kernel(
+    attg_ref, qkv_ref, raw_ref, turn_ref, qgain_ref, kgain_ref, back_ref, gsum_ref,
+    kt_ref, qt_ref, grad_ref, gain_ref,
+):
+    heads = attg_ref.shape[1] // LANES
+    everyone = attg_ref.shape[0]
+    chunk = 256
+    scale = HD ** (-0.5)
+    query_gain = wide_gain(qgain_ref, gain_ref.at[0])
+    key_gain = wide_gain(kgain_ref, gain_ref.at[1])
+    grad_ref[...] = jnp.zeros_like(grad_ref)
+    for head in range(heads):
+        keys = qkv_ref[heads + head]
+        values = qkv_ref[2 * heads + head]
+        kt_ref[...] = keys.T
+
+        def attend(index, carry):
+            rows = pl.ds(pl.multiple_of(index * chunk, chunk), chunk)
+            query = qkv_ref[head, rows, :]
+            upstream = attg_ref[rows, LANES * head : LANES * (head + 1)]
+            expo = jnp.exp2(dot_nt(keys, query) * (scale * math.log2(math.e)))
+            probs = expo * (1.0 / column_sum(expo))
+            weighted = probs * dot_nt(values, upstream)
+            score_grad = (weighted - probs * column_sum(weighted)).astype(jnp.bfloat16)
+            grad_ref[2 * heads + head] += dot_nn(probs.astype(jnp.bfloat16), upstream)
+            grad_ref[heads + head] += dot_nn(score_grad, query)
+            grad_ref[head, rows, :] = dot_nn(kt_ref[...], score_grad).T
+            return carry
+
+        lax.fori_loop(0, everyone // chunk, attend, 0)
+    gsum_ref[...] = jnp.zeros_like(gsum_ref)
+
+    def finish(index, carry):
+        rows = pl.ds(pl.multiple_of(index * LANES, LANES), LANES)
+        turn_cos = turn_ref[0, rows, :]
+        turn_sin = turn_ref[1, rows, :]
+        parts = []
+        for part in range(2 * heads):
+            gain = query_gain if part < heads else key_gain
+            grad = grad_ref[part, rows, :] * scale
+            turned = grad * turn_cos - partner(grad) * turn_sin
+            raw = raw_ref[part, rows, :]
+            rate = unit_rate(raw)
+            unit = raw * rate
+            line = 0 if part < heads else 1
+            gsum_ref[line : line + 1, :] += column_sum(turned * unit)
+            lifted = turned * gain
+            mean = jnp.sum(lifted * unit, axis=-1, keepdims=True) * (1.0 / HD)
+            parts.append((rate * (lifted - unit * mean)).astype(jnp.bfloat16))
+        for part in range(2 * heads, 3 * heads):
+            parts.append(grad_ref[part, rows, :].astype(jnp.bfloat16))
+        back_ref[rows, :] = jnp.zeros((LANES, back_ref.shape[1]), jnp.bfloat16)
+        back_ref[rows, 0 : 3 * heads * HD] = jnp.concatenate(
+            [part[:, 0:HD] for part in parts], axis=1
+        )
+        return carry
+
+    lax.fori_loop(0, everyone // LANES, finish, 0)
+
+
+def qkv_weights_kernel(images, scalars, *refs):
+    pieces, refs = refs[:10], refs[10:]
+    hid_ref, back_ref, att_ref, qgrad_ref, ograd_ref, low_ref = refs
+    tokens, width = pieces[0].shape
+    mine = scalars[0]
+    blocks = hid_ref.shape[0] // tokens
+    heads = HEADS // blocks
+    gather_blocks(
+        pieces, low_ref, lambda index: pl.multiple_of((mine ^ index) * tokens, 16), tokens
+    )
+    grad = dot_tn(hid_ref[...], back_ref[...]).astype(jnp.bfloat16)
+    qgrad_ref[...] = grad.reshape(qgrad_ref.shape)
+    outw = dot_tn(att_ref[...], low_ref[...]).astype(jnp.bfloat16)
+    share = width // images
+    for image in range(images):
+        for head in range(heads):
+            ograd_ref[image, HD * head : HD * (head + 1), :] = outw[
+                LANES * head : LANES * head + HD, share * image : share * (image + 1)
+            ]
+
+
+def join_kernel(images, grad_ref, ograd_ref, out_ref):
+    blocks = grad_ref.shape[0]
+    span = HD * HEADS // blocks
+    whole = jnp.concatenate(
+        [
+            grad_ref[index][:, span * side : span * (side + 1)]
+            for side in range(3)
+            for index in range(blocks)
+        ],
+        axis=1,
+    )
+    share = whole.shape[1] // images
+    for image in range(images):
+        out_ref[image] = jnp.concatenate(
+            [whole[:, share * image : share * (image + 1)], ograd_ref[image]], axis=1
+        )
+
+
+def input_kernel(
+    back_ref, weight_ref, x_ref, mgrad_ref, mod_ref, sums_ref, gsum_ref, scalars,
+    grad_ref, send_ref, acc_ref, flat_ref,
+):
+    step = pl.program_id(0)
+    blocks = back_ref.shape[0]
+    span = HD * HEADS // blocks
+    width = x_ref.shape[1]
+    columns = 6 * width // blocks
+
+    for side in range(3):
+
+        @pl.when(step == side)
+        def _(side=side):
+            natural = jnp.concatenate(
+                [back_ref[index, :, span * side : span * (side + 1)] for index in range(blocks)],
+                axis=1,
+            )
+            part = dot_nt(natural, weight_ref[...])
+            acc_ref[...] = part if side == 0 else acc_ref[...] + part
+
+    @pl.when(step == 2)
+    def _():
+        x = x_ref[...]
+        back = acc_ref[...]
+        inverse = lax.rsqrt(jnp.mean(x * x, axis=-1, keepdims=True) + EPS)
+        unit = x * inverse
+        lifted = back * (1.0 + mod_ref[1:2, :])
+        grad_ref[...] = mgrad_ref[...] + inverse * (
+            lifted - unit * jnp.mean(lifted * unit, axis=-1, keepdims=True)
+        )
+        flat_ref[0:1, 0:width] = column_sum(back)
+        flat_ref[0:1, width : 2 * width] = column_sum(back * unit)
+        for index in range(2, 6):
+            flat_ref[0:1, width * index : width * (index + 1)] = sums_ref[index : index + 1, :]
+        send_ref[...] = jnp.zeros_like(send_ref)
+        for index in range(blocks):
+            send_ref[index : index + 1, 0:columns] = flat_ref[
+                0:1, columns * index : columns * (index + 1)
+            ]
+        send_ref[:, columns : columns + 1] = jnp.broadcast_to(
+            scalars[0].astype(jnp.float32), (blocks, 1)
+        )
+        for line in range(2):
+            start = columns + 16 + HD * line
+            send_ref[:, start : start + HD] = jnp.broadcast_to(
+                gsum_ref[line : line + 1, 0:HD], (blocks, HD)
+            )
+
+
+def whole_spec(shape):
+    return pl.BlockSpec(shape, lambda *_: (0,) * len(shape))
+
+
+def call(kernel, operands, outs, scratch=(), scalars=None, name=None, flops=0):
+    moved = sum(math.prod(a.shape) * a.dtype.itemsize for a in (*operands, *outs))
+    return pl.pallas_call(
+        kernel,
+        out_shape=outs,
+        grid_spec=pltpu.PrefetchScalarGridSpec(
+            num_scalar_prefetch=0 if scalars is None else 1,
+            grid=(1,),
+            in_specs=[
+                pl.BlockSpec(a.shape, lambda *_, n=len(a.shape): (0,) * n) for a in operands
+            ],
+            out_specs=[
+                pl.BlockSpec(o.shape, lambda *_, n=len(o.shape): (0,) * n) for o in outs
+            ],
+            scratch_shapes=list(scratch),
+        ),
+        cost_estimate=pl.CostEstimate(flops=flops, transcendentals=0, bytes_accessed=moved),
+        name=name,
+    )(*(() if scalars is None else (scalars,)), *operands)
+
+
+def struct(shape, dtype=jnp.float32):
+    return jax.ShapeDtypeStruct(shape, dtype)
+
+
+PLANE = ("ty", "tx")
+
+
+def swap(value, bit):
+    return lax.ppermute(value, PLANE, [(index, index ^ bit) for index in range(8)])
+
+
+def gather_plane(value, half):
+    core, xn, yn = swap(value, 2), swap(value, 1), swap(value, 4)
+    d1 = swap(xn[:half], 4)
+    cx = swap(xn, 2)
+    d2 = swap(yn[half:], 1)
+    cy = swap(yn, 2)
+    return (value, core, xn, yn, d1, d2, cx, cy, swap(d1, 2), swap(d2, 2))
+
+
+def exchange(value, axes=PLANE):
+    return lax.all_to_all(value, axes, split_axis=0, concat_axis=0, tiled=True)
+
+
+def line_reduce(pick, images):
+    place = lax.axis_index("img")
+    rising = falling = None
+    for step in range(1, images):
+        value = pick(jnp.clip(place + images - step, 0, images - 1))
+        if rising is not None:
+            value = value + rising.astype(jnp.float32)
+        rising = lax.ppermute(
+            value.astype(jnp.bfloat16),
+            "img",
+            [(i, i + 1) for i in range(images - 1) if i + images - step < images],
+        )
+        value = pick(jnp.clip(place - images + step, 0, images - 1))
+        if falling is not None:
+            value = value + falling.astype(jnp.float32)
+        falling = lax.ppermute(
+            value.astype(jnp.bfloat16),
+            "img",
+            [(i, i - 1) for i in range(1, images) if i - images + step >= 0],
+        )
+    return pick(place) + rising.astype(jnp.float32) + falling.astype(jnp.float32)
+
+
+def on_plane(
+    images,
+    block_in,
+    bucket,
+    tile_anchor,
+    cond_table,
+    mod_weight,
+    mod_bias,
+    qkv_weight,
+    query_gain,
+    key_gain,
+    out_weight,
+    gate_up_weight,
+    down_weight,
+    cotangent,
+):
+    blocks = 8
+    _, tile_rows, tile_cols, width = block_in.shape
+    tokens = tile_rows * tile_cols
+    everyone = blocks * tokens
+    hidden_units = down_weight.shape[0]
+    units = hidden_units // blocks
+    heads = HEADS // blocks
+    span = heads * HD
+    columns = mod_weight.shape[1]
+    bf16 = jnp.bfloat16
+    image = lax.axis_index("img")
+    mine = lax.axis_index("ty") * 2 + lax.axis_index("tx")
+    where = mine.reshape(1).astype(jnp.int32)
+    x = block_in.reshape(tokens, width)
+    cot = cotangent.reshape(tokens, width)
+    half = tokens // 2
+    pay, low_cot = call(
+        open_kernel,
+        (x, cond_table, mod_weight, mod_bias.reshape(1, columns), cot),
+        (struct((tokens + EXTRA, width), bf16), struct((tokens, width), bf16)),
+        [pltpu.VMEM((8, width), jnp.float32)],
+        jnp.concatenate([bucket, tile_anchor.reshape(2)]),
+        "open",
+    )
+    pieces = gather_plane(pay, half)
+    cot_pieces = gather_plane(low_cot, half)
+    own_weight = jnp.concatenate(
+        [
+            lax.dynamic_slice(qkv_weight, (0, width * side + span * mine), (width, span))
+            for side in range(3)
+        ],
+        axis=1,
+    )
+    gains = (query_gain.reshape(1, HD), key_gain.reshape(1, HD))
+    att, hid, qkv, raw, turn, mod = call(
+        functools.partial(attend_kernel, blocks, tile_cols),
+        (*pieces, own_weight, *gains),
+        (
+            struct((everyone, LANES * heads), bf16),
+            struct((everyone, width), bf16),
+            struct((3 * heads, everyone, LANES), bf16),
+            struct((2 * heads, everyone, LANES)),
+            struct((2, everyone, LANES)),
+            struct((8, width)),
+        ),
+        [
+            pltpu.VMEM((width, 3 * heads * LANES), bf16),
+            pltpu.VMEM((8, width), jnp.float32),
+            pltpu.VMEM((1, 6 * width), jnp.float32),
+            pltpu.VMEM((2, 8, LANES), jnp.float32),
+            pltpu.VMEM((2, 8, LANES), jnp.float32),
+            pltpu.VMEM((LANES, everyone), bf16),
+        ],
+        where,
+        "attend",
+        4 * everyone * everyone * LANES * heads,
+    )
+    att_all = exchange(att.reshape(blocks, tokens, LANES * heads))
+    attn_out, middle, hidden_mid = call(
+        middle_kernel,
+        (att_all, out_weight, x, mod),
+        (struct((tokens, width)), struct((tokens, width)), struct((tokens, width), bf16)),
+        name="middle",
+    )
+    hid_pieces = gather_plane(hidden_mid, half)
+    steps = blocks
+    whole = whole_spec
+    output, middle_grad, attn_grad, attg, sums = pl.pallas_call(
+        mlp_kernel,
+        out_shape=(
+            struct((tokens, width)),
+            struct((tokens, width)),
+            struct((tokens, width), bf16),
+            struct((blocks, tokens, LANES * heads), bf16),
+            struct((8, width)),
+        ),
+        grid=(steps,),
+        in_specs=[
+            pl.BlockSpec((width, units), lambda f: (0, f)),
+            pl.BlockSpec((width, units), lambda f: (0, steps + f)),
+            pl.BlockSpec((units, width), lambda f: (f, 0)),
+            whole(out_weight.shape),
+            whole((tokens, width)),
+            whole((tokens, width)),
+            whole((tokens, width)),
+            whole((tokens, width)),
+            whole((8, width)),
+        ],
+        out_specs=(
+            whole((tokens, width)),
+            whole((tokens, width)),
+            whole((tokens, width)),
+            whole((blocks, tokens, LANES * heads)),
+            whole((8, width)),
+        ),
+        scratch_shapes=[
+            pltpu.VMEM((tokens, width), bf16),
+            pltpu.VMEM((tokens, width), jnp.float32),
+            pltpu.VMEM((tokens, width), jnp.float32),
+        ],
+        name="mlp",
+    )(gate_up_weight, gate_up_weight, down_weight, out_weight, hidden_mid, middle, attn_out, cot, mod)
+    grad_pieces = gather_plane(attn_grad, half)
+    gateup_part, down_part = pl.pallas_call(
+        mlp_weights_kernel,
+        out_shape=(
+            struct((blocks, 2, width // blocks, units), bf16),
+            struct((images, width // images, units), bf16),
+        ),
+        grid_spec=pltpu.PrefetchScalarGridSpec(
+            num_scalar_prefetch=1,
+            grid=(1,),
+            in_specs=[
+                *(whole(a.shape) for a in (*hid_pieces, *cot_pieces)),
+                pl.BlockSpec((width, units), lambda i, s: (0, s[0])),
+                pl.BlockSpec((width, units), lambda i, s: (0, blocks + s[0])),
+                pl.BlockSpec((units, width), lambda i, s: (s[0], 0)),
+                whole((8, width)),
+            ],
+            out_specs=(
+                whole((blocks, 2, width // blocks, units)),
+                whole((images, width // images, units)),
+            ),
+            scratch_shapes=[
+                pltpu.VMEM((everyone, width), bf16),
+                pltpu.VMEM((everyone, width), bf16),
+                pltpu.VMEM((3, everyone, units), bf16),
+            ],
+        ),
+        name="mlp_weights",
+    )(where, *hid_pieces, *cot_pieces, gate_up_weight, gate_up_weight, down_weight, mod)
+    gateup_rows = exchange(gateup_part)
+
+    def pick_mlp(owner):
+        gateup = lax.dynamic_slice(
+            gateup_rows,
+            (4 * (owner % 2), owner // 2, 0, 0),
+            (4, 1, width // blocks, units),
+        ).reshape(4 * width // blocks, units)
+        down = lax.dynamic_index_in_dim(down_part, owner, 0, False)
+        return jnp.concatenate([gateup, down], axis=0).astype(jnp.float32)
+
+    mlp_total = line_reduce(pick_mlp, images)
+    attg_all = exchange(attg)
+    back, gain_sums = call(
+        attend_back_kernel,
+        (attg_all.reshape(everyone, LANES * heads), qkv, raw, turn, *gains),
+        (struct((everyone, 512), bf16), struct((8, LANES))),
+        [
+            pltpu.VMEM((LANES, everyone), bf16),
+            pltpu.VMEM((LANES, everyone), bf16),
+            pltpu.VMEM((3 * heads, everyone, LANES), jnp.float32),
+            pltpu.VMEM((2, 8, LANES), jnp.float32),
+        ],
+        None,
+        "attend_back",
+        10 * everyone * everyone * LANES * heads,
+    )
+    back_all = exchange(back.reshape(blocks, tokens, 512))
+    qkv_part, outw_part = call(
+        functools.partial(qkv_weights_kernel, images),
+        (*grad_pieces, hid, back, att),
+        (
+            struct((blocks, width // blocks, 512), bf16),
+            struct((images, span, width // images), bf16),
+        ),
+        [pltpu.VMEM((everyone, width), bf16)],
+        where,
+        "qkv_weights",
+    )
+    qkv_rows = exchange(qkv_part)
+    (joined,) = call(
+        functools.partial(join_kernel, images),
+        (qkv_rows, outw_part),
+        (struct((images, width // blocks, (3 * width + width) // images), bf16),),
+        name="join",
+    )
+    attn_total = line_reduce(
+        lambda owner: lax.dynamic_index_in_dim(joined, owner, 0, False).astype(jnp.float32),
+        images,
+    )
+    in_grad, send = pl.pallas_call(
+        input_kernel,
+        out_shape=(struct((tokens, width)), struct((blocks, 1024))),
+        grid=(3,),
+        in_specs=[
+            whole((blocks, tokens, 512)),
+            pl.BlockSpec((width, width), lambda s: (0, s)),
+            whole((tokens, width)),
+            whole((tokens, width)),
+            whole((8, width)),
+            whole((8, width)),
+            whole((8, LANES)),
+            pl.BlockSpec(memory_space=pltpu.SMEM),
+        ],
+        out_specs=(whole((tokens, width)), whole((blocks, 1024))),
+        scratch_shapes=[
+            pltpu.VMEM((tokens, width), jnp.float32),
+            pltpu.VMEM((1, 6 * width), jnp.float32),
+        ],
+        name="input",
+    )(back_all, qkv_weight, x, middle_grad, mod, sums, gain_sums, bucket)
+    everywhere = exchange(
+        jnp.broadcast_to(send[None], (images, blocks, 1024)).reshape(images * blocks, 1, 1024),
+        ("img", "ty", "tx"),
+    ).reshape(images, blocks, 1024)
+    mod_cols = jnp.sum(everywhere[:, :, :columns], axis=1)
+    buckets = everywhere[:, 0, columns]
+    gain_total = jnp.sum(everywhere[:, :, columns + 16 : columns + 16 + 2 * HD], axis=(0, 1))
+    share = width // images
+    table_part = lax.dynamic_slice(cond_table, (0, share * image), (cond_table.shape[0], share))
+    onehot = (
+        buckets[:, None] == jnp.arange(cond_table.shape[0], dtype=jnp.float32)[None, :]
+    ).astype(jnp.float32)
+    condition = jnp.dot(onehot, table_part, precision=PRECISE)
+    cond_act = jax.nn.silu(condition).astype(bf16).astype(jnp.float32)
+    modw_total = jnp.dot(cond_act.T, mod_cols, precision=PRECISE)
+    modb_total = jnp.sum(mod_cols, axis=0)
+    weight_part = lax.dynamic_slice(mod_weight, (share * image, 0), (share, columns))
+    act_part = jnp.dot(mod_cols, weight_part.astype(jnp.float32).T, precision=PRECISE)
+    act_grad = jnp.sum(
+        exchange(jnp.broadcast_to(act_part[None], (blocks, images, share))), axis=0
+    )
+    cond_grad = act_grad * silu_slope(condition)
+    lines = cond_table.shape[0] // blocks
+    own_hot = lax.dynamic_slice(onehot, (0, lines * mine), (images, lines))
+    table_total = jnp.dot(own_hot.T, cond_grad, precision=PRECISE)
+    rows = width // blocks
+    gateup_total = (
+        mlp_total[: 4 * rows].reshape(4, rows, units).transpose(1, 0, 2).reshape(rows, 4 * units)
+    )
+    down_total = mlp_total[4 * rows :].T
+    return (
+        output.reshape(block_in.shape),
+        in_grad.reshape(block_in.shape),
+        table_total,
+        modw_total,
+        modb_total,
+        attn_total[:, : 3 * share],
+        gain_total[:HD],
+        gain_total[HD:],
+        attn_total[:, 3 * share :],
+        gateup_total,
+        down_total,
+    )
+
+
 def solution(mesh):
+    sizes = mesh.shape
+    fits = sizes["ty"] == 4 and sizes["tx"] == 2 and sizes["img"] == 4
     return jax.shard_map(
-        on_device,
+        functools.partial(on_plane, sizes["img"]) if fits else on_device,
         mesh=mesh,
         in_specs=(
             P("img", "ty", "tx", None),

time: 892 us -> 338 us (0.38)
  waiting for transfers between devices: 595 us -> 103 us
  Pallas kernels: 0 us -> 95.2 us
  matrix products: 93.8 us -> 5.19 us
  starting transfers between devices: 0.92 us -> 70 us
  blocking collectives: 76.2 us -> 26.8 us
  local copies, waits for them, and re-layouts: 70.3 us -> 23.7 us
  other arithmetic: 31.3 us -> 10.7 us
  between operations: 17.5 us -> 2.07 us
    reduce_scatter x7 -> x0, waiting for transfers between devices: 393 us -> none  [the longest x1 102 us: on_device(): lax.psum_scatter(gateup_grad.astype(jnp.bfloat16), ('ty', 'tx'), scatter_...]
    unnamed x22 -> x0, waiting for transfers between devices: 109 us -> none
    pallas_call x0 -> x9, Pallas kernels: none -> 95.2 us  [the longest x6 53.1 us: call(): pl.pallas_call(kernel, out_shape=outs, grid_spec=pltpu.PrefetchScalarGrid...]
    ppermute x0 -> x48, waiting for transfers between devices: none -> 89.5 us  [the longest x36 55.6 us: swap(): lax.ppermute(value, PLANE, [(index, index ^ bit) for index in range(8)])]
    dot_general x21 -> x4, matrix products: 93.8 us -> 5.19 us  [the longest x1 1.69 us: on_plane(): jnp.dot(mod_cols, weight_part.astype(jnp.float32).T, precision=PRECISE)]
    ppermute x0 -> x48, starting transfers between devices: none -> 50.6 us  [the longest x36 25.2 us: swap(): lax.ppermute(value, PLANE, [(index, index ^ bit) for index in range(8)])]
    psum x2 -> x0, blocking collectives: 50.5 us -> none  [the longest x1 39.4 us: on_device(): lax.psum((qgain_part, kgain_part), ('img', 'ty', 'tx'))]
    another operation x1 -> x0, waiting for transfers between devices: 48.2 us -> none
  transfers between devices with their start and end apart: 16 -> 53, of which waited for: 14 -> 18; matrix products, arithmetic and copies ran while one was open for 10% -> 8% of each run, Pallas kernels for 0% -> 9%
where the time goes in v1:
time: 338 us; the launch traced here: 337 us
  waiting for transfers between devices  103 us (30%)
  Pallas kernels  95.2 us (28%)
  starting transfers between devices  70 us (21%)
  blocking collectives  26.8 us (8%)
  local copies, waits for them, and re-layouts  23.7 us (7%)
  other arithmetic  10.7 us (3%)
  matrix products  5.19 us (2%)
    ppermute x36, waiting for transfers between devices, swap(): lax.ppermute(value, PLANE, [(index, index ^ bit) for index in range(8)])  55.6 us
    pallas_call x6, Pallas kernels, call(): pl.pallas_call(kernel, out_shape=outs, grid_spec=pltpu.PrefetchScalarGrid...  53.1 us
    ppermute x6, waiting for transfers between devices, line_reduce(): lax.ppermute(value.astype(jnp.bfloat16), 'img', [(i, i + 1) for i in rang...  27.5 us
    all_to_all x2, blocking collectives, exchange(): return lax.all_to_all(value, axes, split_axis=0, concat_axis=0, tiled=True)  26.8 us
    ppermute x36, starting transfers between devices, swap(): lax.ppermute(value, PLANE, [(index, index ^ bit) for index in range(8)])  25.2 us
    pallas_call x1, Pallas kernels, on_plane(): pl.pallas_call(mlp_kernel, out_shape=(struct((tokens, width)), struct((to...  20.3 us
    all_to_all x5, starting transfers between devices, exchange(): return lax.all_to_all(value, axes, split_axis=0, concat_axis=0, tiled=True)  19.4 us
    ppermute x6, starting transfers between devices, line_reduce(): lax.ppermute(value.astype(jnp.bfloat16), 'img', [(i, i + 1) for i in rang...  18.4 us
  transfers between devices with their start and end apart: 53, of which 18 were waited for; matrix products, arithmetic and copies ran while one was open for 8% of the time, Pallas kernels for 9%

profile of v1, /device:TPU:0, one launch (start us, length us, event | category | flops | bytes accessed | tf_op | source)
XLA Modules:
  0.0 336.5 jit_solution(4478609188961541947)
XLA Ops:
  1.3 4.1 %copy.34.weight_ref = bf16[1152,864]{1,0:T(8,128)(2,1)} copy(bf16[1152,864]{0,1:T(8,128)(2,1)} %param.17) | data formatting | bytes 3981312 | tf_op args[4]
  6.6 3.8 %open.1 = (bf16[144,1152]{1,0:T(8,128)(2,1)}, bf16[128,1152]{1,0:T(8,128)(2,1)}) custom-call(s32[3]{0:T(128)} %pad_add_fusion.scalars, f32[128,1152]{1,0:T(8,128)} %bitcast.63, f32[32,1152]{1,0:T(8,128)} %table_ref.1, bf16[1152,864]{1,0:T(8,128)(2,1)} %copy.34.weight_ref, f32[1,864]{1,0:T(1,128)} %reshape.107.bias_ref, f32[128,1152]{1,0:T(8,128)} %bitcast.68), custom_call_target="tpu_custom_call" | custom-call | bytes 3947904 | tf_op jit(solution)/shard_map/open/pallas_call | solution.py:822
  10.4 2.9 collective-permute-start.1
  14.9 6.5 %collective-permute-done.1.refs_2_ = bf16[144,1152]{1,0:T(8,128)(2,1)S(1)} collective-permute-done((bf16[144,1152]{1,0:T(8,128)(2,1)}, bf16[144,1152]{1,0:T(8,128)(2,1)S(1)}, u32[]{:S(2)}, u32[]{:S(2)}) %collective-permute-start.1) | collective-permute-done | bytes 331808 | tf_op jit(solution)/shard_map/ppermute | solution.py:849
  21.4 1.8 collective-permute-start.3
  23.3 1.6 collective-permute-start.4
  25.3 2.6 constant_dynamic-slice_fusion.10
  28.9 1.8 pad_maximum_fusion.refs_10_
  31.8 17.4 %attend.1 = (bf16[1024,256]{1,0:T(8,128)(2,1)}, bf16[1024,1152]{1,0:T(8,128)(2,1)}, bf16[6,1024,128]{2,1,0:T(8,128)(2,1)}, f32[4,1024,128]{2,1,0:T(8,128)}, f32[2,1024,128]{2,1,0:T(8,128)}, /*index=5*/f32[8,1152]{1,0:T(8,128)}) custom-call(s32[1]{0:T(128)} %bitcast.scalars, bf16[144,1152]{1,0:T(8,128)(2,1)} %get-tuple-element.35.refs_0_, ...), custom_call_target="tpu_custom_call" | custom-call | flops 1073741824 | bytes 11289152 | tf_op jit(solution)/shard_map/attend/pallas_call | solution.py:822
  49.2 13.4 %all_to_all.35.att_ref = bf16[8,128,256]{2,1,0:T(8,128)(2,1)} all-to-all(bf16[8,128,256]{2,1,0:T(8,128)(2,1)} %bitcast.70), channel_id=1, replica_groups=mesh['img'=4,'ty'=4,'tx'=2] {'ty','tx'}, dimensions={0} | all-to-all | bytes 1048576 | tf_op jit(solution)/shard_map/all_to_all | solution.py:862
  62.5 3.8 %middle.1 = (f32[128,1152]{1,0:T(8,128)}, f32[128,1152]{1,0:T(8,128)}, bf16[128,1152]{1,0:T(8,128)(2,1)}) custom-call(bf16[8,128,256]{2,1,0:T(8,128)(2,1)} %all_to_all.35.att_ref, bf16[1152,1152]{1,0:T(8,128)(2,1)} %outw_ref.1, f32[128,1152]{1,0:T(8,128)} %bitcast.64, f32[8,1152]{1,0:T(8,128)} %get-tuple-element.37.mod_ref.refs_23_), custom_call_target="tpu_custom_call" | custom-call | bytes 5279744 | tf_op jit(solution)/shard_map/middle/pallas_call | solution.py:822
  66.3 20.3 %mlp.1 = (f32[128,1152]{1,0:T(8,128)}, f32[128,1152]{1,0:T(8,128)}, bf16[128,1152]{1,0:T(8,128)(2,1)}, bf16[8,128,256]{2,1,0:T(8,128)(2,1)}, f32[8,1152]{1,0:T(8,128)}) custom-call(bf16[1152,6144]{1,0:T(8,128)(2,1)} %refs_21_.1, bf16[1152,6144]{1,0:T(8,128)(2,1)} %refs_21_.1, bf16[3072,1152]{1,0:T(8,128)(2,1)} %refs_22_.1, bf16[1152,1152]{1,0:T(8,128)(2,1)} %outw_ref.1, ...), custom_call_target="tpu_custom_call" | custom-call | tf_op jit(solution)/shard_map/mlp/pallas_call | solution.py:971
  86.6 13.4 %all_to_all.36 = bf16[8,128,256]{2,1,0:T(8,128)(2,1)} all-to-all(bf16[8,128,256]{2,1,0:T(8,128)(2,1)} %get-tuple-element.42), channel_id=1, replica_groups=mesh['img'=4,'ty'=4,'tx'=2] {'ty','tx'}, dimensions={0} | all-to-all | bytes 1048576 | tf_op jit(solution)/shard_map/all_to_all | solution.py:862
  100.0 19.1 %attend_back.1 = (bf16[1024,512]{1,0:T(8,128)(2,1)}, f32[8,128]{1,0:T(8,128)}) custom-call(bf16[1024,256]{1,0:T(8,128)(2,1)} %bitcast.82, bf16[6,1024,128]{2,1,0:T(8,128)(2,1)} %get-tuple-element.43.qkv_ref, f32[4,1024,128]{2,1,0:T(8,128)} %get-tuple-element.44.raw_ref, f32[2,1024,128]{2,1,0:T(8,128)} %get-tuple-element.45.turn_ref, f32[1,72]{1,0:T(1,128)} %bitcast.87, ...), custom_call_target="tpu_custom_call" | custom-call | flops 2684354560 | bytes 6296128 | tf_op jit(solution)/shard_map/attend_back/pallas_call | solution.py:822
  119.1 3.7 %all-to-all-start.2 = ((bf16[8,128,512]{2,1,0:T(8,128)(2,1)}), bf16[8,128,512]{2,1,0:T(8,128)(2,1)S(1)}, u32[]{:S(2)}, u32[]{:S(2)}) async-start(bf16[8,128,512]{2,1,0:T(8,128)(2,1)} %bitcast.66), calls=%async_computation.2 | async-start | bytes 2097152 | tf_op jit(solution)/shard_map/all_to_all | solution.py:862
  122.8 1.9 collective-permute-start.10
  126.2 17.3 %collective-permute-done.10.refs_2_ = bf16[128,1152]{1,0:T(8,128)(2,1)S(1)} collective-permute-done((bf16[128,1152]{1,0:T(8,128)(2,1)S(1)}, bf16[128,1152]{1,0:T(8,128)(2,1)S(1)}, u32[]{:S(2)}, u32[]{:S(2)}) %collective-permute-start.10) | collective-permute-done | bytes 294944 | tf_op jit(solution)/shard_map/ppermute | solution.py:849
  145.7 1.6 collective-permute-start.34
  147.3 2.6 collective-permute-done.12.refs_4_
  154.1 5.8 %qkv_weights.1 = (bf16[8,144,512]{2,1,0:T(8,128)(2,1)}, bf16[4,144,288]{2,1,0:T(8,128)(2,1)}) custom-call(s32[1]{0:T(128)} %bitcast.scalars, bf16[128,1152]{1,0:T(8,128)(2,1)} %get-tuple-element.52.refs_0_, bf16[128,1152]{1,0:T(8,128)(2,1)} %copy-done.28, bf16[128,1152]{1,0:T(8,128)(2,1)} %copy-done.20, bf16[128,1152]{1,0:T(8,128)(2,1)} %copy-done.21, ...), custom_call_target="tpu_custom_call" | custom-call | bytes 7802880 | tf_op jit(solution)/shard_map/qkv_weights/pallas_call | solution.py:822
  159.9 3.7 %all-to-all-start.5 = ((bf16[8,144,512]{2,1,0:T(8,128)(2,1)}), bf16[8,144,512]{2,1,0:T(8,128)(2,1)S(1)}, u32[]{:S(2)}, u32[]{:S(2)}) async-start(bf16[8,144,512]{2,1,0:T(8,128)(2,1)} %get-tuple-element.54), calls=%async_computation.5 | async-start | bytes 2359296 | tf_op jit(solution)/shard_map/all_to_all | solution.py:862
  163.7 2.0 collective-permute-start.36
  167.9 15.2 %collective-permute-done.36.refs_14_ = bf16[64,1152]{1,0:T(8,128)(2,1)S(1)} collective-permute-done((bf16[64,1152]{1,0:T(8,128)(2,1)S(1)}, bf16[64,1152]{1,0:T(8,128)(2,1)S(1)}, u32[]{:S(2)}, u32[]{:S(2)}) %collective-permute-start.36) | collective-permute-done | bytes 147488 | tf_op jit(solution)/shard_map/ppermute | solution.py:849
  183.6 5.4 %collective-permute-done.25.refs_2_ = bf16[128,1152]{1,0:T(8,128)(2,1)S(1)} collective-permute-done((bf16[128,1152]{1,0:T(8,128)(2,1)S(1)}, bf16[128,1152]{1,0:T(8,128)(2,1)S(1)}, u32[]{:S(2)}, u32[]{:S(2)}) %collective-permute-start.25) | collective-permute-done | bytes 294944 | tf_op jit(solution)/shard_map/ppermute | solution.py:849
  193.2 2.7 collective-permute-done.27.refs_4_
  195.9 2.6 collective-permute-done.28.refs_5_
  198.6 1.7 collective-permute-done.32.refs_9_
  200.3 14.7 %mlp_weights.1 = (bf16[8,2,144,384]{3,2,1,0:T(8,128)(2,1)}, bf16[4,288,384]{2,1,0:T(8,128)(2,1)}) custom-call(s32[1]{0:T(128)} %bitcast.scalars, bf16[128,1152]{1,0:T(8,128)(2,1)} %get-tuple-element.38.hid_ref.refs_0_, bf16[128,1152]{1,0:T(8,128)(2,1)} %copy-done.26, bf16[128,1152]{1,0:T(8,128)(2,1)} %copy-done.18, bf16[128,1152]{1,0:T(8,128)(2,1)} %copy-done.19, ...), custom_call_target="tpu_custom_call" | custom-call | tf_op jit(solution)/shard_map/mlp_weights/pallas_call | solution.py:1007
  215.1 2.7 dynamic-slice_bitcast_fusion.8
  217.7 7.0 %input.1 = (f32[128,1152]{1,0:T(8,128)}, f32[8,1024]{1,0:T(8,128)}) custom-call(bf16[8,128,512]{2,1,0:T(8,128)(2,1)} %copy-done.2, bf16[1152,3456]{1,0:T(8,128)(2,1)} %weight_ref.4, f32[128,1152]{1,0:T(8,128)} %bitcast.65, f32[128,1152]{1,0:T(8,128)} %get-tuple-element.47.mgrad_ref, f32[8,1152]{1,0:T(8,128)} %get-tuple-element.37.mod_ref.refs_23_, ...), custom_call_target="tpu_custom_call" | custom-call | tf_op jit(solution)/shard_map/input/pallas_call | solution.py:1085
  226.4 4.4 %all-to-all-start.3 = ((f32[32,1,1024]{2,1,0:T(1,128)}), f32[32,1,1024]{2,1,0:T(1,128)S(1)}, u32[]{:S(2)}, u32[]{:S(2)}) async-start(f32[32,1,1024]{2,1,0:T(1,128)} %reshape.116), calls=%async_computation.3 | async-start | bytes 262144 | tf_op jit(solution)/shard_map/all_to_all | solution.py:862
  230.8 3.2 join.1
  234.1 2.0 dynamic-slice_bitcast_fusion.1
  236.0 4.4 %collective-permute-start.18 = (bf16[144,1152]{1,0:T(8,128)(2,1)}, bf16[144,1152]{1,0:T(8,128)(2,1)}, u32[]{:S(2)}, u32[]{:S(2)}) collective-permute-start(bf16[144,1152]{1,0:T(8,128)(2,1)} %get-tuple-element.73), channel_id=1, source_target_pairs={{0,8},{1,9},{2,10},{3,11},{4,12},{5,13},{6,14},{7,15}} | collective-permute-start | bytes 995336 | tf_op jit(solution)/shard_map/ppermute | solution.py:872
  241.8 3.6 %all-to-all-start.6 = ((bf16[8,2,144,384]{3,2,1,0:T(8,128)(2,1)}), bf16[8,2,144,384]{3,2,1,0:T(8,128)(2,1)S(1)}, u32[]{:S(2)}, u32[]{:S(2)}) async-start(bf16[8,2,144,384]{3,2,1,0:T(8,128)(2,1)} %get-tuple-element.57), calls=%async_computation.6 | async-start | bytes 3538944 | tf_op jit(solution)/shard_map/all_to_all | solution.py:862
  247.5 1.7 fusion.5
  249.7 1.6 fusion.17
  251.3 1.8 fusion.2
  253.1 2.0 collective-permute-start.19
  255.1 13.0 %all-to-all-done.6 = bf16[8,2,144,384]{3,2,1,0:T(8,128)(2,1)S(1)} async-done(((bf16[8,2,144,384]{3,2,1,0:T(8,128)(2,1)}), bf16[8,2,144,384]{3,2,1,0:T(8,128)(2,1)S(1)}, u32[]{:S(2)}, u32[]{:S(2)}) %all-to-all-start.6) | async-done | bytes 1769504 | tf_op jit(solution)/shard_map/all_to_all | solution.py:862
  268.8 4.0 %all-to-all-start.4 = ((f32[8,4,288]{2,1,0:T(4,128)}), f32[8,4,288]{2,1,0:T(4,128)}, u32[]{:S(2)}, u32[]{:S(2)}) async-start(f32[8,4,288]{2,1,0:T(4,128)} %broadcast_in_dim.5), calls=%async_computation.4 | async-start | bytes 98304 | tf_op jit(solution)/shard_map/all_to_all | solution.py:862
  278.5 1.7 collective-permute-start.42
  285.6 9.5 %collective-permute-done.42 = bf16[864,384]{1,0:T(8,128)(2,1)S(1)} collective-permute-done((bf16[864,384]{1,0:T(8,128)(2,1)S(1)}, bf16[864,384]{1,0:T(8,128)(2,1)S(1)}, u32[]{:S(2)}, u32[]{:S(2)}) %collective-permute-start.42) | collective-permute-done | bytes 663584 | tf_op jit(solution)/shard_map/ppermute | solution.py:872
  295.3 4.6 %collective-permute-start.43 = (bf16[864,384]{1,0:T(8,128)(2,1)S(1)}, bf16[864,384]{1,0:T(8,128)(2,1)S(1)}, u32[]{:S(2)}, u32[]{:S(2)}) collective-permute-start(bf16[864,384]{1,0:T(8,128)(2,1)S(1)} %add_convert_fusion.3), channel_id=1, source_target_pairs={{0,8},{8,16},{1,9},{9,17},{2,10},{10,18},{3,11},{11,19},{4,12},{12... | collective-permute-start | bytes 1990664 | tf_op jit(solution)/shard_map/ppermute | solution.py:872
  302.8 13.1 %collective-permute-done.43 = bf16[864,384]{1,0:T(8,128)(2,1)S(1)} collective-permute-done((bf16[864,384]{1,0:T(8,128)(2,1)S(1)}, bf16[864,384]{1,0:T(8,128)(2,1)S(1)}, u32[]{:S(2)}, u32[]{:S(2)}) %collective-permute-start.43) | collective-permute-done | bytes 663584 | tf_op jit(solution)/shard_map/ppermute | solution.py:872
  316.1 4.4 %collective-permute-start.44 = (bf16[864,384]{1,0:T(8,128)(2,1)S(1)}, bf16[864,384]{1,0:T(8,128)(2,1)S(1)}, u32[]{:S(2)}, u32[]{:S(2)}) collective-permute-start(bf16[864,384]{1,0:T(8,128)(2,1)S(1)} %add_convert_fusion.2), channel_id=1, source_target_pairs={{0,8},{8,16},{16,24},{1,9},{9,17},{17,25},{2,10},{10,18},{18,26},{... | collective-permute-start | bytes 1990664 | tf_op jit(solution)/shard_map/ppermute | solution.py:872
  323.2 6.4 %collective-permute-done.47 = bf16[864,384]{1,0:T(8,128)(2,1)S(1)} collective-permute-done((bf16[864,384]{1,0:T(8,128)(2,1)S(1)}, bf16[864,384]{1,0:T(8,128)(2,1)S(1)}, u32[]{:S(2)}, u32[]{:S(2)}) %collective-permute-start.47) | collective-permute-done | bytes 663584 | tf_op jit(solution)/shard_map/ppermute | solution.py:880
  329.6 4.8 %collective-permute-done.44 = bf16[864,384]{1,0:T(8,128)(2,1)S(1)} collective-permute-done((bf16[864,384]{1,0:T(8,128)(2,1)S(1)}, bf16[864,384]{1,0:T(8,128)(2,1)S(1)}, u32[]{:S(2)}, u32[]{:S(2)}) %collective-permute-start.44) | collective-permute-done | bytes 663584 | tf_op jit(solution)/shard_map/ppermute | solution.py:872
  (217 shorter events, 45.1 us)
Async XLA Ops:
  10.4 10.9 %collective-permute-start.1 = (bf16[144,1152]{1,0:T(8,128)(2,1)}, bf16[144,1152]{1,0:T(8,128)(2,1)S(1)}, u32[]{:S(2)}, u32[]{:S(2)}) collective-permute-start(bf16[144,1152]{1,0:T(8,128)(2,1)} %get-tuple-element.35.refs_0_), channel_id=1, source_target_pairs={{0,1},{1,0},{2,3},{3,2},{4,5},{5,4},{6,7},{7,6},{8,9},{9,8},{10,11... | collective-permute-start | bytes 995336 | tf_op jit(solution)/shard_map/ppermute | solution.py:849
  13.4 9.9 %collective-permute-start.2 = (bf16[144,1152]{1,0:T(8,128)(2,1)}, bf16[144,1152]{1,0:T(8,128)(2,1)S(1)}, u32[]{:S(2)}, u32[]{:S(2)}) collective-permute-start(bf16[144,1152]{1,0:T(8,128)(2,1)} %get-tuple-element.35.refs_0_), channel_id=1, source_target_pairs={{0,4},{1,5},{2,6},{3,7},{4,0},{5,1},{6,2},{7,3},{8,12},{9,13},{10,... | collective-permute-start | bytes 995336 | tf_op jit(solution)/shard_map/ppermute | solution.py:849
  14.9 15.8 %collective-permute-start = (bf16[144,1152]{1,0:T(8,128)(2,1)}, bf16[144,1152]{1,0:T(8,128)(2,1)S(1)}, u32[]{:S(2)}, u32[]{:S(2)}) collective-permute-start(bf16[144,1152]{1,0:T(8,128)(2,1)} %get-tuple-element.35.refs_0_), channel_id=1, source_target_pairs={{0,2},{1,3},{2,0},{3,1},{4,6},{5,7},{6,4},{7,5},{8,10},{9,11},{10,... | collective-permute-start | bytes 995336 | tf_op jit(solution)/shard_map/ppermute | solution.py:849
  21.4 6.6 %collective-permute-start.3 = (bf16[64,1152]{1,0:T(8,128)(2,1)S(1)}, bf16[64,1152]{1,0:T(8,128)(2,1)S(1)}, u32[]{:S(2)}, u32[]{:S(2)}) collective-permute-start(bf16[64,1152]{1,0:T(8,128)(2,1)S(1)} %slice.68), channel_id=1, source_target_pairs={{0,4},{1,5},{2,6},{3,7},{4,0},{5,1},{6,2},{7,3},{8,12},{9,13},{10,... | collective-permute-start | bytes 442376 | tf_op jit(solution)/shard_map/ppermute | solution.py:849
  23.3 5.6 %collective-permute-start.4 = (bf16[80,1152]{1,0:T(8,128)(2,1)S(1)}, bf16[80,1152]{1,0:T(8,128)(2,1)S(1)}, u32[]{:S(2)}, u32[]{:S(2)}) collective-permute-start(bf16[80,1152]{1,0:T(8,128)(2,1)S(1)} %slice.69), channel_id=1, source_target_pairs={{0,1},{1,0},{2,3},{3,2},{4,5},{5,4},{6,7},{7,6},{8,9},{9,8},{10,11... | collective-permute-start | bytes 552968 | tf_op jit(solution)/shard_map/ppermute | solution.py:849
  24.8 5.9 %collective-permute-start.5 = (bf16[144,1152]{1,0:T(8,128)(2,1)S(1)}, bf16[144,1152]{1,0:T(8,128)(2,1)S(1)}, u32[]{:S(2)}, u32[]{:S(2)}) collective-permute-start(bf16[144,1152]{1,0:T(8,128)(2,1)S(1)} %collective-permute-done.1.refs_2_), channel_id=1, source_target_pairs={{0,2},{1,3},{2,0},{3,1},{4,6},{5,7},{6,4},{7,5},{8,10},{9,11},{10,... | collective-permute-start | bytes 995336 | tf_op jit(solution)/shard_map/ppermute | solution.py:849
  24.8 6.0 %collective-permute-start.6 = (bf16[144,1152]{1,0:T(8,128)(2,1)S(1)}, bf16[144,1152]{1,0:T(8,128)(2,1)S(1)}, u32[]{:S(2)}, u32[]{:S(2)}) collective-permute-start(bf16[144,1152]{1,0:T(8,128)(2,1)S(1)} %collective-permute-done.2.refs_3_), channel_id=1, source_target_pairs={{0,2},{1,3},{2,0},{3,1},{4,6},{5,7},{6,4},{7,5},{8,10},{9,11},{10,... | collective-permute-start | bytes 995336 | tf_op jit(solution)/shard_map/ppermute | solution.py:849
  28.0 2.7 collective-permute-start.7
  119.1 40.8 %all-to-all-start.2 = ((bf16[8,128,512]{2,1,0:T(8,128)(2,1)}), bf16[8,128,512]{2,1,0:T(8,128)(2,1)S(1)}, u32[]{:S(2)}, u32[]{:S(2)}) async-start(bf16[8,128,512]{2,1,0:T(8,128)(2,1)} %bitcast.66), calls=%async_computation.2 | async-start | bytes 2097152 | tf_op jit(solution)/shard_map/all_to_all | solution.py:862
  122.8 20.7 %collective-permute-start.10 = (bf16[128,1152]{1,0:T(8,128)(2,1)S(1)}, bf16[128,1152]{1,0:T(8,128)(2,1)S(1)}, u32[]{:S(2)}, u32[]{:S(2)}) collective-permute-start(bf16[128,1152]{1,0:T(8,128)(2,1)S(1)} %copy-done.27), channel_id=1, source_target_pairs={{0,1},{1,0},{2,3},{3,2},{4,5},{5,4},{6,7},{7,6},{8,9},{9,8},{10,11... | collective-permute-start | bytes 884744 | tf_op jit(solution)/shard_map/ppermute | solution.py:849
  124.7 20.4 %collective-permute-start.11 = (bf16[128,1152]{1,0:T(8,128)(2,1)S(1)}, bf16[128,1152]{1,0:T(8,128)(2,1)S(1)}, u32[]{:S(2)}, u32[]{:S(2)}) collective-permute-start(bf16[128,1152]{1,0:T(8,128)(2,1)S(1)} %copy-done.27), channel_id=1, source_target_pairs={{0,4},{1,5},{2,6},{3,7},{4,0},{5,1},{6,2},{7,3},{8,12},{9,13},{10,... | collective-permute-start | bytes 884744 | tf_op jit(solution)/shard_map/ppermute | solution.py:849
  126.2 19.5 %collective-permute-start.9 = (bf16[128,1152]{1,0:T(8,128)(2,1)S(1)}, bf16[128,1152]{1,0:T(8,128)(2,1)S(1)}, u32[]{:S(2)}, u32[]{:S(2)}) collective-permute-start(bf16[128,1152]{1,0:T(8,128)(2,1)S(1)} %copy-done.27), channel_id=1, source_target_pairs={{0,2},{1,3},{2,0},{3,1},{4,6},{5,7},{6,4},{7,5},{8,10},{9,11},{10,... | collective-permute-start | bytes 884744 | tf_op jit(solution)/shard_map/ppermute | solution.py:849
  143.5 8.3 %collective-permute-start.14 = (bf16[128,1152]{1,0:T(8,128)(2,1)S(1)}, bf16[128,1152]{1,0:T(8,128)(2,1)S(1)}, u32[]{:S(2)}, u32[]{:S(2)}) collective-permute-start(bf16[128,1152]{1,0:T(8,128)(2,1)S(1)} %collective-permute-done.10.refs_2_), channel_id=1, source_target_pairs={{0,2},{1,3},{2,0},{3,1},{4,6},{5,7},{6,4},{7,5},{8,10},{9,11},{10,... | collective-permute-start | bytes 884744 | tf_op jit(solution)/shard_map/ppermute | solution.py:849
  143.5 6.3 %collective-permute-start.12 = (bf16[64,1152]{1,0:T(8,128)(2,1)S(1)}, bf16[64,1152]{1,0:T(8,128)(2,1)S(1)}, u32[]{:S(2)}, u32[]{:S(2)}) collective-permute-start(bf16[64,1152]{1,0:T(8,128)(2,1)S(1)} %slice.72), channel_id=1, source_target_pairs={{0,4},{1,5},{2,6},{3,7},{4,0},{5,1},{6,2},{7,3},{8,12},{9,13},{10,... | collective-permute-start | bytes 442376 | tf_op jit(solution)/shard_map/ppermute | solution.py:849
  145.1 6.7 %collective-permute-start.13 = (bf16[64,1152]{1,0:T(8,128)(2,1)S(1)}, bf16[64,1152]{1,0:T(8,128)(2,1)S(1)}, u32[]{:S(2)}, u32[]{:S(2)}) collective-permute-start(bf16[64,1152]{1,0:T(8,128)(2,1)S(1)} %slice.73), channel_id=1, source_target_pairs={{0,1},{1,0},{2,3},{3,2},{4,5},{5,4},{6,7},{7,6},{8,9},{9,8},{10,11... | collective-permute-start | bytes 442376 | tf_op jit(solution)/shard_map/ppermute | solution.py:849
  145.7 6.7 %collective-permute-start.15 = (bf16[128,1152]{1,0:T(8,128)(2,1)S(1)}, bf16[128,1152]{1,0:T(8,128)(2,1)S(1)}, u32[]{:S(2)}, u32[]{:S(2)}) collective-permute-start(bf16[128,1152]{1,0:T(8,128)(2,1)S(1)} %collective-permute-done.11.refs_3_), channel_id=1, source_target_pairs={{0,2},{1,3},{2,0},{3,1},{4,6},{5,7},{6,4},{7,5},{8,10},{9,11},{10,... | collective-permute-start | bytes 884744 | tf_op jit(solution)/shard_map/ppermute | solution.py:849
  145.7 17.9 %collective-permute-start.34 = (bf16[128,1152]{1,0:T(8,128)(2,1)S(1)}, bf16[128,1152]{1,0:T(8,128)(2,1)S(1)}, u32[]{:S(2)}, u32[]{:S(2)}) collective-permute-start(bf16[128,1152]{1,0:T(8,128)(2,1)S(1)} %copy-done.22), channel_id=1, source_target_pairs={{0,1},{1,0},{2,3},{3,2},{4,5},{5,4},{6,7},{7,6},{8,9},{9,8},{10,11... | collective-permute-start | bytes 884744 | tf_op jit(solution)/shard_map/ppermute | solution.py:849
  149.8 15.8 %collective-permute-start.35 = (bf16[128,1152]{1,0:T(8,128)(2,1)S(1)}, bf16[128,1152]{1,0:T(8,128)(2,1)S(1)}, u32[]{:S(2)}, u32[]{:S(2)}) collective-permute-start(bf16[128,1152]{1,0:T(8,128)(2,1)S(1)} %copy-done.22), channel_id=1, source_target_pairs={{0,4},{1,5},{2,6},{3,7},{4,0},{5,1},{6,2},{7,3},{8,12},{9,13},{10,... | collective-permute-start | bytes 884744 | tf_op jit(solution)/shard_map/ppermute | solution.py:849
  159.9 66.5 %all-to-all-start.5 = ((bf16[8,144,512]{2,1,0:T(8,128)(2,1)}), bf16[8,144,512]{2,1,0:T(8,128)(2,1)S(1)}, u32[]{:S(2)}, u32[]{:S(2)}) async-start(bf16[8,144,512]{2,1,0:T(8,128)(2,1)} %get-tuple-element.54), calls=%async_computation.5 | async-start | bytes 2359296 | tf_op jit(solution)/shard_map/all_to_all | solution.py:862
  163.7 19.4 %collective-permute-start.36 = (bf16[64,1152]{1,0:T(8,128)(2,1)S(1)}, bf16[64,1152]{1,0:T(8,128)(2,1)S(1)}, u32[]{:S(2)}, u32[]{:S(2)}) collective-permute-start(bf16[64,1152]{1,0:T(8,128)(2,1)S(1)} %slice.79), channel_id=1, source_target_pairs={{0,4},{1,5},{2,6},{3,7},{4,0},{5,1},{6,2},{7,3},{8,12},{9,13},{10,... | collective-permute-start | bytes 442376 | tf_op jit(solution)/shard_map/ppermute | solution.py:849
  165.7 17.4 %collective-permute-start.37 = (bf16[64,1152]{1,0:T(8,128)(2,1)S(1)}, bf16[64,1152]{1,0:T(8,128)(2,1)S(1)}, u32[]{:S(2)}, u32[]{:S(2)}) collective-permute-start(bf16[64,1152]{1,0:T(8,128)(2,1)S(1)} %slice.80), channel_id=1, source_target_pairs={{0,1},{1,0},{2,3},{3,2},{4,5},{5,4},{6,7},{7,6},{8,9},{9,8},{10,11... | collective-permute-start | bytes 442376 | tf_op jit(solution)/shard_map/ppermute | solution.py:849
  167.2 21.7 %collective-permute-start.25 = (bf16[128,1152]{1,0:T(8,128)(2,1)S(1)}, bf16[128,1152]{1,0:T(8,128)(2,1)S(1)}, u32[]{:S(2)}, u32[]{:S(2)}) collective-permute-start(bf16[128,1152]{1,0:T(8,128)(2,1)S(1)} %copy-done.8), channel_id=1, source_target_pairs={{0,1},{1,0},{2,3},{3,2},{4,5},{5,4},{6,7},{7,6},{8,9},{9,8},{10,11... | collective-permute-start | bytes 884744 | tf_op jit(solution)/shard_map/ppermute | solution.py:849
  167.8 21.1 %collective-permute-start.26 = (bf16[128,1152]{1,0:T(8,128)(2,1)S(1)}, bf16[128,1152]{1,0:T(8,128)(2,1)S(1)}, u32[]{:S(2)}, u32[]{:S(2)}) collective-permute-start(bf16[128,1152]{1,0:T(8,128)(2,1)S(1)} %copy-done.8), channel_id=1, source_target_pairs={{0,4},{1,5},{2,6},{3,7},{4,0},{5,1},{6,2},{7,3},{8,12},{9,13},{10,... | collective-permute-start | bytes 884744 | tf_op jit(solution)/shard_map/ppermute | solution.py:849
  167.9 21.6 %collective-permute-start.33 = (bf16[128,1152]{1,0:T(8,128)(2,1)S(1)}, bf16[128,1152]{1,0:T(8,128)(2,1)S(1)}, u32[]{:S(2)}, u32[]{:S(2)}) collective-permute-start(bf16[128,1152]{1,0:T(8,128)(2,1)S(1)} %copy-done.22), channel_id=1, source_target_pairs={{0,2},{1,3},{2,0},{3,1},{4,6},{5,7},{6,4},{7,5},{8,10},{9,11},{10,... | collective-permute-start | bytes 884744 | tf_op jit(solution)/shard_map/ppermute | solution.py:849
  183.0 6.6 %collective-permute-start.38 = (bf16[128,1152]{1,0:T(8,128)(2,1)S(1)}, bf16[128,1152]{1,0:T(8,128)(2,1)S(1)}, u32[]{:S(2)}, u32[]{:S(2)}) collective-permute-start(bf16[128,1152]{1,0:T(8,128)(2,1)S(1)} %collective-permute-done.34.refs_12_), channel_id=1, source_target_pairs={{0,2},{1,3},{2,0},{3,1},{4,6},{5,7},{6,4},{7,5},{8,10},{9,11},{10,... | collective-permute-start | bytes 884744 | tf_op jit(solution)/shard_map/ppermute | solution.py:849
  183.1 8.1 %collective-permute-start.39 = (bf16[128,1152]{1,0:T(8,128)(2,1)S(1)}, bf16[128,1152]{1,0:T(8,128)(2,1)S(1)}, u32[]{:S(2)}, u32[]{:S(2)}) collective-permute-start(bf16[128,1152]{1,0:T(8,128)(2,1)S(1)} %collective-permute-done.35.refs_13_), channel_id=1, source_target_pairs={{0,2},{1,3},{2,0},{3,1},{4,6},{5,7},{6,4},{7,5},{8,10},{9,11},{10,... | collective-permute-start | bytes 884744 | tf_op jit(solution)/shard_map/ppermute | solution.py:849
  188.9 3.1 collective-permute-start.41
  189.5 9.1 %collective-permute-start.24 = (bf16[128,1152]{1,0:T(8,128)(2,1)S(1)}, bf16[128,1152]{1,0:T(8,128)(2,1)S(1)}, u32[]{:S(2)}, u32[]{:S(2)}) collective-permute-start(bf16[128,1152]{1,0:T(8,128)(2,1)S(1)} %copy-done.8), channel_id=1, source_target_pairs={{0,2},{1,3},{2,0},{3,1},{4,6},{5,7},{6,4},{7,5},{8,10},{9,11},{10,... | collective-permute-start | bytes 884744 | tf_op jit(solution)/shard_map/ppermute | solution.py:849
  189.6 6.3 %collective-permute-start.27 = (bf16[64,1152]{1,0:T(8,128)(2,1)S(1)}, bf16[64,1152]{1,0:T(8,128)(2,1)}, u32[]{:S(2)}, u32[]{:S(2)}) collective-permute-start(bf16[64,1152]{1,0:T(8,128)(2,1)S(1)} %slice.77), channel_id=1, source_target_pairs={{0,4},{1,5},{2,6},{3,7},{4,0},{5,1},{6,2},{7,3},{8,12},{9,13},{10,... | collective-permute-start | bytes 442376 | tf_op jit(solution)/shard_map/ppermute | solution.py:849
  191.1 7.5 %collective-permute-start.29 = (bf16[128,1152]{1,0:T(8,128)(2,1)S(1)}, bf16[128,1152]{1,0:T(8,128)(2,1)}, u32[]{:S(2)}, u32[]{:S(2)}) collective-permute-start(bf16[128,1152]{1,0:T(8,128)(2,1)S(1)} %collective-permute-done.25.refs_2_), channel_id=1, source_target_pairs={{0,2},{1,3},{2,0},{3,1},{4,6},{5,7},{6,4},{7,5},{8,10},{9,11},{10,... | collective-permute-start | bytes 884744 | tf_op jit(solution)/shard_map/ppermute | solution.py:849
  191.9 6.7 %collective-permute-start.30 = (bf16[128,1152]{1,0:T(8,128)(2,1)S(1)}, bf16[128,1152]{1,0:T(8,128)(2,1)}, u32[]{:S(2)}, u32[]{:S(2)}) collective-permute-start(bf16[128,1152]{1,0:T(8,128)(2,1)S(1)} %collective-permute-done.26.refs_3_), channel_id=1, source_target_pairs={{0,2},{1,3},{2,0},{3,1},{4,6},{5,7},{6,4},{7,5},{8,10},{9,11},{10,... | collective-permute-start | bytes 884744 | tf_op jit(solution)/shard_map/ppermute | solution.py:849
  192.6 6.0 %collective-permute-start.28 = (bf16[64,1152]{1,0:T(8,128)(2,1)S(1)}, bf16[64,1152]{1,0:T(8,128)(2,1)}, u32[]{:S(2)}, u32[]{:S(2)}) collective-permute-start(bf16[64,1152]{1,0:T(8,128)(2,1)S(1)} %slice.78), channel_id=1, source_target_pairs={{0,1},{1,0},{2,3},{3,2},{4,5},{5,4},{6,7},{7,6},{8,9},{9,8},{10,11... | collective-permute-start | bytes 442376 | tf_op jit(solution)/shard_map/ppermute | solution.py:849
  195.9 2.7 collective-permute-start.31
  226.4 15.5 %all-to-all-start.3 = ((f32[32,1,1024]{2,1,0:T(1,128)}), f32[32,1,1024]{2,1,0:T(1,128)S(1)}, u32[]{:S(2)}, u32[]{:S(2)}) async-start(f32[32,1,1024]{2,1,0:T(1,128)} %reshape.116), calls=%async_computation.3 | async-start | bytes 262144 | tf_op jit(solution)/shard_map/all_to_all | solution.py:862
  236.0 15.3 %collective-permute-start.18 = (bf16[144,1152]{1,0:T(8,128)(2,1)}, bf16[144,1152]{1,0:T(8,128)(2,1)}, u32[]{:S(2)}, u32[]{:S(2)}) collective-permute-start(bf16[144,1152]{1,0:T(8,128)(2,1)} %get-tuple-element.73), channel_id=1, source_target_pairs={{0,8},{1,9},{2,10},{3,11},{4,12},{5,13},{6,14},{7,15}} | collective-permute-start | bytes 995336 | tf_op jit(solution)/shard_map/ppermute | solution.py:872
  240.5 39.7 %collective-permute-start.21 = (bf16[144,1152]{1,0:T(8,128)(2,1)}, bf16[144,1152]{1,0:T(8,128)(2,1)}, u32[]{:S(2)}, u32[]{:S(2)}) collective-permute-start(bf16[144,1152]{1,0:T(8,128)(2,1)} %get-tuple-element.74), channel_id=1, source_target_pairs={{24,16},{25,17},{26,18},{27,19},{28,20},{29,21},{30,22},{31,23}} | collective-permute-start | bytes 995336 | tf_op jit(solution)/shard_map/ppermute | solution.py:880
  241.8 26.3 %all-to-all-start.6 = ((bf16[8,2,144,384]{3,2,1,0:T(8,128)(2,1)}), bf16[8,2,144,384]{3,2,1,0:T(8,128)(2,1)S(1)}, u32[]{:S(2)}, u32[]{:S(2)}) async-start(bf16[8,2,144,384]{3,2,1,0:T(8,128)(2,1)} %get-tuple-element.57), calls=%async_computation.6 | async-start | bytes 3538944 | tf_op jit(solution)/shard_map/all_to_all | solution.py:862
  253.1 27.0 %collective-permute-start.19 = (bf16[144,1152]{1,0:T(8,128)(2,1)}, bf16[144,1152]{1,0:T(8,128)(2,1)}, u32[]{:S(2)}, u32[]{:S(2)}) collective-permute-start(bf16[144,1152]{1,0:T(8,128)(2,1)} %fusion.2), channel_id=1, source_target_pairs={{0,8},{8,16},{1,9},{9,17},{2,10},{10,18},{3,11},{11,19},{4,12},{12... | collective-permute-start | bytes 995336 | tf_op jit(solution)/shard_map/ppermute | solution.py:872
  268.8 8.8 %all-to-all-start.4 = ((f32[8,4,288]{2,1,0:T(4,128)}), f32[8,4,288]{2,1,0:T(4,128)}, u32[]{:S(2)}, u32[]{:S(2)}) async-start(f32[8,4,288]{2,1,0:T(4,128)} %broadcast_in_dim.5), calls=%async_computation.4 | async-start | bytes 98304 | tf_op jit(solution)/shard_map/all_to_all | solution.py:862
  275.1 8.5 %collective-permute-start.45 = (bf16[864,384]{1,0:T(8,128)(2,1)}, bf16[864,384]{1,0:T(8,128)(2,1)}, u32[]{:S(2)}, u32[]{:S(2)}) collective-permute-start(bf16[864,384]{1,0:T(8,128)(2,1)} %pad_maximum_fusion.2), channel_id=1, source_target_pairs={{24,16},{25,17},{26,18},{27,19},{28,20},{29,21},{30,22},{31,23}} | collective-permute-start | bytes 1990664 | tf_op jit(solution)/shard_map/ppermute | solution.py:880
  278.5 16.6 %collective-permute-start.42 = (bf16[864,384]{1,0:T(8,128)(2,1)S(1)}, bf16[864,384]{1,0:T(8,128)(2,1)S(1)}, u32[]{:S(2)}, u32[]{:S(2)}) collective-permute-start(bf16[864,384]{1,0:T(8,128)(2,1)S(1)} %pad_maximum_fusion.1), channel_id=1, source_target_pairs={{0,8},{1,9},{2,10},{3,11},{4,12},{5,13},{6,14},{7,15}} | collective-permute-start | bytes 1990664 | tf_op jit(solution)/shard_map/ppermute | solution.py:872
  281.5 18.4 %collective-permute-start.22 = (bf16[144,1152]{1,0:T(8,128)(2,1)S(1)}, bf16[144,1152]{1,0:T(8,128)(2,1)S(1)}, u32[]{:S(2)}, u32[]{:S(2)}) collective-permute-start(bf16[144,1152]{1,0:T(8,128)(2,1)S(1)} %get-tuple-element.72), channel_id=1, source_target_pairs={{16,8},{24,16},{17,9},{25,17},{18,10},{26,18},{19,11},{27,19},{20,... | collective-permute-start | bytes 995336 | tf_op jit(solution)/shard_map/ppermute | solution.py:880
  282.3 39.2 %collective-permute-start.20 = (bf16[144,1152]{1,0:T(8,128)(2,1)S(1)}, bf16[144,1152]{1,0:T(8,128)(2,1)S(1)}, u32[]{:S(2)}, u32[]{:S(2)}) collective-permute-start(bf16[144,1152]{1,0:T(8,128)(2,1)S(1)} %get-tuple-element.71), channel_id=1, source_target_pairs={{0,8},{8,16},{16,24},{1,9},{9,17},{17,25},{2,10},{10,18},{18,26},{... | collective-permute-start | bytes 995336 | tf_op jit(solution)/shard_map/ppermute | solution.py:872
  284.9 16.4 %collective-permute-start.46 = (bf16[864,384]{1,0:T(8,128)(2,1)S(1)}, bf16[864,384]{1,0:T(8,128)(2,1)S(1)}, u32[]{:S(2)}, u32[]{:S(2)}) collective-permute-start(bf16[864,384]{1,0:T(8,128)(2,1)S(1)} %add_convert_fusion.1), channel_id=1, source_target_pairs={{16,8},{24,16},{17,9},{25,17},{18,10},{26,18},{19,11},{27,19},{20,... | collective-permute-start | bytes 1990664 | tf_op jit(solution)/shard_map/ppermute | solution.py:880
  295.3 20.6 %collective-permute-start.43 = (bf16[864,384]{1,0:T(8,128)(2,1)S(1)}, bf16[864,384]{1,0:T(8,128)(2,1)S(1)}, u32[]{:S(2)}, u32[]{:S(2)}) collective-permute-start(bf16[864,384]{1,0:T(8,128)(2,1)S(1)} %add_convert_fusion.3), channel_id=1, source_target_pairs={{0,8},{8,16},{1,9},{9,17},{2,10},{10,18},{3,11},{11,19},{4,12},{12... | collective-permute-start | bytes 1990664 | tf_op jit(solution)/shard_map/ppermute | solution.py:872
  300.0 21.4 %collective-permute-start.23 = (bf16[144,1152]{1,0:T(8,128)(2,1)S(1)}, bf16[144,1152]{1,0:T(8,128)(2,1)S(1)}, u32[]{:S(2)}, u32[]{:S(2)}) collective-permute-start(bf16[144,1152]{1,0:T(8,128)(2,1)S(1)} %fusion.1), channel_id=1, source_target_pairs={{8,0},{16,8},{24,16},{9,1},{17,9},{25,17},{10,2},{18,10},{26,18},{... | collective-permute-start | bytes 995336 | tf_op jit(solution)/shard_map/ppermute | solution.py:880
  301.5 28.1 %collective-permute-start.47 = (bf16[864,384]{1,0:T(8,128)(2,1)S(1)}, bf16[864,384]{1,0:T(8,128)(2,1)S(1)}, u32[]{:S(2)}, u32[]{:S(2)}) collective-permute-start(bf16[864,384]{1,0:T(8,128)(2,1)S(1)} %add_convert_fusion), channel_id=1, source_target_pairs={{8,0},{16,8},{24,16},{9,1},{17,9},{25,17},{10,2},{18,10},{26,18},{... | collective-permute-start | bytes 1990664 | tf_op jit(solution)/shard_map/ppermute | solution.py:880
  316.1 18.3 %collective-permute-start.44 = (bf16[864,384]{1,0:T(8,128)(2,1)S(1)}, bf16[864,384]{1,0:T(8,128)(2,1)S(1)}, u32[]{:S(2)}, u32[]{:S(2)}) collective-permute-start(bf16[864,384]{1,0:T(8,128)(2,1)S(1)} %add_convert_fusion.2), channel_id=1, source_target_pairs={{0,8},{8,16},{16,24},{1,9},{9,17},{17,25},{2,10},{10,18},{18,26},{... | collective-permute-start | bytes 1990664 | tf_op jit(solution)/shard_map/ppermute | solution.py:872
  (56 other events, 402.4 us)

commit v2 on v0

--- a/solution.py
+++ b/solution.py
@@ -1,8 +1,11 @@
+import functools
 import math
 
 import jax
 import jax.numpy as jnp
 from jax import lax
+from jax.experimental import pallas as pl
+from jax.experimental.pallas import tpu as pltpu
 from jax.sharding import PartitionSpec as P
 
 HEADS = 16
@@ -306,9 +309,1206 @@
     )
 
 
+def sigmoid(value):
+    return 1.0 / (1.0 + jnp.exp(-value))
+
+
+def dot_nn(left, right):
+    return lax.dot_general(
+        left, right, (((1,), (0,)), ((), ())), preferred_element_type=jnp.float32
+    )
+
+
+def dot_nt(left, right):
+    return lax.dot_general(
+        left, right, (((1,), (1,)), ((), ())), preferred_element_type=jnp.float32
+    )
+
+
+def dot_tn(left, right):
+    return lax.dot_general(
+        left, right, (((0,), (0,)), ((), ())), preferred_element_type=jnp.float32
+    )
+
+
+def column_sum(value):
+    return jnp.sum(value, axis=0, keepdims=True)
+
+
+EXTRA = 16
+LANES = 128
+QUARTER = HD // 4
+PLACES = ((0, 0), (QUARTER, LANES // 2), (2 * QUARTER, QUARTER), (3 * QUARTER, LANES // 2 + QUARTER))
+
+
+def lane_entry(lane):
+    low = lane % (LANES // 2)
+    upper = lane // (LANES // 2)
+    column = low // QUARTER
+    entry = jnp.where(
+        low < 2 * QUARTER, low % QUARTER + QUARTER * upper + 2 * QUARTER * column, -1
+    )
+    return entry, column == 1
+
+
+def wide_row(row, ref, line):
+    for source, target in PLACES:
+        ref[line : line + 1, target : target + QUARTER] = row[:, source : source + QUARTER]
+
+
+def open_kernel(
+    bucket_ref, anchor_ref, x_ref, table_ref, weight_ref, bias_ref, cot_ref,
+    pay_ref, low_ref, wide_ref,
+):
+    tokens, width = x_ref.shape
+    columns = weight_ref.shape[0]
+    x = x_ref[...]
+    pay_ref[0:tokens, :] = normed(x).astype(jnp.bfloat16)
+    low_ref[...] = cot_ref[...].astype(jnp.bfloat16)
+    row = table_ref[pl.ds(bucket_ref[0], 1), :]
+    act = (row * sigmoid(row)).astype(jnp.bfloat16)
+    mod = dot_nt(jnp.broadcast_to(act, (8, width)), weight_ref[...])
+    wide_ref[...] = jnp.zeros_like(wide_ref)
+    wide_ref[:, 0:columns] = mod + bias_ref[...].reshape(1, columns)
+    full = wide_ref[0:1, :]
+    high = full.astype(jnp.bfloat16).astype(jnp.float32)
+    rest = full - high
+    middle = rest.astype(jnp.bfloat16).astype(jnp.float32)
+    least = rest - middle
+    lane = lax.broadcasted_iota(jnp.int32, (EXTRA, width), 1)
+    line = lax.broadcasted_iota(jnp.int32, (EXTRA, width), 0)
+    entry, column = lane_entry(lane % LANES)
+    anchor = jnp.where(
+        column, anchor_ref[1].astype(jnp.float32), anchor_ref[0].astype(jnp.float32)
+    )
+    anchor = jnp.where(entry >= 0, anchor, 0.0)
+    extra = jnp.where(
+        line == 0,
+        high,
+        jnp.where(
+            line == 1, middle, jnp.where(line == 2, least, jnp.where(line == 3, anchor, 0.0))
+        ),
+    )
+    pay_ref[tokens : tokens + EXTRA, :] = extra.astype(jnp.bfloat16)
+
+
+def ready_kernel(
+    blocks, tile_cols, scalars, *refs,
+):
+    qkv_parts, refs = refs[:6], refs[6:]
+    (
+        gate_a, gate_b, up_a, up_b, qgain_ref, kgain_ref, table_ref, modw_ref,
+        spread_ref, order_ref, turn_ref, gain_ref, gate_ref, up_ref, tshare_ref, mshare_ref,
+        window_ref, pick_ref,
+    ) = refs
+    mine = scalars[0]
+    share = tshare_ref.shape[1]
+    for image in range(table_ref.shape[1] // share):
+
+        @pl.when(scalars[1] == image)
+        def _(image=image):
+            tshare_ref[...] = table_ref[:, share * image : share * (image + 1)]
+            mshare_ref[...] = modw_ref[:, share * image : share * (image + 1)]
+
+    heads = HEADS // blocks
+    span = heads * HD
+    wide = 3 * heads * LANES
+    for index, part in enumerate(qkv_parts):
+        window_ref[:, LANES * index : LANES * (index + 1)] = part[...]
+    row = lax.broadcasted_iota(jnp.int32, (wide, wide), 0)
+    lane = lax.broadcasted_iota(jnp.int32, (wide, wide), 1)
+    place = lane % LANES
+    part = lane // LANES
+    side = part // heads
+    entry, _ = lane_entry(place)
+    entry = jnp.where(side == 2, jnp.where(place < HD, place, -1), entry)
+    local = HD * (part % heads) + entry
+    skew = mine * (span - LANES)
+    pick = (entry >= 0) & (row == side * (2 * LANES) + skew + local)
+    pick_ref[...] = pick.astype(jnp.float32).astype(jnp.bfloat16)
+    spread_ref[...] = dot_nn(window_ref[...], pick_ref[...]).astype(jnp.bfloat16)
+    columns = order_ref.shape[1]
+    row = lax.broadcasted_iota(jnp.int32, (wide, columns), 0)
+    lane = lax.broadcasted_iota(jnp.int32, (wide, columns), 1)
+    place = row % LANES
+    part = row // LANES
+    side = part // heads
+    entry, _ = lane_entry(place)
+    entry = jnp.where(side == 2, jnp.where(place < HD, place, -1), entry)
+    pick = (entry >= 0) & (lane == side * span + HD * (part % heads) + entry)
+    order_ref[...] = pick.astype(jnp.float32).astype(jnp.bfloat16)
+    tokens = turn_ref.shape[1]
+    token = lax.broadcasted_iota(jnp.int32, (tokens, LANES), 0)
+    entry, column = lane_entry(lax.broadcasted_iota(jnp.int32, (tokens, LANES), 1))
+    rate = jnp.exp((entry % QUARTER).astype(jnp.float32) * (-math.log(10000.0) / QUARTER))
+    rate = jnp.where(entry >= 0, rate, 0.0)
+    offset = jnp.where(column, token % tile_cols, token // tile_cols).astype(jnp.float32) * rate
+    turn_ref[0] = jnp.cos(offset)
+    turn_ref[1] = jnp.sin(offset)
+    turn_ref[2] = rate
+    gain_ref[...] = jnp.zeros_like(gain_ref)
+    wide_row(qgain_ref[...].reshape(1, HD), gain_ref, 0)
+    wide_row(kgain_ref[...].reshape(1, HD), gain_ref, 1)
+    units = gate_ref.shape[1]
+    run = units // 2
+    for parity in range(2):
+
+        @pl.when(mine % 2 == parity)
+        def _(parity=parity):
+            for source_a, source_b, target in ((gate_a, gate_b, gate_ref), (up_a, up_b, up_ref)):
+                target[:, 0:run] = source_a[:, run * parity : run * (parity + 1)]
+                target[:, run:units] = source_b[:, run * parity : run * (parity + 1)]
+
+
+def unit_rate(raw):
+    return lax.rsqrt(jnp.sum(raw * raw, axis=-1, keepdims=True) * (1.0 / HD) + EPS)
+
+
+def block_copies(pieces, ref, place, tokens, sems):
+    if len(pieces) == 8:
+        plan = [(piece, index, tokens, 0) for index, piece in enumerate(pieces)]
+    else:
+        own, xn, core, cx, yn, d1, d2, cy, cd1, cd2 = pieces
+        half = d1.shape[0]
+        plan = [
+            (own, 0, tokens, 0), (xn, 1, tokens, 0), (core, 2, tokens, 0), (cx, 3, tokens, 0),
+            (yn, 4, tokens, 0), (d1, 5, half, 0), (d2, 5, tokens - half, half), (cy, 6, tokens, 0),
+            (cd1, 7, half, 0), (cd2, 7, tokens - half, half),
+        ]
+    return [
+        pltpu.make_async_copy(
+            piece.at[pl.ds(0, rows), :],
+            ref.at[pl.ds(place(index) + offset, rows), :],
+            sems.at[number],
+        )
+        for number, (piece, index, rows, offset) in enumerate(plan)
+    ]
+
+
+def attend_kernel(blocks, scalars, *refs):
+    pieces, refs = refs[:10], refs[10:]
+    (
+        spread_ref, offset_ref, gain_ref,
+        att_ref, hid_ref, qkv_ref, raw_ref, turn_ref, mod_ref, log_ref, mixed_ref,
+        all_ref, extra_ref, rows_ref, flat_ref, anchor_ref, vt_ref, sems, extra_sems,
+    ) = refs
+    mine = scalars[0]
+    own, xn, core, cx, yn, d1, d2, cy, cd1, cd2 = pieces
+    width = own.shape[1]
+    tokens = own.shape[0] - EXTRA
+    columns = 6 * width // blocks
+    half = d1.shape[0]
+    everyone = blocks * tokens
+    heads = HEADS // blocks
+    extras = [
+        pltpu.make_async_copy(
+            piece.at[pl.ds(piece.shape[0] - EXTRA, EXTRA), :],
+            extra_ref.at[index],
+            extra_sems.at[index],
+        )
+        for index, piece in enumerate((own, xn, core, cx, yn, d2, cy, cd2))
+    ]
+    copies = block_copies(
+        pieces,
+        all_ref,
+        lambda index: pl.multiple_of((mine ^ index) * tokens, tokens),
+        tokens,
+        sems,
+    )
+    for copy in (*extras, *copies):
+        copy.start()
+    for copy in extras:
+        copy.wait()
+    for index in range(blocks):
+        extra = extra_ref[index].astype(jnp.float32)
+        place = mine ^ index
+        rows_ref[pl.ds(place, 1), :] = extra[0:1] + extra[1:2] + extra[2:3]
+        anchor_ref[0, pl.ds(place, 1), :] = extra[3:4, 0:LANES]
+    for index in range(blocks):
+        flat_ref[0:1, columns * index : columns * (index + 1)] = rows_ref[
+            index : index + 1, 0:columns
+        ]
+    mod_ref[...] = jnp.zeros_like(mod_ref)
+    for index in range(6):
+        mod_ref[index : index + 1, :] = flat_ref[0:1, width * index : width * (index + 1)]
+    shift_in = mod_ref[0:1, :]
+    scale_in = 1.0 + mod_ref[1:2, :]
+    anchor = anchor_ref[0] * offset_ref[2, 0:blocks, :]
+    anchor_ref[0] = jnp.cos(anchor)
+    anchor_ref[1] = jnp.sin(anchor)
+    lane = lax.broadcasted_iota(jnp.int32, (tokens, LANES), 1)
+    sign = jnp.where(lane < LANES // 2, -1.0, 1.0)
+    offset_cos, offset_sin = offset_ref[0], offset_ref[1]
+    query_gain, key_gain = gain_ref[0:1, :], gain_ref[1:2, :]
+    scale = HD ** (-0.5) * math.log2(math.e)
+    for copy in copies:
+        copy.wait()
+
+    def project(index, carry):
+        rows = pl.ds(pl.multiple_of(index * tokens, tokens), tokens)
+        hidden = (all_ref[rows, :].astype(jnp.float32) * scale_in + shift_in).astype(jnp.bfloat16)
+        hid_ref[rows, :] = hidden
+        anchor_cos = anchor_ref[0, pl.ds(index, 1), :]
+        anchor_sin = anchor_ref[1, pl.ds(index, 1), :]
+        turn_cos = anchor_cos * offset_cos - anchor_sin * offset_sin
+        turn_sin = (anchor_sin * offset_cos + anchor_cos * offset_sin) * sign
+        turn_ref[0, rows, :] = turn_cos
+        turn_ref[1, rows, :] = turn_sin
+        product = dot_nn(hidden, spread_ref[...])
+        for part in range(2 * heads):
+            raw = product[:, LANES * part : LANES * (part + 1)]
+            raw_ref[part, rows, :] = raw
+            gain = query_gain * scale if part < heads else key_gain
+            unit = raw * unit_rate(raw) * gain
+            turned = unit * turn_cos + pltpu.roll(unit, LANES // 2, 1) * turn_sin
+            qkv_ref[part, rows, :] = turned.astype(jnp.bfloat16)
+        for part in range(2 * heads, 3 * heads):
+            qkv_ref[part, rows, :] = product[:, LANES * part : LANES * (part + 1)].astype(
+                jnp.bfloat16
+            )
+        return carry
+
+    lax.fori_loop(0, blocks, project, 0, unroll=2)
+    chunk = 2 * tokens
+    for head in range(heads):
+        vt_ref[head] = qkv_ref[2 * heads + head].T
+
+    def attend(index, carry):
+        rows = pl.ds(pl.multiple_of(index * chunk, chunk), chunk)
+        for head in range(heads):
+            scores = dot_nt(qkv_ref[heads + head], qkv_ref[head, rows, :])
+            expo = jnp.exp2(scores)
+            total = column_sum(expo)
+            mixed = dot_nn(vt_ref[head], expo.astype(jnp.bfloat16)) * (1.0 / total)
+            mixed = mixed.T
+            log_ref[head, pl.ds(index, 1), :] = jnp.log2(total)
+            mixed_ref[head, rows, :] = mixed
+            att_ref[rows, LANES * head : LANES * (head + 1)] = mixed.astype(jnp.bfloat16)
+        return carry
+
+    lax.fori_loop(0, everyone // chunk, attend, 0)
+
+
+def middle_kernel(att_ref, weight_ref, x_ref, mod_ref, out_ref, mid_ref, hid_ref):
+    blocks = att_ref.shape[0]
+    heads = HEADS // blocks
+    attended = jnp.concatenate(
+        [
+            att_ref[index, :, LANES * head : LANES * head + HD]
+            for index in range(blocks)
+            for head in range(heads)
+        ],
+        axis=1,
+    )
+    attn_out = dot_nn(attended, weight_ref[...])
+    out_ref[...] = attn_out
+    middle = x_ref[...] + mod_ref[2:3, :] * attn_out
+    mid_ref[...] = middle
+    hid_ref[...] = (normed(middle) * (1.0 + mod_ref[4:5, :]) + mod_ref[3:4, :]).astype(
+        jnp.bfloat16
+    )
+
+
+def act_grad_kernel(down_ref, cot_ref, mod_ref, out_ref, low_ref):
+    @pl.when(pl.program_id(0) == 0)
+    def _():
+        low_ref[...] = (mod_ref[5:6, :] * cot_ref[...]).astype(jnp.bfloat16)
+
+    out_ref[...] = dot_nt(low_ref[...], down_ref[...])
+
+
+def mlp_kernel(
+    gate_ref, up_ref, outw_ref, hid_ref, mid_ref, attn_ref, cot_ref, agrad_in, mod_ref,
+    act_ref, mgrad_ref, agrad_ref, dgrad_ref, sums_ref, back_ref,
+):
+    step = pl.program_id(0)
+    blocks = dgrad_ref.shape[0]
+    heads = HEADS // blocks
+
+    hidden = hid_ref[...]
+    gate = dot_nn(hidden, gate_ref[...])
+    up = dot_nn(hidden, up_ref[...])
+    sigma = sigmoid(gate)
+    silu = gate * sigma
+    act_ref[...] = (silu * up).astype(jnp.bfloat16)
+    act_grad = agrad_in[...]
+    slope = sigma * (1.0 + gate * (1.0 - sigma))
+    gate_grad = (act_grad * up * slope).astype(jnp.bfloat16)
+    up_grad = (act_grad * silu).astype(jnp.bfloat16)
+    part = dot_nt(gate_grad, gate_ref[...]) + dot_nt(up_grad, up_ref[...])
+
+    @pl.when(step == 0)
+    def _():
+        back_ref[...] = part
+
+    @pl.when(step > 0)
+    def _():
+        back_ref[...] += part
+
+    @pl.when(step == pl.num_programs(0) - 1)
+    def _():
+        middle = mid_ref[...]
+        upstream = cot_ref[...]
+        back = back_ref[...]
+        inverse = lax.rsqrt(jnp.mean(middle * middle, axis=-1, keepdims=True) + EPS)
+        unit = middle * inverse
+        lifted = back * (1.0 + mod_ref[4:5, :])
+        middle_grad = upstream + inverse * (
+            lifted - unit * jnp.mean(lifted * unit, axis=-1, keepdims=True)
+        )
+        mgrad_ref[...] = middle_grad
+        attn_grad = (mod_ref[2:3, :] * middle_grad).astype(jnp.bfloat16)
+        agrad_ref[...] = attn_grad
+        dgrad_ref[...] = jnp.zeros_like(dgrad_ref)
+        for index in range(blocks):
+            rows = outw_ref[HD * heads * index : HD * heads * (index + 1), :]
+            piece = dot_nt(attn_grad, rows).astype(jnp.bfloat16)
+            for head in range(heads):
+                dgrad_ref[index, :, LANES * head : LANES * head + HD] = piece[
+                    :, HD * head : HD * (head + 1)
+                ]
+        sums_ref[...] = jnp.zeros_like(sums_ref)
+        sums_ref[2:3, :] = column_sum(middle_grad * attn_ref[...])
+        sums_ref[3:4, :] = column_sum(back)
+        sums_ref[4:5, :] = column_sum(back * unit)
+
+
+def mlp_out_kernel(act_ref, down_ref, mid_ref, cot_ref, mod_ref, output_ref, sum_ref, acc_ref):
+    step = pl.program_id(0)
+    part = dot_nn(act_ref[...], down_ref[...])
+
+    @pl.when(step == 0)
+    def _():
+        acc_ref[...] = part
+
+    @pl.when(step > 0)
+    def _():
+        acc_ref[...] += part
+
+    @pl.when(step == pl.num_programs(0) - 1)
+    def _():
+        output_ref[...] = mid_ref[...] + mod_ref[5:6, :] * acc_ref[...]
+        sum_ref[...] = jnp.broadcast_to(column_sum(cot_ref[...] * acc_ref[...]), sum_ref.shape)
+
+
+def mlp_weights_kernel(scalars, *refs):
+    hid_pieces, cot_pieces, refs = refs[:8], refs[8:16], refs[16:]
+    (
+        gate_ref, up_ref, down_a, down_b, mod_ref, own_ref, next_ref, two_ref, last_ref, far_ref,
+        all_ref, low_ref, act_ref, down_ref, out_ref, sems, out_sems,
+    ) = refs
+    tokens, width = hid_pieces[0].shape
+    everyone = all_ref.shape[0]
+    run = down_a.shape[0]
+    units = 2 * run
+    copies = [
+        *block_copies(hid_pieces, all_ref, lambda index: index * tokens, tokens, sems.at[0]),
+        *block_copies(cot_pieces, low_ref, lambda index: index * tokens, tokens, sems.at[1]),
+    ]
+    for copy in copies:
+        copy.start()
+    down_ref[0:run, :] = down_a[...]
+    down_ref[run:units, :] = down_b[...]
+    gate_mid = mod_ref[5:6, :]
+    for copy in copies:
+        copy.wait()
+    chunk = everyone // 4
+
+    def chunked(index, carry):
+        span = pl.ds(pl.multiple_of(index * chunk, chunk), chunk)
+        low = (low_ref[span, :].astype(jnp.float32) * gate_mid).astype(jnp.bfloat16)
+        low_ref[span, :] = low
+        hidden = all_ref[span, :]
+        gate = dot_nn(hidden, gate_ref[...])
+        up = dot_nn(hidden, up_ref[...])
+        act_grad = dot_nt(low, down_ref[...])
+        sigma = sigmoid(gate)
+        silu = gate * sigma
+        slope = sigma * (1.0 + gate * (1.0 - sigma))
+        act_ref[0, span, :] = (silu * up).astype(jnp.bfloat16)
+        act_ref[1, span, :] = (act_grad * up * slope).astype(jnp.bfloat16)
+        act_ref[2, span, :] = (act_grad * silu).astype(jnp.bfloat16)
+        return carry
+
+    lax.fori_loop(0, everyone // chunk, chunked, 0, unroll=2)
+    lanes = width // units
+    for side in range(2):
+        grad = dot_tn(act_ref[1 + side], all_ref[...]).astype(jnp.bfloat16)
+        for part in range(2):
+            for index in range(lanes):
+                out_ref[2 * side + part, run * index : run * (index + 1), :] = grad[
+                    run * part : run * (part + 1), units * index : units * (index + 1)
+                ]
+    down = dot_tn(act_ref[0], low_ref[...]).astype(jnp.bfloat16).T
+    share = width // out_ref.shape[0]
+    for image in range(out_ref.shape[0]):
+        out_ref[image, run * lanes : run * lanes + share, :] = down[
+            share * image : share * (image + 1), :
+        ]
+    deal(out_ref, scalars[1], (own_ref, next_ref, two_ref, last_ref, far_ref), out_sems)
+
+
+def deal(ref, place, targets, sems):
+    owners = [place, (place + 1) % 4, (place + 2) % 4, (place + 3) % 4, 3 - place]
+    copies = [
+        pltpu.make_async_copy(ref.at[owner], target, sems.at[index])
+        for index, (owner, target) in enumerate(zip(owners, targets, strict=False))
+    ]
+    for copy in copies:
+        copy.start()
+    for copy in copies:
+        copy.wait()
+
+
+def summed(refs, rows):
+    total = refs[0][rows, :].astype(jnp.float32)
+    for ref in refs[1:]:
+        total = total + ref[rows, :].astype(jnp.float32)
+    return total
+
+
+def turn_kernel(scalars, *refs):
+    parts, refs = refs[:3], refs[3:]
+    send_ref, first_ref, second_ref = refs
+    blocks, rows, run = send_ref.shape
+    units = parts[0].shape[1]
+    lanes = rows * blocks // units
+    whole = jnp.concatenate(
+        [summed(parts, pl.ds(run * index, run)).T for index in range(lanes)], axis=0
+    )
+    send_ref[...] = whole.astype(jnp.bfloat16).reshape(send_ref.shape)
+    down = summed(parts, pl.ds(run * lanes, first_ref.shape[0])).astype(jnp.bfloat16)
+    even = scalars[0] % 2 == 0
+    for parity in range(2):
+
+        @pl.when(scalars[0] % 2 == parity)
+        def _(parity=parity):
+            first_ref[...] = down[:, run * parity : run * (parity + 1)]
+            second_ref[...] = down[:, run * (1 - parity) : run * (2 - parity)]
+
+
+def lay_kernel(scalars, got_ref, first_ref, second_ref, out_ref, down_ref):
+    out_ref[...] = jnp.concatenate(
+        [got_ref[index].astype(jnp.float32) for index in range(got_ref.shape[0])], axis=1
+    )
+    run = first_ref.shape[1]
+    first = first_ref[...].astype(jnp.float32)
+    second = second_ref[...].astype(jnp.float32)
+    half = got_ref.shape[0] // 2
+
+    @pl.when(scalars[0] < half)
+    def _():
+        down_ref[...] = jnp.concatenate([first, second], axis=1)
+
+    @pl.when(scalars[0] >= half)
+    def _():
+        down_ref[...] = jnp.concatenate([second, first], axis=1)
+
+
+def finish_kernel(*refs):
+    parts, (qkv_ref, out_ref) = refs[:3], refs[3:]
+    total = summed(parts, pl.ds(0, qkv_ref.shape[0]))
+    columns = qkv_ref.shape[1]
+    qkv_ref[...] = total[:, 0:columns]
+    out_ref[...] = total[:, columns:]
+
+
+def dot_exact(left, right, dims):
+    total = None
+    for _ in range(3):
+        part = left.astype(jnp.bfloat16)
+        left = left - part.astype(jnp.float32)
+        product = lax.dot_general(
+            part, right, (dims, ((), ())), preferred_element_type=jnp.float32
+        )
+        total = product if total is None else total + product
+    return total
+
+
+def tail_kernel(
+    got_ref, table_ref, weight_ref,
+    modw_ref, modb_ref, qgain_ref, kgain_ref, send_ref, cond_ref, bucket_ref,
+    cols_ref, act_ref,
+):
+    columns = modb_ref.shape[0]
+    blocks = send_ref.shape[0]
+    images = got_ref.shape[0] // blocks
+    lines = table_ref.shape[0]
+    cols_ref[...] = jnp.zeros_like(cols_ref)
+    act_ref[...] = jnp.zeros_like(act_ref)
+    bucket_ref[...] = jnp.full(bucket_ref.shape, -1.0, jnp.float32)
+    cond_ref[...] = jnp.zeros_like(cond_ref)
+    gains = None
+    line = lax.broadcasted_iota(jnp.int32, (lines, 1), 0).astype(jnp.float32)
+    for image in range(images):
+        total = got_ref[blocks * image]
+        for index in range(1, blocks):
+            total = total + got_ref[blocks * image + index]
+        row = jnp.concatenate([total[index : index + 1, :] for index in range(8)], axis=1)
+        cols_ref[image : image + 1, :] = row[:, 0:columns]
+        gains = row if gains is None else gains + row
+        first = got_ref[blocks * image]
+        place = columns // LANES
+        bucket = first[place : place + 1, columns % LANES : columns % LANES + 1]
+        bucket_ref[image : image + 1, :] = jnp.broadcast_to(bucket, (1, LANES))
+        cond = jnp.sum(
+            jnp.where(line == bucket, table_ref[...], 0.0), axis=0, keepdims=True
+        )
+        cond_ref[image : image + 1, :] = cond
+        act_ref[image : image + 1, :] = (
+            (cond * sigmoid(cond)).astype(jnp.bfloat16).astype(jnp.float32)
+        )
+    cols = cols_ref[...]
+    modw_ref[...] = lax.dot_general(
+        act_ref[...], cols, (((0,), (0,)), ((), ())),
+        precision=PRECISE, preferred_element_type=jnp.float32,
+    )
+    modb_ref[...] = column_sum(cols).reshape(columns)
+    start = columns + 16
+    qgain_ref[...] = gains[:, start : start + HD].reshape(HD)
+    kgain_ref[...] = gains[:, start + HD : start + 2 * HD].reshape(HD)
+    part = dot_exact(cols, weight_ref[...], ((1,), (0,)))
+    send_ref[...] = jnp.broadcast_to(part[None], send_ref.shape)
+
+
+def table_kernel(scalars, got_ref, cond_ref, bucket_ref, out_ref):
+    total = jnp.sum(got_ref[...], axis=0)
+    cond = cond_ref[...]
+    sigma = sigmoid(cond)
+    grad = total * (sigma * (1.0 + cond * (1.0 - sigma)))
+    lines = out_ref.shape[0]
+    line = lax.broadcasted_iota(jnp.int32, (lines, 1), 0) + scalars[0] * lines
+    out = jnp.zeros(out_ref.shape, jnp.float32)
+    for image in range(4):
+        hot = line.astype(jnp.float32) == bucket_ref[image : image + 1, 0:1]
+        out = out + jnp.where(hot, grad[image : image + 1, :], 0.0)
+    out_ref[...] = out
+
+
+def attend_back_kernel(
+    attg_ref, qkv_ref, raw_ref, turn_ref, log_ref, mixed_ref, gain_ref, order_ref,
+    back_ref, gsum_ref, kt_ref, grad_ref,
+):
+    heads = attg_ref.shape[1] // LANES
+    everyone = attg_ref.shape[0]
+    lines, chunk = log_ref.shape[1:]
+    scale = HD ** (-0.5)
+    query_gain, key_gain = gain_ref[0:1, :], gain_ref[1:2, :]
+    for head in range(heads):
+        kt_ref[head] = qkv_ref[heads + head].T
+    ones = jnp.ones((8, LANES), jnp.bfloat16)
+
+    def attend(index, first):
+        rows = pl.ds(pl.multiple_of(index * chunk, chunk), chunk)
+        for head in range(heads):
+            query = qkv_ref[head, rows, :]
+            upstream = attg_ref[rows, LANES * head : LANES * (head + 1)]
+            weighted = upstream.astype(jnp.float32) * mixed_ref[head, rows, :]
+            high = weighted.astype(jnp.bfloat16)
+            low = (weighted - high.astype(jnp.float32)).astype(jnp.bfloat16)
+            delta = (dot_nt(ones, high) + dot_nt(ones, low))[0:1, :]
+            probs = jnp.exp2(
+                dot_nt(qkv_ref[heads + head], query) - log_ref[head, pl.ds(index, 1), :]
+            )
+            score_grad = (probs * (dot_nt(qkv_ref[2 * heads + head], upstream) - delta)).astype(
+                jnp.bfloat16
+            )
+            value_part = dot_nn(probs.astype(jnp.bfloat16), upstream)
+            key_part = dot_nn(score_grad, query)
+            if first:
+                grad_ref[2 * heads + head] = value_part
+                grad_ref[heads + head] = key_part
+            else:
+                grad_ref[2 * heads + head] += value_part
+                grad_ref[heads + head] += key_part
+            grad_ref[head, rows, :] = dot_nn(kt_ref[head], score_grad).T
+
+    attend(0, True)
+
+    def later(index, carry):
+        attend(index, False)
+        return carry
+
+    lax.fori_loop(1, lines, later, 0)
+    gsum_ref[...] = jnp.zeros_like(gsum_ref)
+    step = 2 * LANES
+
+    def finish(index, carry):
+        rows = pl.ds(pl.multiple_of(index * step, step), step)
+        turn_cos = turn_ref[0, rows, :]
+        turn_sin = turn_ref[1, rows, :]
+        parts = []
+        for part in range(2 * heads):
+            gain = query_gain if part < heads else key_gain
+            grad = grad_ref[part, rows, :] * (scale if part < heads else math.log(2.0))
+            turned = grad * turn_cos - pltpu.roll(grad, LANES // 2, 1) * turn_sin
+            raw = raw_ref[part, rows, :]
+            rate = unit_rate(raw)
+            unit = raw * rate
+            line = 0 if part < heads else 1
+            product = turned * unit
+            gsum_ref[line : line + 1, :] += column_sum(product)
+            lifted = turned * gain
+            mean = jnp.sum(product * gain, axis=-1, keepdims=True) * (1.0 / HD)
+            parts.append((rate * (lifted - unit * mean)).astype(jnp.bfloat16))
+        for part in range(2 * heads, 3 * heads):
+            parts.append(grad_ref[part, rows, :].astype(jnp.bfloat16))
+        back_ref[rows, :] = dot_nn(jnp.concatenate(parts, axis=1), order_ref[...]).astype(
+            jnp.bfloat16
+        )
+        return carry
+
+    lax.fori_loop(0, everyone // step, finish, 0)
+
+
+def qkv_weights_kernel(hid_ref, back_ref, grad_ref):
+    grad = dot_tn(hid_ref[...], back_ref[...]).astype(jnp.bfloat16)
+    grad_ref[...] = grad.reshape(grad_ref.shape)
+
+
+def out_weights_kernel(images, scalars, *refs):
+    pieces, refs = refs[:8], refs[8:]
+    att_ref, ograd_ref, low_ref, sems = refs
+    tokens, width = pieces[0].shape
+    mine = scalars[0]
+    heads = att_ref.shape[1] // LANES
+    copies = block_copies(
+        pieces,
+        low_ref,
+        lambda index: pl.multiple_of((mine ^ index) * tokens, tokens),
+        tokens,
+        sems,
+    )
+    for copy in copies:
+        copy.start()
+    for copy in copies:
+        copy.wait()
+    outw = dot_tn(att_ref[...], low_ref[...]).astype(jnp.bfloat16)
+    share = width // images
+    for image in range(images):
+        for head in range(heads):
+            ograd_ref[image, HD * head : HD * (head + 1), :] = outw[
+                LANES * head : LANES * head + HD, share * image : share * (image + 1)
+            ]
+
+
+def join_kernel(scalars, grad_ref, ograd_ref, *refs):
+    targets, (out_ref, sems) = refs[:5], refs[5:]
+    images = out_ref.shape[0]
+    blocks = grad_ref.shape[0]
+    span = HD * HEADS // blocks
+    whole = jnp.concatenate(
+        [
+            grad_ref[index][:, span * side : span * (side + 1)]
+            for side in range(3)
+            for index in range(blocks)
+        ],
+        axis=1,
+    )
+    share = whole.shape[1] // images
+    for image in range(images):
+        out_ref[image] = jnp.concatenate(
+            [whole[:, share * image : share * (image + 1)], ograd_ref[image]], axis=1
+        )
+    deal(out_ref, scalars[1], targets, sems)
+
+
+def input_kernel(
+    back_ref, weight_ref, x_ref, mgrad_ref, mod_ref, sums_ref, gmid_ref, gsum_ref, bucket_ref,
+    grad_ref, send_ref, acc_ref, flat_ref, row_ref,
+):
+    step = pl.program_id(0)
+    blocks = back_ref.shape[0]
+    span = HD * HEADS // blocks
+    width = x_ref.shape[1]
+    columns = 6 * width // blocks
+
+    for side in range(3):
+
+        @pl.when(step == side)
+        def _(side=side):
+            natural = jnp.concatenate(
+                [back_ref[index, :, span * side : span * (side + 1)] for index in range(blocks)],
+                axis=1,
+            )
+            part = dot_nt(natural, weight_ref[...])
+            acc_ref[...] = part if side == 0 else acc_ref[...] + part
+
+    @pl.when(step == 2)
+    def _():
+        x = x_ref[...]
+        back = acc_ref[...]
+        inverse = lax.rsqrt(jnp.mean(x * x, axis=-1, keepdims=True) + EPS)
+        unit = x * inverse
+        lifted = back * (1.0 + mod_ref[1:2, :])
+        grad_ref[...] = mgrad_ref[...] + inverse * (
+            lifted - unit * jnp.mean(lifted * unit, axis=-1, keepdims=True)
+        )
+        flat_ref[0:1, 0:width] = column_sum(back)
+        flat_ref[0:1, width : 2 * width] = column_sum(back * unit)
+        for index in range(2, 5):
+            flat_ref[0:1, width * index : width * (index + 1)] = sums_ref[index : index + 1, :]
+        flat_ref[0:1, width * 5 : width * 6] = gmid_ref[0:1, :]
+        row_ref[...] = jnp.zeros_like(row_ref)
+        for index in range(blocks):
+            row_ref[index : index + 1, 0:columns] = flat_ref[
+                0:1, columns * index : columns * (index + 1)
+            ]
+        row_ref[:, columns : columns + 1] = jnp.broadcast_to(
+            bucket_ref[0].astype(jnp.float32), (blocks, 1)
+        )
+        for line in range(2):
+            for source, target in PLACES:
+                start = columns + 16 + HD * line + source
+                row_ref[:, start : start + QUARTER] = jnp.broadcast_to(
+                    gsum_ref[line : line + 1, target : target + QUARTER], (blocks, QUARTER)
+                )
+        for index in range(blocks):
+            tile = jnp.concatenate(
+                [
+                    row_ref[index : index + 1, LANES * part : LANES * (part + 1)]
+                    for part in range(8)
+                ],
+                axis=0,
+            )
+            for image in range(send_ref.shape[0] // blocks):
+                send_ref[blocks * image + index] = tile
+
+
+def whole_spec(shape):
+    return pl.BlockSpec(tuple(shape), lambda *_, n=len(shape): (0,) * n)
+
+
+ANY = pl.BlockSpec(memory_space=pl.ANY)
+SMEM = pl.BlockSpec(memory_space=pltpu.SMEM)
+
+
+def call(
+    kernel, operands, outs, scratch=(), scalars=None, name=None, micros=5, specs=None, grid=(1,),
+    out_specs=None,
+):
+    return pl.pallas_call(
+        kernel,
+        out_shape=outs,
+        grid_spec=pltpu.PrefetchScalarGridSpec(
+            num_scalar_prefetch=0 if scalars is None else 1,
+            grid=grid,
+            in_specs=[
+                (specs or {}).get(index) or whole_spec(a.shape) for index, a in enumerate(operands)
+            ],
+            out_specs=[
+                (out_specs or {}).get(index) or whole_spec(o.shape) for index, o in enumerate(outs)
+            ],
+            scratch_shapes=list(scratch),
+        ),
+        cost_estimate=pl.CostEstimate(
+            flops=int(micros * 1e9), transcendentals=0, bytes_accessed=int(micros * 1e6)
+        ),
+        name=name,
+    )(*(() if scalars is None else (scalars,)), *operands)
+
+
+def struct(shape, dtype=jnp.float32):
+    return jax.ShapeDtypeStruct(shape, dtype)
+
+
+PLANE = ("ty", "tx")
+
+
+def swap(value, bit):
+    return lax.ppermute(value, PLANE, [(index, index ^ bit) for index in range(8)])
+
+
+def first_round(value):
+    return swap(value, 2), swap(value, 1), swap(value, 4)
+
+
+def split_round(xn, yn, half):
+    d1 = swap(xn[:half], 4)
+    cx = swap(xn, 2)
+    d2 = swap(yn[half:], 1)
+    return d1, d2, cx, swap(yn, 2)
+
+
+def second_round(xn, yn):
+    return swap(xn, 4), swap(xn, 2), swap(yn, 2)
+
+
+def tie(*values):
+    return lax.optimization_barrier(values)
+
+
+def exchange(value, axes=PLANE):
+    return lax.all_to_all(value, axes, split_axis=0, concat_axis=0, tiled=True)
+
+
+def shift(value, pairs):
+    return lax.ppermute(value, "img", pairs)
+
+
+def onward(value, step):
+    return shift(value, [(i, (i + step) % 4) for i in range(4)])
+
+
+def add(left, right):
+    return (left.astype(jnp.float32) + right.astype(jnp.float32)).astype(jnp.bfloat16)
+
+
+def line_first(shares):
+    return shift(shares[4], [(0, 1), (3, 2)])
+
+
+def line_second(shares, first):
+    value = add(shares[2], first)
+    return shift(value, [(0, 1), (1, 2)]), shift(value, [(3, 2), (2, 1)])
+
+
+def line_third(shares, up, down):
+    return (
+        shift(add(shares[1], up), [(0, 1), (1, 2), (2, 3)]),
+        shift(add(shares[3], down), [(3, 2), (2, 1), (1, 0)]),
+    )
+
+
+def on_plane(
+    images,
+    block_in,
+    bucket,
+    tile_anchor,
+    cond_table,
+    mod_weight,
+    mod_bias,
+    qkv_weight,
+    query_gain,
+    key_gain,
+    out_weight,
+    gate_up_weight,
+    down_weight,
+    cotangent,
+):
+    blocks = 8
+    _, tile_rows, tile_cols, width = block_in.shape
+    tokens = tile_rows * tile_cols
+    everyone = blocks * tokens
+    hidden_units = down_weight.shape[0]
+    units = hidden_units // blocks
+    run = units // 2
+    lanes = width // units
+    heads = HEADS // blocks
+    span = heads * HD
+    columns = mod_weight.shape[1]
+    wide = 3 * heads * LANES
+    packed = -(-3 * span // LANES) * LANES
+    bf16 = jnp.bfloat16
+    image = lax.axis_index("img")
+    mine = lax.axis_index("ty") * 2 + lax.axis_index("tx")
+    where = jnp.stack([mine, image]).astype(jnp.int32)
+    share = width // images
+    x = block_in.reshape(tokens, width)
+    cot = cotangent.reshape(tokens, width)
+    half = tokens // 2
+    pay, low_cot = call(
+        open_kernel,
+        (bucket, tile_anchor.reshape(2), x, cond_table, mod_weight.T, mod_bias, cot),
+        (struct((tokens + EXTRA, width), bf16), struct((tokens, width), bf16)),
+        [pltpu.VMEM((8, width), jnp.float32)],
+        name="open",
+        specs={0: SMEM, 1: SMEM},
+    )
+    core, xn, yn = first_round(pay)
+    spread, order, offsets, gains, own_gate, own_up, table_share, modw_share = call(
+        functools.partial(ready_kernel, blocks, tile_cols),
+        (*[qkv_weight] * 6, *[gate_up_weight] * 4, query_gain, key_gain, cond_table, mod_weight.T),
+        (
+            struct((width, wide), bf16),
+            struct((wide, packed), bf16),
+            struct((3, tokens, LANES)),
+            struct((8, LANES)),
+            struct((width, units), bf16),
+            struct((width, units), bf16),
+            struct((cond_table.shape[0], share)),
+            struct((columns, share), bf16),
+        ),
+        [pltpu.VMEM((width, wide), bf16), pltpu.VMEM((wide, wide), bf16)],
+        where,
+        "ready",
+        specs={
+            **{
+                2 * side + n: pl.BlockSpec(
+                    (width, LANES), lambda i, s, c=side * width // LANES + n: (0, c + s[0])
+                )
+                for side in range(3)
+                for n in range(2)
+            },
+            **{
+                6 + n: pl.BlockSpec((width, units), lambda i, s, n=n: (0, n * 4 + s[0] // 2))
+                for n in range(4)
+            },
+        },
+    )
+    xn, yn, spread, order, offsets, gains, own_gate, own_up = tie(
+        xn, yn, spread, order, offsets, gains, own_gate, own_up
+    )
+    d1, d2, cx, cy = split_round(xn, yn, half)
+    pieces = (pay, xn, core, cx, yn, d1, d2, cy, swap(d1, 2), swap(d2, 2))
+    c_core, c_xn, c_yn = first_round(low_cot)
+    att, hid, qkv, raw, turn, mod, logs, mixed = call(
+        functools.partial(attend_kernel, blocks),
+        (*pieces, spread, offsets, gains),
+        (
+            struct((everyone, LANES * heads), bf16),
+            struct((everyone, width), bf16),
+            struct((3 * heads, everyone, LANES), bf16),
+            struct((2 * heads, everyone, LANES)),
+            struct((2, everyone, LANES)),
+            struct((8, width)),
+            struct((heads, everyone // (2 * tokens), 2 * tokens)),
+            struct((heads, everyone, LANES)),
+        ),
+        [
+            pltpu.VMEM((everyone, width), bf16),
+            pltpu.VMEM((blocks, EXTRA, width), bf16),
+            pltpu.VMEM((8, width), jnp.float32),
+            pltpu.VMEM((1, 6 * width), jnp.float32),
+            pltpu.VMEM((2, 8, LANES), jnp.float32),
+            pltpu.VMEM((heads, LANES, everyone), bf16),
+            pltpu.SemaphoreType.DMA((10,)),
+            pltpu.SemaphoreType.DMA((blocks,)),
+        ],
+        where,
+        "attend",
+        15,
+        {index: ANY for index in range(10)},
+    )
+    att, c_core, c_xn, c_yn = tie(att, c_core, c_xn, c_yn)
+    att_all = exchange(att.reshape(blocks, tokens, LANES * heads))
+    c_dn, c_cx, c_cy = second_round(c_xn, c_yn)
+    mlp_steps = 4
+    step_units = hidden_units // mlp_steps
+    (act_grad,) = call(
+        act_grad_kernel,
+        (down_weight, cot, mod),
+        (struct((tokens, hidden_units)),),
+        [pltpu.VMEM((tokens, width), bf16)],
+        name="act_grad",
+        specs={0: pl.BlockSpec((step_units, width), lambda f: (f, 0))},
+        out_specs={0: pl.BlockSpec((tokens, step_units), lambda f: (0, f))},
+        grid=(mlp_steps,),
+    )
+    att_all, c_dn, c_cx, c_cy, act_grad = tie(att_all, c_dn, c_cx, c_cy, act_grad)
+    cot_pieces = (low_cot, c_xn, c_core, c_cx, c_yn, c_dn, c_cy, swap(c_dn, 2))
+    attn_out, middle, hidden_mid = call(
+        middle_kernel,
+        (att_all, out_weight, x, mod),
+        (struct((tokens, width)), struct((tokens, width)), struct((tokens, width), bf16)),
+        name="middle",
+    )
+    h_core, h_xn, h_yn = first_round(hidden_mid)
+    act, middle_grad, attn_grad, attg, sums = call(
+        mlp_kernel,
+        (gate_up_weight, gate_up_weight, out_weight, hidden_mid, middle, attn_out, cot, act_grad, mod),
+        (
+            struct((tokens, hidden_units), bf16),
+            struct((tokens, width)),
+            struct((tokens, width), bf16),
+            struct((blocks, tokens, LANES * heads), bf16),
+            struct((8, width)),
+        ),
+        [pltpu.VMEM((tokens, width), jnp.float32)],
+        name="mlp",
+        micros=12,
+        specs={
+            0: pl.BlockSpec((width, step_units), lambda f: (0, f)),
+            1: pl.BlockSpec((width, step_units), lambda f: (0, mlp_steps + f)),
+            7: pl.BlockSpec((tokens, step_units), lambda f: (0, f)),
+        },
+        out_specs={0: pl.BlockSpec((tokens, step_units), lambda f: (0, f))},
+        grid=(mlp_steps,),
+    )
+    attg, h_core, h_xn, h_yn = tie(attg, h_core, h_xn, h_yn)
+    attg_all = exchange(attg)
+    h_dn, h_cx, h_cy = second_round(h_xn, h_yn)
+    output, gmid = call(
+        mlp_out_kernel,
+        (act, down_weight, middle, cot, mod),
+        (struct((tokens, width)), struct((8, width))),
+        [pltpu.VMEM((tokens, width), jnp.float32)],
+        name="mlp_out",
+        specs={
+            0: pl.BlockSpec((tokens, step_units), lambda f: (0, f)),
+            1: pl.BlockSpec((step_units, width), lambda f: (f, 0)),
+        },
+        grid=(mlp_steps,),
+    )
+    h_dn, h_cx, h_cy, gmid = tie(h_dn, h_cx, h_cy, gmid)
+    hid_pieces = (hidden_mid, h_xn, h_core, h_cx, h_yn, h_dn, h_cy, swap(h_dn, 2))
+    zrows = run * lanes + width // images
+    a_core, a_xn, a_yn = first_round(attn_grad)
+    shares = call(
+        mlp_weights_kernel,
+        (*hid_pieces, *cot_pieces, own_gate, own_up, down_weight, down_weight, mod),
+        (struct((zrows, units), bf16),) * 5,
+        [
+            pltpu.VMEM((everyone, width), bf16),
+            pltpu.VMEM((everyone, width), bf16),
+            pltpu.VMEM((3, everyone, units), bf16),
+            pltpu.VMEM((units, width), bf16),
+            pltpu.VMEM((images, zrows, units), bf16),
+            pltpu.SemaphoreType.DMA((2, blocks)),
+            pltpu.SemaphoreType.DMA((5,)),
+        ],
+        where,
+        "mlp_weights",
+        12,
+        {
+            **{index: ANY for index in range(16)},
+            18: pl.BlockSpec((run, width), lambda i, s: (s[0], 0)),
+            19: pl.BlockSpec((run, width), lambda i, s: (8 + s[0], 0)),
+        },
+        out_specs={index: ANY for index in range(5)},
+    )
+    attg_all, a_core, a_xn, a_yn, *shares = tie(attg_all, a_core, a_xn, a_yn, *shares)
+    way = line_first(shares)
+    a_dn, a_cx, a_cy = second_round(a_xn, a_yn)
+    back, gain_sums = call(
+        attend_back_kernel,
+        (attg_all.reshape(everyone, LANES * heads), qkv, raw, turn, logs, mixed, gains, order),
+        (struct((everyone, packed), bf16), struct((8, LANES))),
+        [
+            pltpu.VMEM((heads, LANES, everyone), bf16),
+            pltpu.VMEM((3 * heads, everyone, LANES), jnp.float32),
+        ],
+        name="attend_back",
+        micros=15,
+    )
+    back, way, a_dn, a_cx, a_cy = tie(back, way, a_dn, a_cx, a_cy)
+    back_all = exchange(back.reshape(blocks, tokens, packed))
+    a_cd = swap(a_dn, 2)
+    own_back, a_cd, way = tie(back, a_cd, way)
+    up, down = line_second(shares, way)
+    grad_pieces = (attn_grad, a_xn, a_core, a_cx, a_yn, a_dn, a_cy, a_cd)
+    (qkv_part,) = call(
+        qkv_weights_kernel,
+        (hid, own_back),
+        (struct((blocks, width // blocks, packed), bf16),),
+        name="qkv_weights",
+    )
+    qkv_part, att = tie(qkv_part, att)
+    qkv_rows = exchange(qkv_part)
+    (outw_part,) = call(
+        functools.partial(out_weights_kernel, images),
+        (*grad_pieces, att),
+        (struct((images, span, width // images), bf16),),
+        [pltpu.VMEM((everyone, width), bf16), pltpu.SemaphoreType.DMA((blocks,))],
+        where,
+        "out_weights",
+        specs={index: ANY for index in range(blocks)},
+    )
+    back_all, outw_part, up, down = tie(back_all, outw_part, up, down)
+    up, down = line_third(shares, up, down)
+    in_grad, send = call(
+        input_kernel,
+        (back_all, qkv_weight, x, middle_grad, mod, sums, gmid, gain_sums, bucket),
+        (struct((tokens, width)), struct((images * blocks, 8, LANES))),
+        [
+            pltpu.VMEM((tokens, width), jnp.float32),
+            pltpu.VMEM((1, 6 * width), jnp.float32),
+            pltpu.VMEM((blocks, 1024), jnp.float32),
+        ],
+        name="input",
+        micros=7,
+        specs={1: pl.BlockSpec((width, width), lambda s: (0, s)), 8: SMEM},
+        grid=(3,),
+    )
+    send_gateup, first, second = call(
+        turn_kernel,
+        (shares[0], up, down),
+        (
+            struct((blocks, width // blocks, run), bf16),
+            struct((share, run), bf16),
+            struct((share, run), bf16),
+        ),
+        scalars=where,
+        name="turn",
+    )
+    joined = call(
+        join_kernel,
+        (qkv_rows, outw_part),
+        (struct((width // blocks, 4 * share), bf16),) * 5,
+        [
+            pltpu.VMEM((images, width // blocks, 4 * share), bf16),
+            pltpu.SemaphoreType.DMA((5,)),
+        ],
+        where,
+        "join",
+        out_specs={index: ANY for index in range(5)},
+    )
+    way = line_first(joined)
+    send, joined = tie(send, joined)
+    everywhere = exchange(send, ("img", "ty", "tx"))
+    everywhere, way, send_gateup = tie(everywhere, way, send_gateup)
+    up, down = line_second(joined, way)
+    modw_total, modb_total, qgain_total, kgain_total, act_send, condition, buckets = call(
+        tail_kernel,
+        (everywhere, table_share, modw_share),
+        (
+            struct((share, columns)),
+            struct((columns,)),
+            struct((HD,)),
+            struct((HD,)),
+            struct((blocks, 8, share)),
+            struct((8, share)),
+            struct((8, LANES)),
+        ),
+        [pltpu.VMEM((8, columns), jnp.float32), pltpu.VMEM((8, share), jnp.float32)],
+        name="tail",
+    )
+    act_parts = exchange(act_send)
+    act_parts, up, down = tie(act_parts, up, down)
+    up, down = line_third(joined, up, down)
+    gateup_rows = exchange(send_gateup)
+    first = lax.ppermute(first, PLANE, [(t, t // 2 + 4 * (t % 2)) for t in range(8)])
+    second = lax.ppermute(second, PLANE, [(t, t // 2 + 4 * (1 - t % 2)) for t in range(8)])
+    (table_total,) = call(
+        table_kernel,
+        (act_parts, condition, buckets),
+        (struct((cond_table.shape[0] // blocks, share)),),
+        scalars=where,
+        name="table",
+    )
+    gateup_total, down_total = call(
+        lay_kernel,
+        (gateup_rows, first, second),
+        (struct((width // blocks, blocks * run)), struct((share, units))),
+        scalars=where,
+        name="lay",
+    )
+    qkv_total, outw_total = call(
+        finish_kernel,
+        (joined[0], up, down),
+        (struct((width // blocks, 3 * share)), struct((width // blocks, share))),
+        name="finish",
+    )
+    return (
+        output.reshape(block_in.shape),
+        in_grad.reshape(block_in.shape),
+        table_total,
+        modw_total,
+        modb_total,
+        qkv_total,
+        qgain_total,
+        kgain_total,
+        outw_total,
+        gateup_total,
+        down_total.T,
+    )
+
+
 def solution(mesh):
+    sizes = mesh.shape
+    fits = sizes["ty"] == 4 and sizes["tx"] == 2 and sizes["img"] == 4
     return jax.shard_map(
-        on_device,
+        functools.partial(on_plane, sizes["img"]) if fits else on_device,
         mesh=mesh,
         in_specs=(
             P("img", "ty", "tx", None),

time: 892 us -> 234 us (0.26)
  waiting for transfers between devices: 595 us -> 19.5 us
  Pallas kernels: 0 us -> 124 us
  matrix products: 93.8 us -> 0 us
  blocking collectives: 76.2 us -> 0 us
  starting transfers between devices: 0.92 us -> 74.9 us
  local copies, waits for them, and re-layouts: 70.3 us -> 9.15 us
  other arithmetic: 31.3 us -> 3.41 us
  between operations: 17.5 us -> 2.2 us
    reduce_scatter x7 -> x0, waiting for transfers between devices: 393 us -> none  [the longest x1 102 us: on_device(): lax.psum_scatter(gateup_grad.astype(jnp.bfloat16), ('ty', 'tx'), scatter_...]
    pallas_call x0 -> x18, Pallas kernels: none -> 124 us  [call(): pl.pallas_call(kernel, out_shape=outs, grid_spec=pltpu.PrefetchScalarGrid...]
    unnamed x22 -> x0, waiting for transfers between devices: 109 us -> none
    dot_general x21 -> x0, matrix products: 93.8 us -> none  [the longest x4 25.4 us: product_rt(): jnp.einsum('ik,jk->ij', left, right, preferred_element_type=jnp.float32)]
    psum x2 -> x0, blocking collectives: 50.5 us -> none  [the longest x1 39.4 us: on_device(): lax.psum((qgain_part, kgain_part), ('img', 'ty', 'tx'))]
    ppermute x0 -> x42, starting transfers between devices: none -> 50.2 us  [the longest x10 27.8 us: shift(): return lax.ppermute(value, 'img', pairs)]
    another operation x1 -> x0, waiting for transfers between devices: 48.2 us -> none
    all_gather x2 -> x0, waiting for transfers between devices: 45.4 us -> none  [the longest x1 24.4 us: on_device(): lax.all_gather(value_low, ('ty', 'tx'), axis=1, tiled=True)]
  transfers between devices with their start and end apart: 16 -> 49, of which waited for: 14 -> 8; matrix products, arithmetic and copies ran while one was open for 10% -> 1% of each run, Pallas kernels for 0% -> 49%
where the time goes in v2:
time: 234 us; the launch traced here: 233 us
  Pallas kernels  124 us (53%)
  starting transfers between devices  74.9 us (32%)
  waiting for transfers between devices  19.5 us (8%)
  local copies, waits for them, and re-layouts  9.15 us (4%)
  other arithmetic  3.41 us (1%)
    pallas_call x18, Pallas kernels, call(): pl.pallas_call(kernel, out_shape=outs, grid_spec=pltpu.PrefetchScalarGrid...  124 us
    ppermute x10, starting transfers between devices, shift(): return lax.ppermute(value, 'img', pairs)  27.8 us
    all_to_all x7, starting transfers between devices, exchange(): return lax.all_to_all(value, axes, split_axis=0, concat_axis=0, tiled=True)  24.7 us
    ppermute x30, starting transfers between devices, swap(): lax.ppermute(value, PLANE, [(index, index ^ bit) for index in range(8)])  18.4 us
    all_to_all x7, waiting for transfers between devices, exchange(): return lax.all_to_all(value, axes, split_axis=0, concat_axis=0, tiled=True)  11.1 us
    unnamed x106, local copies, waits for them, and re-layouts  9.12 us
    ppermute x30, waiting for transfers between devices, swap(): lax.ppermute(value, PLANE, [(index, index ^ bit) for index in range(8)])  8.37 us
  transfers between devices with their start and end apart: 49, of which 8 were waited for; matrix products, arithmetic and copies ran while one was open for 1% of the time, Pallas kernels for 49%

profile of v2, /device:TPU:0, one launch (start us, length us, event | category | flops | bytes accessed | tf_op | source)
XLA Modules:
  0.0 232.9 jit_solution(1114758184264271106)
XLA Ops:
  1.3 3.5 %open.1 = (bf16[144,1152]{1,0:T(8,128)(2,1)}, bf16[128,1152]{1,0:T(8,128)(2,1)}) custom-call(s32[1]{0:T(128)S(6)} %copy.24.bucket_ref, s32[2]{0:T(128)} %bitcast.24, f32[128,1152]{1,0:T(8,128)} %bitcast.21, f32[32,1152]{1,0:T(8,128)} %refs_12_.1, bf16[864,1152]{1,0:T(8,128)(2,1)} %bitcast.12, f32[864]{0:T(1024)} %bias_ref.1, f32[128,1152]{1,0:T(8,128)} %bitcast.17), custom_call_target="tpu_custom_call" | custom-call | flops 5000000000 | bytes 5000000 | tf_op jit(solution)/shard_map/open/pallas_call | solution.py:1090
  4.8 2.9 %collective-permute-start = (bf16[144,1152]{1,0:T(8,128)(2,1)}, bf16[144,1152]{1,0:T(8,128)(2,1)S(1)}, u32[]{:S(2)}, u32[]{:S(2)}) collective-permute-start(bf16[144,1152]{1,0:T(8,128)(2,1)} %get-tuple-element.126.refs_0_), channel_id=1, source_target_pairs={{0,1},{1,0},{2,3},{3,2},{4,5},{5,4},{6,7},{7,6},{8,9},{9,8},{10,11... | collective-permute-start | bytes 995336 | tf_op jit(solution)/shard_map/ppermute | solution.py:1119
  7.7 1.5 collective-permute-start.1
  9.9 9.0 %ready.1 = (bf16[1152,768]{1,0:T(8,128)(2,1)}, bf16[768,512]{1,0:T(8,128)(2,1)}, f32[3,128,128]{2,1,0:T(8,128)}, f32[8,128]{1,0:T(8,128)}, bf16[1152,384]{1,0:T(...) custom-call(s32[2]{0:T(128)} %pad_add_fusion.scalars, ...), custom_call_target="tpu_custom_call" | custom-call | flops 5000000000 | bytes 5000000 | tf_op jit(solution)/shard_map/ready/pallas_call | solution.py:1090
  20.3 4.5 %collective-permute-done.5.refs_6_ = bf16[80,1152]{1,0:T(8,128)(2,1)S(1)} collective-permute-done((bf16[80,1152]{1,0:T(8,128)(2,1)S(1)}, bf16[80,1152]{1,0:T(8,128)(2,1)S(1)}, u32[]{:S(2)}, u32[]{:S(2)}) %collective-permute-start.5) | collective-permute-done | bytes 184352 | tf_op jit(solution)/shard_map/ppermute | solution.py:1119
  24.9 1.6 collective-permute-done.4.refs_5_
  26.5 1.5 collective-permute-start.10
  30.1 14.5 %attend.1 = (bf16[1024,256]{1,0:T(8,128)(2,1)}, bf16[1024,1152]{1,0:T(8,128)(2,1)}, bf16[6,1024,128]{2,1,0:T(8,128)(2,1)}, f32[4,1024,128]{2,1,0:T(8,128)}, f32[...) custom-call(s32[2]{0:T(128)} %pad_add_fusion.scalars, ...), custom_call_target="tpu_custom_call" | custom-call | flops 15000000512 | bytes 15000000 | tf_op jit(solution)/shard_map/attend/pallas_call | solution.py:1090
  44.6 1.6 collective-permute-start.12
  46.7 3.7 %all-to-all-start = ((bf16[8,128,256]{2,1,0:T(8,128)(2,1)}), bf16[8,128,256]{2,1,0:T(8,128)(2,1)S(1)}, u32[]{:S(2)}, u32[]{:S(2)}) async-start(bf16[8,128,256]{2,1,0:T(8,128)(2,1)} %bitcast.15), calls=%async_computation | async-start | bytes 1048576 | tf_op jit(solution)/shard_map/all_to_all | solution.py:1142
  50.4 6.1 %act_grad.1.agrad_in = f32[128,3072]{1,0:T(8,128)} custom-call(bf16[3072,1152]{1,0:T(8,128)(2,1)} %refs_19_.1, f32[128,1152]{1,0:T(8,128)} %bitcast.18, f32[8,1152]{1,0:T(8,128)} %get-tuple-element.143.mod_ref.refs_20_), custom_call_target="tpu_custom_call" | custom-call | flops 5000000000 | bytes 5000000 | tf_op jit(solution)/shard_map/act_grad/pallas_call | solution.py:1090
  56.6 3.1 %all-to-all-done.att_ref = bf16[8,128,256]{2,1,0:T(8,128)(2,1)S(1)} async-done(((bf16[8,128,256]{2,1,0:T(8,128)(2,1)}), bf16[8,128,256]{2,1,0:T(8,128)(2,1)S(1)}, u32[]{:S(2)}, u32[]{:S(2)}) %all-to-all-start) | async-done | bytes 524320 | tf_op jit(solution)/shard_map/all_to_all | solution.py:1142
  60.5 3.8 %middle.1 = (f32[128,1152]{1,0:T(8,128)}, f32[128,1152]{1,0:T(8,128)}, bf16[128,1152]{1,0:T(8,128)(2,1)}) custom-call(bf16[8,128,256]{2,1,0:T(8,128)(2,1)} %copy-done.9, bf16[1152,1152]{1,0:T(8,128)(2,1)} %outw_ref.1, f32[128,1152]{1,0:T(8,128)} %bitcast.22, f32[8,1152]{1,0:T(8,128)} %get-tuple-element.143.mod_ref.refs_20_), custom_call_target="tpu_custom_call" | custom-call | flops 5000000000 | bytes 5000000 | tf_op jit(solution)/shard_map/middle/pallas_call | solution.py:1090
  64.2 1.5 collective-permute-start.16
  65.7 1.5 collective-permute-start.17
  67.2 14.2 %mlp.1 = (bf16[128,3072]{1,0:T(8,128)(2,1)}, f32[128,1152]{1,0:T(8,128)}, bf16[128,1152]{1,0:T(8,128)(2,1)}, bf16[8,128,256]{2,1,0:T(8,128)(2,1)}, f32[8,1152]{1,0:T(8,128)}) custom-call(bf16[1152,6144]{1,0:T(8,128)(2,1)} %up_ref.1, bf16[1152,6144]{1,0:T(8,128)(2,1)} %up_ref.1, bf16[1152,1152]{1,0:T(8,128)(2,1)} %outw_ref.1, ...), custom_call_target="tpu_custom_call" | custom-call | flops 12000000000 | bytes 12000000 | tf_op jit(solution)/shard_map/mlp/pallas_call | solution.py:1090
  82.6 6.2 %mlp_out.1 = (f32[128,1152]{1,0:T(8,128)}, f32[8,1152]{1,0:T(8,128)}) custom-call(bf16[128,3072]{1,0:T(8,128)(2,1)} %get-tuple-element.149.act_ref, bf16[3072,1152]{1,0:T(8,128)(2,1)} %refs_19_.1, f32[128,1152]{1,0:T(8,128)} %get-tuple-element.146.mid_ref, f32[128,1152]{1,0:T(8,128)} %bitcast.20, f32[8,1152]{1,0:T(8,128)} %get-tuple-element.143.mod_ref.refs_20_), custom_call_target="tpu_custom_call" | custom-call | flops 5000000000 | bytes 5000000 | tf_op jit(solution)/shard_map/mlp_out/pallas_call | solution.py:1090
  88.8 2.2 collective-permute-done.21.refs_5_
  92.7 3.6 %all-to-all-start.1 = ((bf16[8,128,256]{2,1,0:T(8,128)(2,1)}), bf16[8,128,256]{2,1,0:T(8,128)(2,1)S(1)}, u32[]{:S(2)}, u32[]{:S(2)}) async-start(bf16[8,128,256]{2,1,0:T(8,128)(2,1)} %get-tuple-element.152), calls=%async_computation.1 | async-start | bytes 1048576 | tf_op jit(solution)/shard_map/all_to_all | solution.py:1142
  97.8 14.2 %mlp_weights.1 = (bf16[864,384]{1,0:T(8,128)(2,1)}, bf16[864,384]{1,0:T(8,128)(2,1)}, bf16[864,384]{1,0:T(8,128)(2,1)}, bf16[864,384]{1,0:T(8,128)(2,1)}, bf16[864,384]{1,0:T(8,128)(2,1)}) custom-call(s32[2]{0:T(128)} %pad_add_fusion.scalars, bf16[128,1152]{1,0:T(8,128)(2,1)} %get-tuple-element.145.hid_ref.refs_0_, bf16[128,1152]{1,0:T(8,128)(2,1)} %copy-done.36, ...), custom_call_target="tpu_custom_call" | custom-call | flops 12000000000 | bytes 12000000 | tf_op jit(solution)/shard_map/mlp_weights/pallas_call | solution.py:1090
  112.1 2.1 collective-permute-start.27
  114.2 4.0 %collective-permute-start.26 = (bf16[864,384]{1,0:T(8,128)(2,1)}, bf16[864,384]{1,0:T(8,128)(2,1)S(1)}, u32[]{:S(2)}, u32[]{:S(2)}) collective-permute-start(bf16[864,384]{1,0:T(8,128)(2,1)} %get-tuple-element.180), channel_id=1, source_target_pairs={{0,8},{24,16},{1,9},{25,17},{2,10},{26,18},{3,11},{27,19},{4,12},{... | collective-permute-start | bytes 1990664 | tf_op jit(solution)/shard_map/ppermute | solution.py:1146
  118.4 16.9 %attend_back.1 = (bf16[1024,512]{1,0:T(8,128)(2,1)}, f32[8,128]{1,0:T(8,128)}) custom-call(bf16[1024,256]{1,0:T(8,128)(2,1)} %bitcast.16, bf16[6,1024,128]{2,1,0:T(8,128)(2,1)} %get-tuple-element.173.qkv_ref, f32[4,1024,128]{2,1,0:T(8,128)} %get-tuple-element.174.raw_ref, f32[2,1024,128]{2,1,0:T(8,128)} %get-tuple-element.175.turn_ref, ...), custom_call_target="tpu_custom_call" | custom-call | flops 15000000512 | bytes 15000000 | tf_op jit(solution)/shard_map/attend_back/pallas_call | solution.py:1090
  136.2 3.6 %all-to-all-start.2 = ((bf16[8,128,512]{2,1,0:T(8,128)(2,1)}), bf16[8,128,512]{2,1,0:T(8,128)(2,1)S(1)}, u32[]{:S(2)}, u32[]{:S(2)}) async-start(bf16[8,128,512]{2,1,0:T(8,128)(2,1)} %bitcast.14), calls=%async_computation.2 | async-start | bytes 2097152 | tf_op jit(solution)/shard_map/all_to_all | solution.py:1142
  140.8 1.6 collective-permute-start.31
  142.3 1.5 collective-permute-start.32
  143.9 4.4 %qkv_weights.1 = bf16[8,144,512]{2,1,0:T(8,128)(2,1)} custom-call(bf16[1024,1152]{1,0:T(8,128)(2,1)} %get-tuple-element.190.hid_ref, bf16[1024,512]{1,0:T(8,128)(2,1)} %get-tuple-element.191.back_ref), custom_call_target="tpu_custom_call" | custom-call | flops 5000000000 | bytes 5000000 | tf_op jit(solution)/shard_map/qkv_weights/pallas_call | solution.py:1090
  148.2 5.1 %out_weights.1.ograd_ref = bf16[4,144,288]{2,1,0:T(8,128)(2,1)} custom-call(s32[2]{0:T(128)} %pad_add_fusion.scalars, bf16[128,1152]{1,0:T(8,128)(2,1)} %get-tuple-element.153.refs_0_, bf16[128,1152]{1,0:T(8,128)(2,1)} %copy-done.33, bf16[128,1152]{1,0:T(8,128)(2,1)} %copy-done.31, bf16[128,1152]{1,0:T(8,128)(2,1)} %copy-done.42, ...), custom_call_target="tpu_custom_call" | custom-call | flops 5000000000 | bytes 5000000 | tf_op jit(solution)/shard_map/out_weights/pallas_call | solution.py:1090
  154.6 3.6 %all-to-all-start.3 = ((bf16[8,144,512]{2,1,0:T(8,128)(2,1)}), bf16[8,144,512]{2,1,0:T(8,128)(2,1)S(1)}, u32[]{:S(2)}, u32[]{:S(2)}) async-start(bf16[8,144,512]{2,1,0:T(8,128)(2,1)} %qkv_weights.1), calls=%async_computation.3 | async-start | bytes 2359296 | tf_op jit(solution)/shard_map/all_to_all | solution.py:1142
  159.0 1.3 add_convert_fusion
  160.4 1.3 collective-permute-start.35
  161.9 7.4 %collective-permute-start.34 = (bf16[864,384]{1,0:T(8,128)(2,1)S(1)}, bf16[864,384]{1,0:T(8,128)(2,1)}, u32[]{:S(2)}, u32[]{:S(2)}) collective-permute-start(bf16[864,384]{1,0:T(8,128)(2,1)S(1)} %add_convert_fusion.1), channel_id=1, source_target_pairs={{0,8},{8,16},{16,24},{1,9},{9,17},{17,25},{2,10},{10,18},{18,26},{... | collective-permute-start | bytes 1990664 | tf_op jit(solution)/shard_map/ppermute | solution.py:1146
  169.2 7.1 %input.1 = (f32[128,1152]{1,0:T(8,128)}, f32[32,8,128]{2,1,0:T(8,128)}) custom-call(bf16[8,128,512]{2,1,0:T(8,128)(2,1)} %copy-done.1, bf16[1152,3456]{1,0:T(8,128)(2,1)} %weight_ref.3, f32[128,1152]{1,0:T(8,128)} %bitcast.23, f32[128,1152]{1,0:T(8,128)} %get-tuple-element.196.mgrad_ref, f32[8,1152]{1,0:T(8,128)} %get-tuple-element.143.mod_ref.refs_20_, ...), custom_call_target="tpu_custom_call" | custom-call | flops 7000000000 | bytes 7000000 | tf_op jit(solution)/shard_map/input/pallas_call | solution.py:1090
  177.4 4.0 %join.1 = (bf16[144,1152]{1,0:T(8,128)(2,1)}, bf16[144,1152]{1,0:T(8,128)(2,1)}, bf16[144,1152]{1,0:T(8,128)(2,1)}, bf16[144,1152]{1,0:T(8,128)(2,1)}, bf16[144,1152]{1,0:T(8,128)(2,1)}) custom-call(s32[2]{0:T(128)} %pad_add_fusion.scalars, bf16[8,144,512]{2,1,0:T(8,128)(2,1)} %copy-done, bf16[4,144,288]{2,1,0:T(8,128)(2,1)} %out_weights.1.ograd_ref), custom_call_target="tpu_custom_call" | custom-call | flops 5000000000 | bytes 5000000 | tf_op jit(solution)/shard_map/join/pallas_call | solution.py:1090
  181.4 3.1 %collective-permute-start.33 = (bf16[144,1152]{1,0:T(8,128)(2,1)}, bf16[144,1152]{1,0:T(8,128)(2,1)S(1)}, u32[]{:S(2)}, u32[]{:S(2)}) collective-permute-start(bf16[144,1152]{1,0:T(8,128)(2,1)} %get-tuple-element.208), channel_id=1, source_target_pairs={{0,8},{24,16},{1,9},{25,17},{2,10},{26,18},{3,11},{27,19},{4,12},{... | collective-permute-start | bytes 995336 | tf_op jit(solution)/shard_map/ppermute | solution.py:1146
  184.6 3.3 %all-to-all-start.4 = ((f32[32,8,128]{2,1,0:T(8,128)}), f32[32,8,128]{2,1,0:T(8,128)S(1)}, u32[]{:S(2)}, u32[]{:S(2)}) async-start(f32[32,8,128]{2,1,0:T(8,128)} %get-tuple-element.209), calls=%async_computation.4 | async-start | bytes 262144 | tf_op jit(solution)/shard_map/all_to_all | solution.py:1142
  188.7 3.6 %turn.1 = (bf16[8,144,192]{2,1,0:T(8,128)(2,1)}, bf16[288,192]{1,0:T(8,128)(2,1)}, bf16[288,192]{1,0:T(8,128)(2,1)}) custom-call(s32[2]{0:T(128)} %pad_add_fusion.scalars, bf16[864,384]{1,0:T(8,128)(2,1)} %get-tuple-element.210.refs_0_, bf16[864,384]{1,0:T(8,128)(2,1)} %collective-permute-done.34.refs_1_, bf16[864,384]{1,0:T(8,128)(2,1)} %copy-done.17), custom_call_target="tpu_custom_call" | custom-call | flops 5000000000 | bytes 5000000 | tf_op jit(solution)/shard_map/turn/pallas_call | solution.py:1090
  192.3 4.5 %all-to-all-done.4.got_ref = f32[32,8,128]{2,1,0:T(8,128)S(1)} async-done(((f32[32,8,128]{2,1,0:T(8,128)}), f32[32,8,128]{2,1,0:T(8,128)S(1)}, u32[]{:S(2)}, u32[]{:S(2)}) %all-to-all-start.4) | async-done | bytes 131104 | tf_op jit(solution)/shard_map/all_to_all | solution.py:1142
  196.8 2.1 collective-permute-start.36
  199.9 3.5 %tail.1 = (f32[288,864]{1,0:T(8,128)}, f32[864]{0:T(1024)}, f32[72]{0:T(128)}, f32[72]{0:T(128)}, f32[8,8,288]{2,1,0:T(8,128)}, /*index=5*/f32[8,288]{1,0:T(8,128)}, f32[8,128]{1,0:T(8,128)}) custom-call(f32[32,8,128]{2,1,0:T(8,128)} %copy-done.13, f32[32,288]{1,0:T(8,128)} %get-tuple-element.217.table_ref, bf16[864,288]{1,0:T(8,128)(2,1)} %get-tuple-element.218.weight_ref), custom_call_target="tpu_custom_call" | custom-call | flops 5000000000 | bytes 5000000 | tf_op jit(solution)/shard_map/tail/pallas_call | solution.py:1090
  203.5 3.5 %all-to-all-start.5 = ((f32[8,8,288]{2,1,0:T(8,128)}), f32[8,8,288]{2,1,0:T(8,128)S(1)}, u32[]{:S(2)}, u32[]{:S(2)}) async-start(f32[8,8,288]{2,1,0:T(8,128)} %get-tuple-element.219), calls=%async_computation.5 | async-start | bytes 196608 | tf_op jit(solution)/shard_map/all_to_all | solution.py:1142
  207.7 3.3 %collective-permute-start.41 = (bf16[288,192]{1,0:T(8,128)(2,1)S(1)}, bf16[288,192]{1,0:T(8,128)(2,1)S(1)}, u32[]{:S(2)}, u32[]{:S(2)}) collective-permute-start(bf16[288,192]{1,0:T(8,128)(2,1)S(1)} %copy-done.48), channel_id=1, source_target_pairs={{0,4},{1,0},{2,5},{3,1},{4,6},{5,2},{6,7},{7,3},{8,12},{9,8},{10,1... | collective-permute-start | bytes 331784 | tf_op jit(solution)/shard_map/ppermute | solution.py:1471
  211.8 3.5 %all-to-all-start.6 = ((bf16[8,144,192]{2,1,0:T(8,128)(2,1)}), bf16[8,144,192]{2,1,0:T(8,128)(2,1)S(1)}, u32[]{:S(2)}, u32[]{:S(2)}) async-start(bf16[8,144,192]{2,1,0:T(8,128)(2,1)} %get-tuple-element.236), calls=%async_computation.6 | async-start | bytes 1179648 | tf_op jit(solution)/shard_map/all_to_all | solution.py:1142
  216.9 4.6 %collective-permute-start.38 = (bf16[144,1152]{1,0:T(8,128)(2,1)S(1)}, bf16[144,1152]{1,0:T(8,128)(2,1)S(1)}, u32[]{:S(2)}, u32[]{:S(2)}) collective-permute-start(bf16[144,1152]{1,0:T(8,128)(2,1)S(1)} %add_convert_fusion.4), channel_id=1, source_target_pairs={{0,8},{8,16},{16,24},{1,9},{9,17},{17,25},{2,10},{10,18},{18,26},{... | collective-permute-start | bytes 995336 | tf_op jit(solution)/shard_map/ppermute | solution.py:1146
  221.5 2.2 table.1
  223.8 1.5 all-to-all-done.6.got_ref
  226.1 3.2 %lay.1 = (f32[144,1536]{1,0:T(8,128)}, f32[288,384]{1,0:T(8,128)}) custom-call(s32[2]{0:T(128)} %pad_add_fusion.scalars, bf16[8,144,192]{2,1,0:T(8,128)(2,1)} %copy-done.7, bf16[288,192]{1,0:T(8,128)(2,1)} %copy-done.51, bf16[288,192]{1,0:T(8,128)(2,1)} %copy-done.52), custom_call_target="tpu_custom_call" | custom-call | flops 5000000000 | bytes 5000000 | tf_op jit(solution)/shard_map/lay/pallas_call | solution.py:1090
  230.7 2.2 finish.1
  (183 shorter events, 22.1 us)
Async XLA Ops:
  4.8 14.1 %collective-permute-start = (bf16[144,1152]{1,0:T(8,128)(2,1)}, bf16[144,1152]{1,0:T(8,128)(2,1)S(1)}, u32[]{:S(2)}, u32[]{:S(2)}) collective-permute-start(bf16[144,1152]{1,0:T(8,128)(2,1)} %get-tuple-element.126.refs_0_), channel_id=1, source_target_pairs={{0,1},{1,0},{2,3},{3,2},{4,5},{5,4},{6,7},{7,6},{8,9},{9,8},{10,11... | collective-permute-start | bytes 995336 | tf_op jit(solution)/shard_map/ppermute | solution.py:1119
  7.7 11.2 %collective-permute-start.1 = (bf16[144,1152]{1,0:T(8,128)(2,1)}, bf16[144,1152]{1,0:T(8,128)(2,1)S(1)}, u32[]{:S(2)}, u32[]{:S(2)}) collective-permute-start(bf16[144,1152]{1,0:T(8,128)(2,1)} %get-tuple-element.126.refs_0_), channel_id=1, source_target_pairs={{0,4},{1,5},{2,6},{3,7},{4,0},{5,1},{6,2},{7,3},{8,12},{9,13},{10,... | collective-permute-start | bytes 995336 | tf_op jit(solution)/shard_map/ppermute | solution.py:1119
  19.0 5.9 %collective-permute-start.5 = (bf16[80,1152]{1,0:T(8,128)(2,1)S(1)}, bf16[80,1152]{1,0:T(8,128)(2,1)S(1)}, u32[]{:S(2)}, u32[]{:S(2)}) collective-permute-start(bf16[80,1152]{1,0:T(8,128)(2,1)S(1)} %slice.7), channel_id=1, source_target_pairs={{0,1},{1,0},{2,3},{3,2},{4,5},{5,4},{6,7},{7,6},{8,9},{9,8},{10,11... | collective-permute-start | bytes 552968 | tf_op jit(solution)/shard_map/ppermute | solution.py:1119
  19.6 6.9 %collective-permute-start.2 = (bf16[144,1152]{1,0:T(8,128)(2,1)S(1)}, bf16[144,1152]{1,0:T(8,128)(2,1)S(1)}, u32[]{:S(2)}, u32[]{:S(2)}) collective-permute-start(bf16[144,1152]{1,0:T(8,128)(2,1)S(1)} %copy-done.18), channel_id=1, source_target_pairs={{0,2},{1,3},{2,0},{3,1},{4,6},{5,7},{6,4},{7,5},{8,10},{9,11},{10,... | collective-permute-start | bytes 995336 | tf_op jit(solution)/shard_map/ppermute | solution.py:1119
  19.6 8.9 %collective-permute-start.3 = (bf16[144,1152]{1,0:T(8,128)(2,1)S(1)}, bf16[144,1152]{1,0:T(8,128)(2,1)S(1)}, u32[]{:S(2)}, u32[]{:S(2)}) collective-permute-start(bf16[144,1152]{1,0:T(8,128)(2,1)S(1)} %collective-permute-done.refs_1_), channel_id=1, source_target_pairs={{0,2},{1,3},{2,0},{3,1},{4,6},{5,7},{6,4},{7,5},{8,10},{9,11},{10,... | collective-permute-start | bytes 995336 | tf_op jit(solution)/shard_map/ppermute | solution.py:1119
  20.1 8.4 %collective-permute-start.6 = (bf16[144,1152]{1,0:T(8,128)(2,1)S(1)}, bf16[144,1152]{1,0:T(8,128)(2,1)S(1)}, u32[]{:S(2)}, u32[]{:S(2)}) collective-permute-start(bf16[144,1152]{1,0:T(8,128)(2,1)S(1)} %collective-permute-done.1.refs_4_), channel_id=1, source_target_pairs={{0,2},{1,3},{2,0},{3,1},{4,6},{5,7},{6,4},{7,5},{8,10},{9,11},{10,... | collective-permute-start | bytes 995336 | tf_op jit(solution)/shard_map/ppermute | solution.py:1119
  20.1 6.3 %collective-permute-start.4 = (bf16[64,1152]{1,0:T(8,128)(2,1)S(1)}, bf16[64,1152]{1,0:T(8,128)(2,1)S(1)}, u32[]{:S(2)}, u32[]{:S(2)}) collective-permute-start(bf16[64,1152]{1,0:T(8,128)(2,1)S(1)} %slice.6), channel_id=1, source_target_pairs={{0,4},{1,5},{2,6},{3,7},{4,0},{5,1},{6,2},{7,3},{8,12},{9,13},{10,... | collective-permute-start | bytes 442376 | tf_op jit(solution)/shard_map/ppermute | solution.py:1119
  24.9 3.7 %collective-permute-start.8 = (bf16[80,1152]{1,0:T(8,128)(2,1)S(1)}, bf16[80,1152]{1,0:T(8,128)(2,1)S(1)}, u32[]{:S(2)}, u32[]{:S(2)}) collective-permute-start(bf16[80,1152]{1,0:T(8,128)(2,1)S(1)} %collective-permute-done.5.refs_6_), channel_id=1, source_target_pairs={{0,2},{1,3},{2,0},{3,1},{4,6},{5,7},{6,4},{7,5},{8,10},{9,11},{10,... | collective-permute-start | bytes 552968 | tf_op jit(solution)/shard_map/ppermute | solution.py:1119
  26.5 18.1 %collective-permute-start.10 = (bf16[128,1152]{1,0:T(8,128)(2,1)S(1)}, bf16[128,1152]{1,0:T(8,128)(2,1)S(1)}, u32[]{:S(2)}, u32[]{:S(2)}) collective-permute-start(bf16[128,1152]{1,0:T(8,128)(2,1)S(1)} %copy-done.24), channel_id=1, source_target_pairs={{0,1},{1,0},{2,3},{3,2},{4,5},{5,4},{6,7},{7,6},{8,9},{9,8},{10,11... | collective-permute-start | bytes 884744 | tf_op jit(solution)/shard_map/ppermute | solution.py:1119
  28.0 16.6 %collective-permute-start.11 = (bf16[128,1152]{1,0:T(8,128)(2,1)S(1)}, bf16[128,1152]{1,0:T(8,128)(2,1)S(1)}, u32[]{:S(2)}, u32[]{:S(2)}) collective-permute-start(bf16[128,1152]{1,0:T(8,128)(2,1)S(1)} %copy-done.24), channel_id=1, source_target_pairs={{0,4},{1,5},{2,6},{3,7},{4,0},{5,1},{6,2},{7,3},{8,12},{9,13},{10,... | collective-permute-start | bytes 884744 | tf_op jit(solution)/shard_map/ppermute | solution.py:1119
  28.5 16.1 %collective-permute-start.9 = (bf16[128,1152]{1,0:T(8,128)(2,1)S(1)}, bf16[128,1152]{1,0:T(8,128)(2,1)S(1)}, u32[]{:S(2)}, u32[]{:S(2)}) collective-permute-start(bf16[128,1152]{1,0:T(8,128)(2,1)S(1)} %copy-done.24), channel_id=1, source_target_pairs={{0,2},{1,3},{2,0},{3,1},{4,6},{5,7},{6,4},{7,5},{8,10},{9,11},{10,... | collective-permute-start | bytes 884744 | tf_op jit(solution)/shard_map/ppermute | solution.py:1119
  44.6 11.9 %collective-permute-start.12 = (bf16[128,1152]{1,0:T(8,128)(2,1)S(1)}, bf16[128,1152]{1,0:T(8,128)(2,1)S(1)}, u32[]{:S(2)}, u32[]{:S(2)}) collective-permute-start(bf16[128,1152]{1,0:T(8,128)(2,1)S(1)} %collective-permute-done.10.refs_9_), channel_id=1, source_target_pairs={{0,4},{1,5},{2,6},{3,7},{4,0},{5,1},{6,2},{7,3},{8,12},{9,13},{10,... | collective-permute-start | bytes 884744 | tf_op jit(solution)/shard_map/ppermute | solution.py:1119
  46.2 10.3 %collective-permute-start.13 = (bf16[128,1152]{1,0:T(8,128)(2,1)S(1)}, bf16[128,1152]{1,0:T(8,128)(2,1)S(1)}, u32[]{:S(2)}, u32[]{:S(2)}) collective-permute-start(bf16[128,1152]{1,0:T(8,128)(2,1)S(1)} %collective-permute-done.10.refs_9_), channel_id=1, source_target_pairs={{0,2},{1,3},{2,0},{3,1},{4,6},{5,7},{6,4},{7,5},{8,10},{9,11},{10,... | collective-permute-start | bytes 884744 | tf_op jit(solution)/shard_map/ppermute | solution.py:1119
  46.4 10.2 %collective-permute-start.14 = (bf16[128,1152]{1,0:T(8,128)(2,1)S(1)}, bf16[128,1152]{1,0:T(8,128)(2,1)S(1)}, u32[]{:S(2)}, u32[]{:S(2)}) collective-permute-start(bf16[128,1152]{1,0:T(8,128)(2,1)S(1)} %collective-permute-done.11.refs_12_), channel_id=1, source_target_pairs={{0,2},{1,3},{2,0},{3,1},{4,6},{5,7},{6,4},{7,5},{8,10},{9,11},{10,... | collective-permute-start | bytes 884744 | tf_op jit(solution)/shard_map/ppermute | solution.py:1119
  46.7 12.9 %all-to-all-start = ((bf16[8,128,256]{2,1,0:T(8,128)(2,1)}), bf16[8,128,256]{2,1,0:T(8,128)(2,1)S(1)}, u32[]{:S(2)}, u32[]{:S(2)}) async-start(bf16[8,128,256]{2,1,0:T(8,128)(2,1)} %bitcast.15), calls=%async_computation | async-start | bytes 1048576 | tf_op jit(solution)/shard_map/all_to_all | solution.py:1142
  64.2 17.2 %collective-permute-start.15 = (bf16[128,1152]{1,0:T(8,128)(2,1)}, bf16[128,1152]{1,0:T(8,128)(2,1)S(1)}, u32[]{:S(2)}, u32[]{:S(2)}) collective-permute-start(bf16[128,1152]{1,0:T(8,128)(2,1)} %get-tuple-element.145.hid_ref.refs_0_), channel_id=1, source_target_pairs={{0,2},{1,3},{2,0},{3,1},{4,6},{5,7},{6,4},{7,5},{8,10},{9,11},{10,... | collective-permute-start | bytes 884744 | tf_op jit(solution)/shard_map/ppermute | solution.py:1119
  64.2 17.2 %collective-permute-start.16 = (bf16[128,1152]{1,0:T(8,128)(2,1)}, bf16[128,1152]{1,0:T(8,128)(2,1)S(1)}, u32[]{:S(2)}, u32[]{:S(2)}) collective-permute-start(bf16[128,1152]{1,0:T(8,128)(2,1)} %get-tuple-element.145.hid_ref.refs_0_), channel_id=1, source_target_pairs={{0,1},{1,0},{2,3},{3,2},{4,5},{5,4},{6,7},{7,6},{8,9},{9,8},{10,11... | collective-permute-start | bytes 884744 | tf_op jit(solution)/shard_map/ppermute | solution.py:1119
  65.7 15.8 %collective-permute-start.17 = (bf16[128,1152]{1,0:T(8,128)(2,1)}, bf16[128,1152]{1,0:T(8,128)(2,1)S(1)}, u32[]{:S(2)}, u32[]{:S(2)}) collective-permute-start(bf16[128,1152]{1,0:T(8,128)(2,1)} %get-tuple-element.145.hid_ref.refs_0_), channel_id=1, source_target_pairs={{0,4},{1,5},{2,6},{3,7},{4,0},{5,1},{6,2},{7,3},{8,12},{9,13},{10,... | collective-permute-start | bytes 884744 | tf_op jit(solution)/shard_map/ppermute | solution.py:1119
  67.2 29.1 %collective-permute-start.25 = (bf16[128,1152]{1,0:T(8,128)(2,1)S(1)}, bf16[128,1152]{1,0:T(8,128)(2,1)S(1)}, u32[]{:S(2)}, u32[]{:S(2)}) collective-permute-start(bf16[128,1152]{1,0:T(8,128)(2,1)S(1)} %collective-permute-done.12.refs_13_), channel_id=1, source_target_pairs={{0,2},{1,3},{2,0},{3,1},{4,6},{5,7},{6,4},{7,5},{8,10},{9,11},{10,... | collective-permute-start | bytes 884744 | tf_op jit(solution)/shard_map/ppermute | solution.py:1119
  81.5 9.5 %collective-permute-start.21 = (bf16[128,1152]{1,0:T(8,128)(2,1)S(1)}, bf16[128,1152]{1,0:T(8,128)(2,1)S(1)}, u32[]{:S(2)}, u32[]{:S(2)}) collective-permute-start(bf16[128,1152]{1,0:T(8,128)(2,1)S(1)} %collective-permute-done.16.refs_1_), channel_id=1, source_target_pairs={{0,4},{1,5},{2,6},{3,7},{4,0},{5,1},{6,2},{7,3},{8,12},{9,13},{10,... | collective-permute-start | bytes 884744 | tf_op jit(solution)/shard_map/ppermute | solution.py:1119
  82.1 8.9 %collective-permute-start.22 = (bf16[128,1152]{1,0:T(8,128)(2,1)S(1)}, bf16[128,1152]{1,0:T(8,128)(2,1)S(1)}, u32[]{:S(2)}, u32[]{:S(2)}) collective-permute-start(bf16[128,1152]{1,0:T(8,128)(2,1)S(1)} %collective-permute-done.16.refs_1_), channel_id=1, source_target_pairs={{0,2},{1,3},{2,0},{3,1},{4,6},{5,7},{6,4},{7,5},{8,10},{9,11},{10,... | collective-permute-start | bytes 884744 | tf_op jit(solution)/shard_map/ppermute | solution.py:1119
  82.3 8.7 %collective-permute-start.23 = (bf16[128,1152]{1,0:T(8,128)(2,1)S(1)}, bf16[128,1152]{1,0:T(8,128)(2,1)S(1)}, u32[]{:S(2)}, u32[]{:S(2)}) collective-permute-start(bf16[128,1152]{1,0:T(8,128)(2,1)S(1)} %collective-permute-done.17.refs_4_), channel_id=1, source_target_pairs={{0,2},{1,3},{2,0},{3,1},{4,6},{5,7},{6,4},{7,5},{8,10},{9,11},{10,... | collective-permute-start | bytes 884744 | tf_op jit(solution)/shard_map/ppermute | solution.py:1119
  91.0 5.4 %collective-permute-start.24 = (bf16[128,1152]{1,0:T(8,128)(2,1)S(1)}, bf16[128,1152]{1,0:T(8,128)(2,1)S(1)}, u32[]{:S(2)}, u32[]{:S(2)}) collective-permute-start(bf16[128,1152]{1,0:T(8,128)(2,1)S(1)} %collective-permute-done.21.refs_5_), channel_id=1, source_target_pairs={{0,2},{1,3},{2,0},{3,1},{4,6},{5,7},{6,4},{7,5},{8,10},{9,11},{10,... | collective-permute-start | bytes 884744 | tf_op jit(solution)/shard_map/ppermute | solution.py:1119
  91.1 20.9 %collective-permute-start.18 = (bf16[128,1152]{1,0:T(8,128)(2,1)S(1)}, bf16[128,1152]{1,0:T(8,128)(2,1)S(1)}, u32[]{:S(2)}, u32[]{:S(2)}) collective-permute-start(bf16[128,1152]{1,0:T(8,128)(2,1)S(1)} %copy-done.27), channel_id=1, source_target_pairs={{0,2},{1,3},{2,0},{3,1},{4,6},{5,7},{6,4},{7,5},{8,10},{9,11},{10,... | collective-permute-start | bytes 884744 | tf_op jit(solution)/shard_map/ppermute | solution.py:1119
  91.6 20.4 %collective-permute-start.19 = (bf16[128,1152]{1,0:T(8,128)(2,1)S(1)}, bf16[128,1152]{1,0:T(8,128)(2,1)S(1)}, u32[]{:S(2)}, u32[]{:S(2)}) collective-permute-start(bf16[128,1152]{1,0:T(8,128)(2,1)S(1)} %copy-done.27), channel_id=1, source_target_pairs={{0,1},{1,0},{2,3},{3,2},{4,5},{5,4},{6,7},{7,6},{8,9},{9,8},{10,11... | collective-permute-start | bytes 884744 | tf_op jit(solution)/shard_map/ppermute | solution.py:1119
  92.2 19.8 %collective-permute-start.20 = (bf16[128,1152]{1,0:T(8,128)(2,1)S(1)}, bf16[128,1152]{1,0:T(8,128)(2,1)S(1)}, u32[]{:S(2)}, u32[]{:S(2)}) collective-permute-start(bf16[128,1152]{1,0:T(8,128)(2,1)S(1)} %copy-done.27), channel_id=1, source_target_pairs={{0,4},{1,5},{2,6},{3,7},{4,0},{5,1},{6,2},{7,3},{8,12},{9,13},{10,... | collective-permute-start | bytes 884744 | tf_op jit(solution)/shard_map/ppermute | solution.py:1119
  92.7 19.4 %all-to-all-start.1 = ((bf16[8,128,256]{2,1,0:T(8,128)(2,1)}), bf16[8,128,256]{2,1,0:T(8,128)(2,1)S(1)}, u32[]{:S(2)}, u32[]{:S(2)}) async-start(bf16[8,128,256]{2,1,0:T(8,128)(2,1)} %get-tuple-element.152), calls=%async_computation.1 | async-start | bytes 1048576 | tf_op jit(solution)/shard_map/all_to_all | solution.py:1142
  112.1 23.3 %collective-permute-start.27 = (bf16[128,1152]{1,0:T(8,128)(2,1)S(1)}, bf16[128,1152]{1,0:T(8,128)(2,1)S(1)}, u32[]{:S(2)}, u32[]{:S(2)}) collective-permute-start(bf16[128,1152]{1,0:T(8,128)(2,1)S(1)} %collective-permute-done.19.refs_1_), channel_id=1, source_target_pairs={{0,4},{1,5},{2,6},{3,7},{4,0},{5,1},{6,2},{7,3},{8,12},{9,13},{10,... | collective-permute-start | bytes 884744 | tf_op jit(solution)/shard_map/ppermute | solution.py:1119
  114.2 21.3 %collective-permute-start.28 = (bf16[128,1152]{1,0:T(8,128)(2,1)S(1)}, bf16[128,1152]{1,0:T(8,128)(2,1)S(1)}, u32[]{:S(2)}, u32[]{:S(2)}) collective-permute-start(bf16[128,1152]{1,0:T(8,128)(2,1)S(1)} %collective-permute-done.19.refs_1_), channel_id=1, source_target_pairs={{0,2},{1,3},{2,0},{3,1},{4,6},{5,7},{6,4},{7,5},{8,10},{9,11},{10,... | collective-permute-start | bytes 884744 | tf_op jit(solution)/shard_map/ppermute | solution.py:1119
  114.2 21.3 %collective-permute-start.26 = (bf16[864,384]{1,0:T(8,128)(2,1)}, bf16[864,384]{1,0:T(8,128)(2,1)S(1)}, u32[]{:S(2)}, u32[]{:S(2)}) collective-permute-start(bf16[864,384]{1,0:T(8,128)(2,1)} %get-tuple-element.180), channel_id=1, source_target_pairs={{0,8},{24,16},{1,9},{25,17},{2,10},{26,18},{3,11},{27,19},{4,12},{... | collective-permute-start | bytes 1990664 | tf_op jit(solution)/shard_map/ppermute | solution.py:1146
  118.1 17.3 %collective-permute-start.29 = (bf16[128,1152]{1,0:T(8,128)(2,1)S(1)}, bf16[128,1152]{1,0:T(8,128)(2,1)}, u32[]{:S(2)}, u32[]{:S(2)}) collective-permute-start(bf16[128,1152]{1,0:T(8,128)(2,1)S(1)} %collective-permute-done.20.refs_4_), channel_id=1, source_target_pairs={{0,2},{1,3},{2,0},{3,1},{4,6},{5,7},{6,4},{7,5},{8,10},{9,11},{10,... | collective-permute-start | bytes 884744 | tf_op jit(solution)/shard_map/ppermute | solution.py:1119
  135.5 4.3 %collective-permute-start.30 = (bf16[128,1152]{1,0:T(8,128)(2,1)S(1)}, bf16[128,1152]{1,0:T(8,128)(2,1)S(1)}, u32[]{:S(2)}, u32[]{:S(2)}) collective-permute-start(bf16[128,1152]{1,0:T(8,128)(2,1)S(1)} %collective-permute-done.27.refs_5_), channel_id=1, source_target_pairs={{0,2},{1,3},{2,0},{3,1},{4,6},{5,7},{6,4},{7,5},{8,10},{9,11},{10,... | collective-permute-start | bytes 884744 | tf_op jit(solution)/shard_map/ppermute | solution.py:1119
  136.2 18.4 %all-to-all-start.2 = ((bf16[8,128,512]{2,1,0:T(8,128)(2,1)}), bf16[8,128,512]{2,1,0:T(8,128)(2,1)S(1)}, u32[]{:S(2)}, u32[]{:S(2)}) async-start(bf16[8,128,512]{2,1,0:T(8,128)(2,1)} %bitcast.14), calls=%async_computation.2 | async-start | bytes 2097152 | tf_op jit(solution)/shard_map/all_to_all | solution.py:1142
  140.8 17.4 %collective-permute-start.31 = (bf16[864,384]{1,0:T(8,128)(2,1)}, bf16[864,384]{1,0:T(8,128)(2,1)S(1)}, u32[]{:S(2)}, u32[]{:S(2)}) collective-permute-start(bf16[864,384]{1,0:T(8,128)(2,1)} %add_convert_fusion.2), channel_id=1, source_target_pairs={{0,8},{8,16},{1,9},{9,17},{2,10},{10,18},{3,11},{11,19},{4,12},{12... | collective-permute-start | bytes 1990664 | tf_op jit(solution)/shard_map/ppermute | solution.py:1146
  142.3 16.7 %collective-permute-start.32 = (bf16[864,384]{1,0:T(8,128)(2,1)}, bf16[864,384]{1,0:T(8,128)(2,1)}, u32[]{:S(2)}, u32[]{:S(2)}) collective-permute-start(bf16[864,384]{1,0:T(8,128)(2,1)} %add_convert_fusion.2), channel_id=1, source_target_pairs={{24,16},{16,8},{25,17},{17,9},{26,18},{18,10},{27,19},{19,11},{28,... | collective-permute-start | bytes 1990664 | tf_op jit(solution)/shard_map/ppermute | solution.py:1146
  154.6 21.8 %all-to-all-start.3 = ((bf16[8,144,512]{2,1,0:T(8,128)(2,1)}), bf16[8,144,512]{2,1,0:T(8,128)(2,1)S(1)}, u32[]{:S(2)}, u32[]{:S(2)}) async-start(bf16[8,144,512]{2,1,0:T(8,128)(2,1)} %qkv_weights.1), calls=%async_computation.3 | async-start | bytes 2359296 | tf_op jit(solution)/shard_map/all_to_all | solution.py:1142
  160.4 27.5 %collective-permute-start.35 = (bf16[864,384]{1,0:T(8,128)(2,1)S(1)}, bf16[864,384]{1,0:T(8,128)(2,1)S(1)}, u32[]{:S(2)}, u32[]{:S(2)}) collective-permute-start(bf16[864,384]{1,0:T(8,128)(2,1)S(1)} %add_convert_fusion), channel_id=1, source_target_pairs={{24,16},{16,8},{8,0},{25,17},{17,9},{9,1},{26,18},{18,10},{10,2},{... | collective-permute-start | bytes 1990664 | tf_op jit(solution)/shard_map/ppermute | solution.py:1146
  161.9 26.0 %collective-permute-start.34 = (bf16[864,384]{1,0:T(8,128)(2,1)S(1)}, bf16[864,384]{1,0:T(8,128)(2,1)}, u32[]{:S(2)}, u32[]{:S(2)}) collective-permute-start(bf16[864,384]{1,0:T(8,128)(2,1)S(1)} %add_convert_fusion.1), channel_id=1, source_target_pairs={{0,8},{8,16},{16,24},{1,9},{9,17},{17,25},{2,10},{10,18},{18,26},{... | collective-permute-start | bytes 1990664 | tf_op jit(solution)/shard_map/ppermute | solution.py:1146
  181.4 15.3 %collective-permute-start.33 = (bf16[144,1152]{1,0:T(8,128)(2,1)}, bf16[144,1152]{1,0:T(8,128)(2,1)S(1)}, u32[]{:S(2)}, u32[]{:S(2)}) collective-permute-start(bf16[144,1152]{1,0:T(8,128)(2,1)} %get-tuple-element.208), channel_id=1, source_target_pairs={{0,8},{24,16},{1,9},{25,17},{2,10},{26,18},{3,11},{27,19},{4,12},{... | collective-permute-start | bytes 995336 | tf_op jit(solution)/shard_map/ppermute | solution.py:1146
  184.6 12.2 %all-to-all-start.4 = ((f32[32,8,128]{2,1,0:T(8,128)}), f32[32,8,128]{2,1,0:T(8,128)S(1)}, u32[]{:S(2)}, u32[]{:S(2)}) async-start(f32[32,8,128]{2,1,0:T(8,128)} %get-tuple-element.209), calls=%async_computation.4 | async-start | bytes 262144 | tf_op jit(solution)/shard_map/all_to_all | solution.py:1142
  196.8 18.5 %collective-permute-start.36 = (bf16[144,1152]{1,0:T(8,128)(2,1)S(1)}, bf16[144,1152]{1,0:T(8,128)(2,1)S(1)}, u32[]{:S(2)}, u32[]{:S(2)}) collective-permute-start(bf16[144,1152]{1,0:T(8,128)(2,1)S(1)} %add_convert_fusion.5), channel_id=1, source_target_pairs={{0,8},{8,16},{1,9},{9,17},{2,10},{10,18},{3,11},{11,19},{4,12},{12... | collective-permute-start | bytes 995336 | tf_op jit(solution)/shard_map/ppermute | solution.py:1146
  199.0 16.4 %collective-permute-start.37 = (bf16[144,1152]{1,0:T(8,128)(2,1)S(1)}, bf16[144,1152]{1,0:T(8,128)(2,1)S(1)}, u32[]{:S(2)}, u32[]{:S(2)}) collective-permute-start(bf16[144,1152]{1,0:T(8,128)(2,1)S(1)} %add_convert_fusion.5), channel_id=1, source_target_pairs={{24,16},{16,8},{25,17},{17,9},{26,18},{18,10},{27,19},{19,11},{28,... | collective-permute-start | bytes 995336 | tf_op jit(solution)/shard_map/ppermute | solution.py:1146
  203.5 8.4 %all-to-all-start.5 = ((f32[8,8,288]{2,1,0:T(8,128)}), f32[8,8,288]{2,1,0:T(8,128)S(1)}, u32[]{:S(2)}, u32[]{:S(2)}) async-start(f32[8,8,288]{2,1,0:T(8,128)} %get-tuple-element.219), calls=%async_computation.5 | async-start | bytes 196608 | tf_op jit(solution)/shard_map/all_to_all | solution.py:1142
  207.0 16.7 %collective-permute-start.40 = (bf16[288,192]{1,0:T(8,128)(2,1)S(1)}, bf16[288,192]{1,0:T(8,128)(2,1)S(1)}, u32[]{:S(2)}, u32[]{:S(2)}) collective-permute-start(bf16[288,192]{1,0:T(8,128)(2,1)S(1)} %copy-done.49), channel_id=1, source_target_pairs={{0,0},{1,4},{2,1},{3,5},{4,2},{5,6},{6,3},{7,7},{8,8},{9,12},{10,9... | collective-permute-start | bytes 331784 | tf_op jit(solution)/shard_map/ppermute | solution.py:1470
  207.7 16.1 %collective-permute-start.41 = (bf16[288,192]{1,0:T(8,128)(2,1)S(1)}, bf16[288,192]{1,0:T(8,128)(2,1)S(1)}, u32[]{:S(2)}, u32[]{:S(2)}) collective-permute-start(bf16[288,192]{1,0:T(8,128)(2,1)S(1)} %copy-done.48), channel_id=1, source_target_pairs={{0,4},{1,0},{2,5},{3,1},{4,6},{5,2},{6,7},{7,3},{8,12},{9,8},{10,1... | collective-permute-start | bytes 331784 | tf_op jit(solution)/shard_map/ppermute | solution.py:1471
  211.8 13.4 %all-to-all-start.6 = ((bf16[8,144,192]{2,1,0:T(8,128)(2,1)}), bf16[8,144,192]{2,1,0:T(8,128)(2,1)S(1)}, u32[]{:S(2)}, u32[]{:S(2)}) async-start(bf16[8,144,192]{2,1,0:T(8,128)(2,1)} %get-tuple-element.236), calls=%async_computation.6 | async-start | bytes 1179648 | tf_op jit(solution)/shard_map/all_to_all | solution.py:1142
  215.5 13.8 %collective-permute-start.39 = (bf16[144,1152]{1,0:T(8,128)(2,1)S(1)}, bf16[144,1152]{1,0:T(8,128)(2,1)S(1)}, u32[]{:S(2)}, u32[]{:S(2)}) collective-permute-start(bf16[144,1152]{1,0:T(8,128)(2,1)S(1)} %add_convert_fusion.3), channel_id=1, source_target_pairs={{24,16},{16,8},{8,0},{25,17},{17,9},{9,1},{26,18},{18,10},{10,2},{... | collective-permute-start | bytes 995336 | tf_op jit(solution)/shard_map/ppermute | solution.py:1146
  216.9 12.4 %collective-permute-start.38 = (bf16[144,1152]{1,0:T(8,128)(2,1)S(1)}, bf16[144,1152]{1,0:T(8,128)(2,1)S(1)}, u32[]{:S(2)}, u32[]{:S(2)}) collective-permute-start(bf16[144,1152]{1,0:T(8,128)(2,1)S(1)} %add_convert_fusion.4), channel_id=1, source_target_pairs={{0,8},{8,16},{16,24},{1,9},{9,17},{17,25},{2,10},{10,18},{18,26},{... | collective-permute-start | bytes 995336 | tf_op jit(solution)/shard_map/ppermute | solution.py:1146
  (54 other events, 338.4 us)

commit v3 on v2

--- a/solution.py
+++ b/solution.py
@@ -415,28 +415,20 @@
     wide = 3 * heads * LANES
     for index, part in enumerate(qkv_parts):
         window_ref[:, LANES * index : LANES * (index + 1)] = part[...]
-    row = lax.broadcasted_iota(jnp.int32, (wide, wide), 0)
-    lane = lax.broadcasted_iota(jnp.int32, (wide, wide), 1)
+    lane = lax.broadcasted_iota(jnp.int32, (1, wide), 1)
     place = lane % LANES
     part = lane // LANES
     side = part // heads
     entry, _ = lane_entry(place)
     entry = jnp.where(side == 2, jnp.where(place < HD, place, -1), entry)
     local = HD * (part % heads) + entry
-    skew = mine * (span - LANES)
-    pick = (entry >= 0) & (row == side * (2 * LANES) + skew + local)
-    pick_ref[...] = pick.astype(jnp.float32).astype(jnp.bfloat16)
+    source = jnp.where(entry >= 0, side * (2 * LANES) + mine * (span - LANES) + local, -1)
+    row = lax.broadcasted_iota(jnp.int32, (wide, wide), 0)
+    pick_ref[...] = (row == source).astype(jnp.float32).astype(jnp.bfloat16)
     spread_ref[...] = dot_nn(window_ref[...], pick_ref[...]).astype(jnp.bfloat16)
-    columns = order_ref.shape[1]
-    row = lax.broadcasted_iota(jnp.int32, (wide, columns), 0)
-    lane = lax.broadcasted_iota(jnp.int32, (wide, columns), 1)
-    place = row % LANES
-    part = row // LANES
-    side = part // heads
-    entry, _ = lane_entry(place)
-    entry = jnp.where(side == 2, jnp.where(place < HD, place, -1), entry)
-    pick = (entry >= 0) & (lane == side * span + HD * (part % heads) + entry)
-    order_ref[...] = pick.astype(jnp.float32).astype(jnp.bfloat16)
+    source = jnp.where(entry >= 0, side * span + local, -1)
+    row = lax.broadcasted_iota(jnp.int32, order_ref.shape, 0)
+    order_ref[...] = (row == source).astype(jnp.float32).astype(jnp.bfloat16)
     tokens = turn_ref.shape[1]
     token = lax.broadcasted_iota(jnp.int32, (tokens, LANES), 0)
     entry, column = lane_entry(lax.broadcasted_iota(jnp.int32, (tokens, LANES), 1))
@@ -489,8 +481,9 @@
     pieces, refs = refs[:10], refs[10:]
     (
         spread_ref, offset_ref, gain_ref,
-        att_ref, hid_ref, qkv_ref, raw_ref, turn_ref, mod_ref, log_ref, mixed_ref,
-        all_ref, extra_ref, rows_ref, flat_ref, anchor_ref, vt_ref, sems, extra_sems,
+        att_ref, hid_any, qkv_any, unit_any, turn_any, mod_ref, log_ref, mixed_ref,
+        all_ref, extra_ref, rows_ref, flat_ref, anchor_ref, vt_ref,
+        hid_ref, qkv_ref, unit_ref, turn_ref, sems, extra_sems, out_sems,
     ) = refs
     mine = scalars[0]
     own, xn, core, cx, yn, d1, d2, cy, cd1, cd2 = pieces
@@ -557,9 +550,11 @@
         product = dot_nn(hidden, spread_ref[...])
         for part in range(2 * heads):
             raw = product[:, LANES * part : LANES * (part + 1)]
-            raw_ref[part, rows, :] = raw
             gain = query_gain * scale if part < heads else key_gain
-            unit = raw * unit_rate(raw) * gain
+            rate = unit_rate(raw)
+            unit = raw * rate
+            unit_ref[part, rows, :] = jnp.where(lane < LANES - 1, unit, rate)
+            unit = unit * gain
             turned = unit * turn_cos + pltpu.roll(unit, LANES // 2, 1) * turn_sin
             qkv_ref[part, rows, :] = turned.astype(jnp.bfloat16)
         for part in range(2 * heads, 3 * heads):
@@ -569,6 +564,14 @@
         return carry
 
     lax.fori_loop(0, blocks, project, 0, unroll=2)
+    leaving = [
+        pltpu.make_async_copy(source, target, out_sems.at[index])
+        for index, (source, target) in enumerate(
+            ((qkv_ref, qkv_any), (unit_ref, unit_any), (hid_ref, hid_any), (turn_ref, turn_any))
+        )
+    ]
+    for copy in leaving:
+        copy.start()
     chunk = 2 * tokens
     for head in range(heads):
         vt_ref[head] = qkv_ref[2 * heads + head].T
@@ -580,27 +583,22 @@
             expo = jnp.exp2(scores)
             total = column_sum(expo)
             mixed = dot_nn(vt_ref[head], expo.astype(jnp.bfloat16)) * (1.0 / total)
-            mixed = mixed.T
             log_ref[head, pl.ds(index, 1), :] = jnp.log2(total)
-            mixed_ref[head, rows, :] = mixed
-            att_ref[rows, LANES * head : LANES * (head + 1)] = mixed.astype(jnp.bfloat16)
+            mixed_ref[head, :, rows] = mixed
+            for block in range(chunk // tokens):
+                att_ref[index * (chunk // tokens) + block, HD * head : HD * (head + 1), :] = mixed[
+                    0:HD, tokens * block : tokens * (block + 1)
+                ].astype(jnp.bfloat16)
         return carry
 
-    lax.fori_loop(0, everyone // chunk, attend, 0)
+    lax.fori_loop(0, everyone // chunk, attend, 0, unroll=2)
+    for copy in leaving:
+        copy.wait()
 
 
 def middle_kernel(att_ref, weight_ref, x_ref, mod_ref, out_ref, mid_ref, hid_ref):
-    blocks = att_ref.shape[0]
-    heads = HEADS // blocks
-    attended = jnp.concatenate(
-        [
-            att_ref[index, :, LANES * head : LANES * head + HD]
-            for index in range(blocks)
-            for head in range(heads)
-        ],
-        axis=1,
-    )
-    attn_out = dot_nn(attended, weight_ref[...])
+    attended = att_ref[...].reshape(weight_ref.shape[0], att_ref.shape[2])
+    attn_out = dot_tn(attended, weight_ref[...])
     out_ref[...] = attn_out
     middle = x_ref[...] + mod_ref[2:3, :] * attn_out
     mid_ref[...] = middle
@@ -622,8 +620,6 @@
     act_ref, mgrad_ref, agrad_ref, dgrad_ref, sums_ref, back_ref,
 ):
     step = pl.program_id(0)
-    blocks = dgrad_ref.shape[0]
-    heads = HEADS // blocks
 
     hidden = hid_ref[...]
     gate = dot_nn(hidden, gate_ref[...])
@@ -659,14 +655,8 @@
         mgrad_ref[...] = middle_grad
         attn_grad = (mod_ref[2:3, :] * middle_grad).astype(jnp.bfloat16)
         agrad_ref[...] = attn_grad
-        dgrad_ref[...] = jnp.zeros_like(dgrad_ref)
-        for index in range(blocks):
-            rows = outw_ref[HD * heads * index : HD * heads * (index + 1), :]
-            piece = dot_nt(attn_grad, rows).astype(jnp.bfloat16)
-            for head in range(heads):
-                dgrad_ref[index, :, LANES * head : LANES * head + HD] = piece[
-                    :, HD * head : HD * (head + 1)
-                ]
+        attended = dot_nt(outw_ref[...], attn_grad).astype(jnp.bfloat16)
+        dgrad_ref[...] = attended.reshape(dgrad_ref.shape)
         sums_ref[...] = jnp.zeros_like(sums_ref)
         sums_ref[2:3, :] = column_sum(middle_grad * attn_ref[...])
         sums_ref[3:4, :] = column_sum(back)
@@ -694,7 +684,7 @@
 def mlp_weights_kernel(scalars, *refs):
     hid_pieces, cot_pieces, refs = refs[:8], refs[8:16], refs[16:]
     (
-        gate_ref, up_ref, down_a, down_b, mod_ref, own_ref, next_ref, two_ref, last_ref, far_ref,
+        gate_ref, up_ref, down_a, down_b, mod_ref, own_ref, near_ref, two_ref, far_ref,
         all_ref, low_ref, act_ref, down_ref, out_ref, sems, out_sems,
     ) = refs
     tokens, width = hid_pieces[0].shape
@@ -710,11 +700,18 @@
     down_ref[0:run, :] = down_a[...]
     down_ref[run:units, :] = down_b[...]
     gate_mid = mod_ref[5:6, :]
-    for copy in copies:
+    chunk = everyone // 2
+    early = [copies[index] for index in (0, 1, 2, 3, 8, 9, 10, 11)]
+    late = [copies[index] for index in (4, 5, 6, 7, 12, 13, 14, 15)]
+    for copy in early:
         copy.wait()
-    chunk = everyone // 4
 
     def chunked(index, carry):
+        @pl.when(index == 1)
+        def _():
+            for copy in late:
+                copy.wait()
+
         span = pl.ds(pl.multiple_of(index * chunk, chunk), chunk)
         low = (low_ref[span, :].astype(jnp.float32) * gate_mid).astype(jnp.bfloat16)
         low_ref[span, :] = low
@@ -730,7 +727,7 @@
         act_ref[2, span, :] = (act_grad * silu).astype(jnp.bfloat16)
         return carry
 
-    lax.fori_loop(0, everyone // chunk, chunked, 0, unroll=2)
+    lax.fori_loop(0, everyone // chunk, chunked, 0)
     lanes = width // units
     for side in range(2):
         grad = dot_tn(act_ref[1 + side], all_ref[...]).astype(jnp.bfloat16)
@@ -745,14 +742,14 @@
         out_ref[image, run * lanes : run * lanes + share, :] = down[
             share * image : share * (image + 1), :
         ]
-    deal(out_ref, scalars[1], (own_ref, next_ref, two_ref, last_ref, far_ref), out_sems)
+    deal(out_ref, scalars[1], (own_ref, near_ref, two_ref, far_ref), out_sems)
 
 
 def deal(ref, place, targets, sems):
-    owners = [place, (place + 1) % 4, (place + 2) % 4, (place + 3) % 4, 3 - place]
+    owners = [place ^ bits for bits in range(4)]
     copies = [
         pltpu.make_async_copy(ref.at[owner], target, sems.at[index])
-        for index, (owner, target) in enumerate(zip(owners, targets, strict=False))
+        for index, (owner, target) in enumerate(zip(owners, targets, strict=True))
     ]
     for copy in copies:
         copy.start()
@@ -768,7 +765,7 @@
 
 
 def turn_kernel(scalars, *refs):
-    parts, refs = refs[:3], refs[3:]
+    parts, refs = refs[:5], refs[5:]
     send_ref, first_ref, second_ref = refs
     blocks, rows, run = send_ref.shape
     units = parts[0].shape[1]
@@ -787,11 +784,11 @@
             second_ref[...] = down[:, run * (1 - parity) : run * (2 - parity)]
 
 
-def lay_kernel(scalars, got_ref, first_ref, second_ref, out_ref, down_ref):
-    out_ref[...] = jnp.concatenate(
+def lay_kernel(scalars, got_ref, first_ref, second_ref, *refs):
+    parts, (gateup_ref, down_ref, qkv_ref, out_ref) = refs[:5], refs[5:]
+    gateup_ref[...] = jnp.concatenate(
         [got_ref[index].astype(jnp.float32) for index in range(got_ref.shape[0])], axis=1
     )
-    run = first_ref.shape[1]
     first = first_ref[...].astype(jnp.float32)
     second = second_ref[...].astype(jnp.float32)
     half = got_ref.shape[0] // 2
@@ -804,9 +801,6 @@
     def _():
         down_ref[...] = jnp.concatenate([second, first], axis=1)
 
-
-def finish_kernel(*refs):
-    parts, (qkv_ref, out_ref) = refs[:3], refs[3:]
     total = summed(parts, pl.ds(0, qkv_ref.shape[0]))
     columns = qkv_ref.shape[1]
     qkv_ref[...] = total[:, 0:columns]
@@ -886,52 +880,61 @@
 
 
 def attend_back_kernel(
-    attg_ref, qkv_ref, raw_ref, turn_ref, log_ref, mixed_ref, gain_ref, order_ref,
-    back_ref, gsum_ref, kt_ref, grad_ref,
+    attg_ref, qkv_ref, log_ref, mixed_ref, gain_ref, unit_any, turn_any, order_any,
+    back_ref, gsum_ref, kt_ref, up_ref, upt_ref, grad_ref, unit_ref, turn_ref, order_ref, sems,
 ):
-    heads = attg_ref.shape[1] // LANES
-    everyone = attg_ref.shape[0]
+    blocks, _, tokens = attg_ref.shape
+    heads = HEADS // blocks
+    everyone = blocks * tokens
     lines, chunk = log_ref.shape[1:]
     scale = HD ** (-0.5)
+    late = [
+        pltpu.make_async_copy(source, target, sems.at[index])
+        for index, (source, target) in enumerate(
+            ((unit_any, unit_ref), (turn_any, turn_ref), (order_any, order_ref))
+        )
+    ]
+    for copy in late:
+        copy.start()
     query_gain, key_gain = gain_ref[0:1, :], gain_ref[1:2, :]
     for head in range(heads):
         kt_ref[head] = qkv_ref[heads + head].T
-    ones = jnp.ones((8, LANES), jnp.bfloat16)
-
-    def attend(index, first):
+        grad_ref[heads + head] = jnp.zeros((everyone, LANES), jnp.float32)
+        grad_ref[2 * heads + head] = jnp.zeros((everyone, LANES), jnp.float32)
+        for block in range(blocks):
+            piece = jnp.concatenate(
+                [
+                    attg_ref[block, HD * head : HD * (head + 1), :],
+                    jnp.zeros((LANES - HD, tokens), jnp.bfloat16),
+                ],
+                axis=0,
+            )
+            upt_ref[head, :, tokens * block : tokens * (block + 1)] = piece
+        up_ref[head] = upt_ref[head].T
+
+    def attend(index, carry):
         rows = pl.ds(pl.multiple_of(index * chunk, chunk), chunk)
         for head in range(heads):
             query = qkv_ref[head, rows, :]
-            upstream = attg_ref[rows, LANES * head : LANES * (head + 1)]
-            weighted = upstream.astype(jnp.float32) * mixed_ref[head, rows, :]
-            high = weighted.astype(jnp.bfloat16)
-            low = (weighted - high.astype(jnp.float32)).astype(jnp.bfloat16)
-            delta = (dot_nt(ones, high) + dot_nt(ones, low))[0:1, :]
+            upstream = up_ref[head, rows, :]
+            turned = upt_ref[head, :, rows]
+            delta = column_sum(turned.astype(jnp.float32) * mixed_ref[head, :, rows])
             probs = jnp.exp2(
                 dot_nt(qkv_ref[heads + head], query) - log_ref[head, pl.ds(index, 1), :]
             )
-            score_grad = (probs * (dot_nt(qkv_ref[2 * heads + head], upstream) - delta)).astype(
+            score_grad = (probs * (dot_nn(qkv_ref[2 * heads + head], turned) - delta)).astype(
                 jnp.bfloat16
             )
-            value_part = dot_nn(probs.astype(jnp.bfloat16), upstream)
-            key_part = dot_nn(score_grad, query)
-            if first:
-                grad_ref[2 * heads + head] = value_part
-                grad_ref[heads + head] = key_part
-            else:
-                grad_ref[2 * heads + head] += value_part
-                grad_ref[heads + head] += key_part
+            grad_ref[2 * heads + head] += dot_nn(probs.astype(jnp.bfloat16), upstream)
+            grad_ref[heads + head] += dot_nn(score_grad, query)
             grad_ref[head, rows, :] = dot_nn(kt_ref[head], score_grad).T
-
-    attend(0, True)
-
-    def later(index, carry):
-        attend(index, False)
         return carry
 
-    lax.fori_loop(1, lines, later, 0)
+    lax.fori_loop(0, lines, attend, 0, unroll=2)
     gsum_ref[...] = jnp.zeros_like(gsum_ref)
-    step = 2 * LANES
+    step = tokens
+    for copy in late:
+        copy.wait()
 
     def finish(index, carry):
         rows = pl.ds(pl.multiple_of(index * step, step), step)
@@ -942,28 +945,32 @@
             gain = query_gain if part < heads else key_gain
             grad = grad_ref[part, rows, :] * (scale if part < heads else math.log(2.0))
             turned = grad * turn_cos - pltpu.roll(grad, LANES // 2, 1) * turn_sin
-            raw = raw_ref[part, rows, :]
-            rate = unit_rate(raw)
-            unit = raw * rate
+            unit = unit_ref[part, rows, :]
+            rate = unit[:, LANES - 1 : LANES]
             line = 0 if part < heads else 1
             product = turned * unit
             gsum_ref[line : line + 1, :] += column_sum(product)
-            lifted = turned * gain
             mean = jnp.sum(product * gain, axis=-1, keepdims=True) * (1.0 / HD)
-            parts.append((rate * (lifted - unit * mean)).astype(jnp.bfloat16))
+            parts.append((rate * (turned * gain - unit * mean)).astype(jnp.bfloat16))
         for part in range(2 * heads, 3 * heads):
             parts.append(grad_ref[part, rows, :].astype(jnp.bfloat16))
-        back_ref[rows, :] = dot_nn(jnp.concatenate(parts, axis=1), order_ref[...]).astype(
+        back_ref[index] = dot_nt(order_ref[...], jnp.concatenate(parts, axis=1)).astype(
             jnp.bfloat16
         )
         return carry
 
-    lax.fori_loop(0, everyone // step, finish, 0)
+    lax.fori_loop(0, everyone // step, finish, 0, unroll=2)
 
 
 def qkv_weights_kernel(hid_ref, back_ref, grad_ref):
-    grad = dot_tn(hid_ref[...], back_ref[...]).astype(jnp.bfloat16)
-    grad_ref[...] = grad.reshape(grad_ref.shape)
+    blocks = back_ref.shape[0]
+    back = jnp.concatenate([back_ref[index] for index in range(blocks)], axis=1)
+    grad = dot_nn(back, hid_ref[...]).astype(jnp.bfloat16).T
+    columns = grad.shape[1]
+    grad_ref[:, :, LANES * (columns // LANES) :] = jnp.zeros(
+        (*grad_ref.shape[:2], grad_ref.shape[2] - LANES * (columns // LANES)), jnp.bfloat16
+    )
+    grad_ref[:, :, 0:columns] = grad.reshape(*grad_ref.shape[:2], columns)
 
 
 def out_weights_kernel(images, scalars, *refs):
@@ -971,7 +978,6 @@
     att_ref, ograd_ref, low_ref, sems = refs
     tokens, width = pieces[0].shape
     mine = scalars[0]
-    heads = att_ref.shape[1] // LANES
     copies = block_copies(
         pieces,
         low_ref,
@@ -983,17 +989,15 @@
         copy.start()
     for copy in copies:
         copy.wait()
-    outw = dot_tn(att_ref[...], low_ref[...]).astype(jnp.bfloat16)
+    attended = jnp.concatenate([att_ref[index] for index in range(att_ref.shape[0])], axis=1)
+    outw = dot_nn(attended, low_ref[...]).astype(jnp.bfloat16)
     share = width // images
     for image in range(images):
-        for head in range(heads):
-            ograd_ref[image, HD * head : HD * (head + 1), :] = outw[
-                LANES * head : LANES * head + HD, share * image : share * (image + 1)
-            ]
+        ograd_ref[image] = outw[:, share * image : share * (image + 1)]
 
 
 def join_kernel(scalars, grad_ref, ograd_ref, *refs):
-    targets, (out_ref, sems) = refs[:5], refs[5:]
+    targets, (out_ref, sems) = refs[:4], refs[4:]
     images = out_ref.shape[0]
     blocks = grad_ref.shape[0]
     span = HD * HEADS // blocks
@@ -1028,10 +1032,13 @@
         @pl.when(step == side)
         def _(side=side):
             natural = jnp.concatenate(
-                [back_ref[index, :, span * side : span * (side + 1)] for index in range(blocks)],
-                axis=1,
+                [back_ref[index, span * side : span * (side + 1), :] for index in range(blocks)],
+                axis=0,
             )
-            part = dot_nt(natural, weight_ref[...])
+            part = lax.dot_general(
+                natural, weight_ref[...], (((0,), (1,)), ((), ())),
+                preferred_element_type=jnp.float32,
+            )
             acc_ref[...] = part if side == 0 else acc_ref[...] + part
 
     @pl.when(step == 2)
@@ -1155,18 +1162,14 @@
 
 
 def line_first(shares):
-    return shift(shares[4], [(0, 1), (3, 2)])
-
-
-def line_second(shares, first):
-    value = add(shares[2], first)
-    return shift(value, [(0, 1), (1, 2)]), shift(value, [(3, 2), (2, 1)])
-
-
-def line_third(shares, up, down):
+    return shift(shares[3], [(0, 1), (3, 2)]), shift(shares[3], [(1, 2), (2, 1)])
+
+
+def line_second(shares, way):
     return (
-        shift(add(shares[1], up), [(0, 1), (1, 2), (2, 3)]),
-        shift(add(shares[3], down), [(3, 2), (2, 1), (1, 0)]),
+        shift(add(shares[2], way), [(1, 3), (2, 0)]),
+        shift(shares[2], [(0, 2), (3, 1)]),
+        shift(shares[1], [(0, 1), (1, 0), (2, 3), (3, 2)]),
     )
 
 
@@ -1221,7 +1224,7 @@
         (*[qkv_weight] * 6, *[gate_up_weight] * 4, query_gain, key_gain, cond_table, mod_weight.T),
         (
             struct((width, wide), bf16),
-            struct((wide, packed), bf16),
+            struct((3 * span, wide), bf16),
             struct((3, tokens, LANES)),
             struct((8, LANES)),
             struct((width, units), bf16),
@@ -1252,18 +1255,18 @@
     d1, d2, cx, cy = split_round(xn, yn, half)
     pieces = (pay, xn, core, cx, yn, d1, d2, cy, swap(d1, 2), swap(d2, 2))
     c_core, c_xn, c_yn = first_round(low_cot)
-    att, hid, qkv, raw, turn, mod, logs, mixed = call(
+    att, hid, qkv, unit, turn, mod, logs, mixed = call(
         functools.partial(attend_kernel, blocks),
         (*pieces, spread, offsets, gains),
         (
-            struct((everyone, LANES * heads), bf16),
+            struct((blocks, span, tokens), bf16),
             struct((everyone, width), bf16),
             struct((3 * heads, everyone, LANES), bf16),
             struct((2 * heads, everyone, LANES)),
             struct((2, everyone, LANES)),
             struct((8, width)),
             struct((heads, everyone // (2 * tokens), 2 * tokens)),
-            struct((heads, everyone, LANES)),
+            struct((heads, LANES, everyone)),
         ),
         [
             pltpu.VMEM((everyone, width), bf16),
@@ -1272,16 +1275,22 @@
             pltpu.VMEM((1, 6 * width), jnp.float32),
             pltpu.VMEM((2, 8, LANES), jnp.float32),
             pltpu.VMEM((heads, LANES, everyone), bf16),
+            pltpu.VMEM((everyone, width), bf16),
+            pltpu.VMEM((3 * heads, everyone, LANES), bf16),
+            pltpu.VMEM((2 * heads, everyone, LANES), jnp.float32),
+            pltpu.VMEM((2, everyone, LANES), jnp.float32),
             pltpu.SemaphoreType.DMA((10,)),
             pltpu.SemaphoreType.DMA((blocks,)),
+            pltpu.SemaphoreType.DMA((4,)),
         ],
         where,
         "attend",
         15,
         {index: ANY for index in range(10)},
+        out_specs={index: ANY for index in range(1, 5)},
     )
     att, c_core, c_xn, c_yn = tie(att, c_core, c_xn, c_yn)
-    att_all = exchange(att.reshape(blocks, tokens, LANES * heads))
+    att_all = exchange(att)
     c_dn, c_cx, c_cy = second_round(c_xn, c_yn)
     mlp_steps = 4
     step_units = hidden_units // mlp_steps
@@ -1311,7 +1320,7 @@
             struct((tokens, hidden_units), bf16),
             struct((tokens, width)),
             struct((tokens, width), bf16),
-            struct((blocks, tokens, LANES * heads), bf16),
+            struct((blocks, span, tokens), bf16),
             struct((8, width)),
         ),
         [pltpu.VMEM((tokens, width), jnp.float32)],
@@ -1347,7 +1356,7 @@
     shares = call(
         mlp_weights_kernel,
         (*hid_pieces, *cot_pieces, own_gate, own_up, down_weight, down_weight, mod),
-        (struct((zrows, units), bf16),) * 5,
+        (struct((zrows, units), bf16),) * 4,
         [
             pltpu.VMEM((everyone, width), bf16),
             pltpu.VMEM((everyone, width), bf16),
@@ -1355,7 +1364,7 @@
             pltpu.VMEM((units, width), bf16),
             pltpu.VMEM((images, zrows, units), bf16),
             pltpu.SemaphoreType.DMA((2, blocks)),
-            pltpu.SemaphoreType.DMA((5,)),
+            pltpu.SemaphoreType.DMA((4,)),
         ],
         where,
         "mlp_weights",
@@ -1365,27 +1374,34 @@
             18: pl.BlockSpec((run, width), lambda i, s: (s[0], 0)),
             19: pl.BlockSpec((run, width), lambda i, s: (8 + s[0], 0)),
         },
-        out_specs={index: ANY for index in range(5)},
+        out_specs={index: ANY for index in range(4)},
     )
     attg_all, a_core, a_xn, a_yn, *shares = tie(attg_all, a_core, a_xn, a_yn, *shares)
-    way = line_first(shares)
+    way, mid = line_first(shares)
     a_dn, a_cx, a_cy = second_round(a_xn, a_yn)
     back, gain_sums = call(
         attend_back_kernel,
-        (attg_all.reshape(everyone, LANES * heads), qkv, raw, turn, logs, mixed, gains, order),
-        (struct((everyone, packed), bf16), struct((8, LANES))),
+        (attg_all, qkv, logs, mixed, gains, unit, turn, order),
+        (struct((blocks, 3 * span, tokens), bf16), struct((8, LANES))),
         [
             pltpu.VMEM((heads, LANES, everyone), bf16),
+            pltpu.VMEM((heads, everyone, LANES), bf16),
+            pltpu.VMEM((heads, LANES, everyone), bf16),
             pltpu.VMEM((3 * heads, everyone, LANES), jnp.float32),
+            pltpu.VMEM(unit.shape, jnp.float32),
+            pltpu.VMEM(turn.shape, jnp.float32),
+            pltpu.VMEM(order.shape, bf16),
+            pltpu.SemaphoreType.DMA((3,)),
         ],
+        specs={5: ANY, 6: ANY, 7: ANY},
         name="attend_back",
         micros=15,
     )
-    back, way, a_dn, a_cx, a_cy = tie(back, way, a_dn, a_cx, a_cy)
-    back_all = exchange(back.reshape(blocks, tokens, packed))
+    back, way, mid, a_dn, a_cx, a_cy = tie(back, way, mid, a_dn, a_cx, a_cy)
+    back_all = exchange(back)
     a_cd = swap(a_dn, 2)
     own_back, a_cd, way = tie(back, a_cd, way)
-    up, down = line_second(shares, way)
+    other, two, near = line_second(shares, way)
     grad_pieces = (attn_grad, a_xn, a_core, a_cx, a_yn, a_dn, a_cy, a_cd)
     (qkv_part,) = call(
         qkv_weights_kernel,
@@ -1404,8 +1420,7 @@
         "out_weights",
         specs={index: ANY for index in range(blocks)},
     )
-    back_all, outw_part, up, down = tie(back_all, outw_part, up, down)
-    up, down = line_third(shares, up, down)
+    back_all, outw_part = tie(back_all, outw_part)
     in_grad, send = call(
         input_kernel,
         (back_all, qkv_weight, x, middle_grad, mod, sums, gmid, gain_sums, bucket),
@@ -1420,9 +1435,26 @@
         specs={1: pl.BlockSpec((width, width), lambda s: (0, s)), 8: SMEM},
         grid=(3,),
     )
+    send, qkv_rows = tie(send, qkv_rows)
+    everywhere = exchange(send, ("img", "ty", "tx"))
+    joined = call(
+        join_kernel,
+        (qkv_rows, outw_part),
+        (struct((width // blocks, 4 * share), bf16),) * 4,
+        [
+            pltpu.VMEM((images, width // blocks, 4 * share), bf16),
+            pltpu.SemaphoreType.DMA((4,)),
+        ],
+        where,
+        "join",
+        out_specs={index: ANY for index in range(4)},
+    )
+    way, j_mid = line_first(joined)
+    other, way, j_mid = tie(other, way, j_mid)
+    j_other, j_two, j_near = line_second(joined, way)
     send_gateup, first, second = call(
         turn_kernel,
-        (shares[0], up, down),
+        (shares[0], mid, near, two, other),
         (
             struct((blocks, width // blocks, run), bf16),
             struct((share, run), bf16),
@@ -1431,23 +1463,6 @@
         scalars=where,
         name="turn",
     )
-    joined = call(
-        join_kernel,
-        (qkv_rows, outw_part),
-        (struct((width // blocks, 4 * share), bf16),) * 5,
-        [
-            pltpu.VMEM((images, width // blocks, 4 * share), bf16),
-            pltpu.SemaphoreType.DMA((5,)),
-        ],
-        where,
-        "join",
-        out_specs={index: ANY for index in range(5)},
-    )
-    way = line_first(joined)
-    send, joined = tie(send, joined)
-    everywhere = exchange(send, ("img", "ty", "tx"))
-    everywhere, way, send_gateup = tie(everywhere, way, send_gateup)
-    up, down = line_second(joined, way)
     modw_total, modb_total, qgain_total, kgain_total, act_send, condition, buckets = call(
         tail_kernel,
         (everywhere, table_share, modw_share),
@@ -1464,8 +1479,7 @@
         name="tail",
     )
     act_parts = exchange(act_send)
-    act_parts, up, down = tie(act_parts, up, down)
-    up, down = line_third(joined, up, down)
+    act_parts, send_gateup = tie(act_parts, send_gateup)
     gateup_rows = exchange(send_gateup)
     first = lax.ppermute(first, PLANE, [(t, t // 2 + 4 * (t % 2)) for t in range(8)])
     second = lax.ppermute(second, PLANE, [(t, t // 2 + 4 * (1 - t % 2)) for t in range(8)])
@@ -1476,18 +1490,18 @@
         scalars=where,
         name="table",
     )
-    gateup_total, down_total = call(
+    gateup_rows, table_total, j_other = tie(gateup_rows, table_total, j_other)
+    gateup_total, down_total, qkv_total, outw_total = call(
         lay_kernel,
-        (gateup_rows, first, second),
-        (struct((width // blocks, blocks * run)), struct((share, units))),
+        (gateup_rows, first, second, joined[0], j_mid, j_near, j_two, j_other),
+        (
+            struct((width // blocks, blocks * run)),
+            struct((share, units)),
+            struct((width // blocks, 3 * share)),
+            struct((width // blocks, share)),
+        ),
         scalars=where,
         name="lay",
-    )
-    qkv_total, outw_total = call(
-        finish_kernel,
-        (joined[0], up, down),
-        (struct((width // blocks, 3 * share)), struct((width // blocks, share))),
-        name="finish",
     )
     return (
         output.reshape(block_in.shape),

time: 234 us -> 224 us (0.957); the launches traced: 233 us -> 220 us
  Pallas kernels: 124 us -> 115 us
  waiting for transfers between devices: 19.5 us -> 23.7 us
  starting transfers between devices: 74.9 us -> 71.1 us
  other arithmetic: 3.41 us -> 0.91 us
    pallas_call x18 -> x17, Pallas kernels: 124 us -> 115 us  [call(): pl.pallas_call(kernel, out_shape=outs, grid_spec=pltpu.PrefetchScalarGrid...]
    ppermute x10, starting transfers between devices: 27.8 us -> 22.1 us  [shift(): return lax.ppermute(value, 'img', pairs)]
    ppermute x10, waiting for transfers between devices: 0.03 us -> 3.65 us  [shift(): return lax.ppermute(value, 'img', pairs)]
    ppermute x1, waiting for transfers between devices: 0.01 us -> 2.71 us  [on_plane(): lax.ppermute(second, PLANE, [(t, t // 2 + 4 * (1 - t % 2)) for t in range...]
    convert_element_type x6 -> x2, other arithmetic: 2.76 us -> 0.25 us  [add(): (left.astype(jnp.float32) + right.astype(jnp.float32)).astype(jnp.bfloat16)]
    unnamed x106 -> x90, local copies, waits for them, and re-layouts: 9.12 us -> 7.31 us
  transfers between devices with their start and end apart: 49 -> 49, of which waited for: 8 -> 9; matrix products, arithmetic and copies ran while one was open for 1% -> 0% of each run, Pallas kernels for 49% -> 47%
where the time goes in v3:
time: 224 us; the launch traced here: 220 us
  Pallas kernels  115 us (51%)
  starting transfers between devices  71.1 us (32%)
  waiting for transfers between devices  23.7 us (11%)
  local copies, waits for them, and re-layouts  7.33 us (3%)
    pallas_call x17, Pallas kernels, call(): pl.pallas_call(kernel, out_shape=outs, grid_spec=pltpu.PrefetchScalarGrid...  115 us
    all_to_all x7, starting transfers between devices, exchange(): return lax.all_to_all(value, axes, split_axis=0, concat_axis=0, tiled=True)  27.1 us
    ppermute x10, starting transfers between devices, shift(): return lax.ppermute(value, 'img', pairs)  22.1 us
    ppermute x30, starting transfers between devices, swap(): lax.ppermute(value, PLANE, [(index, index ^ bit) for index in range(8)])  17.9 us
    all_to_all x7, waiting for transfers between devices, exchange(): return lax.all_to_all(value, axes, split_axis=0, concat_axis=0, tiled=True)  8.85 us
    ppermute x30, waiting for transfers between devices, swap(): lax.ppermute(value, PLANE, [(index, index ^ bit) for index in range(8)])  8.47 us
    unnamed x90, local copies, waits for them, and re-layouts  7.31 us
  transfers between devices with their start and end apart: 49, of which 9 were waited for; matrix products, arithmetic and copies ran while one was open for 0% of the time, Pallas kernels for 47%

profile of v3, /device:TPU:0, one launch (start us, length us, event | category | flops | bytes accessed | tf_op | source)
XLA Modules:
  0.0 220.4 jit_solution(4750453093319033756)
XLA Ops:
  1.3 3.5 %open.1 = (bf16[144,1152]{1,0:T(8,128)(2,1)}, bf16[128,1152]{1,0:T(8,128)(2,1)}) custom-call(s32[1]{0:T(128)S(6)} %copy.24.bucket_ref, s32[2]{0:T(128)} %bitcast.18, f32[128,1152]{1,0:T(8,128)} %bitcast.15, f32[32,1152]{1,0:T(8,128)} %refs_12_.1, bf16[864,1152]{1,0:T(8,128)(2,1)} %bitcast.9, f32[864]{0:T(1024)} %bias_ref.1, f32[128,1152]{1,0:T(8,128)} %bitcast.11), custom_call_target="tpu_custom_call" | custom-call | flops 5000000000 | bytes 5000000 | tf_op jit(solution)/shard_map/open/pallas_call | solution.py:1097
  4.8 2.9 %collective-permute-start = (bf16[144,1152]{1,0:T(8,128)(2,1)}, bf16[144,1152]{1,0:T(8,128)(2,1)S(1)}, u32[]{:S(2)}, u32[]{:S(2)}) collective-permute-start(bf16[144,1152]{1,0:T(8,128)(2,1)} %get-tuple-element.121.refs_0_), channel_id=1, source_target_pairs={{0,1},{1,0},{2,3},{3,2},{4,5},{5,4},{6,7},{7,6},{8,9},{9,8},{10,11... | collective-permute-start | bytes 995336 | tf_op jit(solution)/shard_map/ppermute | solution.py:1126
  7.7 1.5 collective-permute-start.1
  9.9 8.9 %ready.1 = (bf16[1152,768]{1,0:T(8,128)(2,1)}, bf16[432,768]{1,0:T(8,128)(2,1)}, f32[3,128,128]{2,1,0:T(8,128)}, f32[8,128]{1,0:T(8,128)}, bf16[1152,384]{1,0:T(...) custom-call(s32[2]{0:T(128)} %pad_add_fusion.scalars, ...), custom_call_target="tpu_custom_call" | custom-call | flops 5000000000 | bytes 5000000 | tf_op jit(solution)/shard_map/ready/pallas_call | solution.py:1097
  20.2 4.5 %collective-permute-done.5.refs_6_ = bf16[80,1152]{1,0:T(8,128)(2,1)S(1)} collective-permute-done((bf16[80,1152]{1,0:T(8,128)(2,1)S(1)}, bf16[80,1152]{1,0:T(8,128)(2,1)S(1)}, u32[]{:S(2)}, u32[]{:S(2)}) %collective-permute-start.5) | collective-permute-done | bytes 184352 | tf_op jit(solution)/shard_map/ppermute | solution.py:1126
  24.7 1.6 collective-permute-done.4.refs_5_
  26.3 1.5 collective-permute-start.10
  29.9 12.8 %attend.1 = (bf16[8,144,128]{2,1,0:T(8,128)(2,1)}, bf16[1024,1152]{1,0:T(8,128)(2,1)}, bf16[6,1024,128]{2,1,0:T(8,128)(2,1)}, f32[4,1024,128]{2,1,0:T(8,128)}, f...) custom-call(s32[2]{0:T(128)} %pad_add_fusion.scalars, ...), custom_call_target="tpu_custom_call" | custom-call | flops 15000000512 | bytes 15000000 | tf_op jit(solution)/shard_map/attend/pallas_call | solution.py:1097
  42.7 1.6 collective-permute-start.12
  44.8 3.6 %all-to-all-start = ((bf16[8,144,128]{2,1,0:T(8,128)(2,1)}), bf16[8,144,128]{2,1,0:T(8,128)(2,1)S(1)}, u32[]{:S(2)}, u32[]{:S(2)}) async-start(bf16[8,144,128]{2,1,0:T(8,128)(2,1)} %get-tuple-element.186.refs_8_), calls=%async_computation | async-start | bytes 589824 | tf_op jit(solution)/shard_map/all_to_all | solution.py:1149
  48.4 6.1 %act_grad.1.agrad_in = f32[128,3072]{1,0:T(8,128)} custom-call(bf16[3072,1152]{1,0:T(8,128)(2,1)} %refs_19_.1, f32[128,1152]{1,0:T(8,128)} %bitcast.12, f32[8,1152]{1,0:T(8,128)} %get-tuple-element.138.mod_ref.refs_20_), custom_call_target="tpu_custom_call" | custom-call | flops 5000000000 | bytes 5000000 | tf_op jit(solution)/shard_map/act_grad/pallas_call | solution.py:1097
  56.1 3.8 %middle.1 = (f32[128,1152]{1,0:T(8,128)}, f32[128,1152]{1,0:T(8,128)}, bf16[128,1152]{1,0:T(8,128)(2,1)}) custom-call(bf16[8,144,128]{2,1,0:T(8,128)(2,1)} %copy-done.6, bf16[1152,1152]{1,0:T(8,128)(2,1)} %outw_ref.1, f32[128,1152]{1,0:T(8,128)} %bitcast.16, f32[8,1152]{1,0:T(8,128)} %get-tuple-element.138.mod_ref.refs_20_), custom_call_target="tpu_custom_call" | custom-call | flops 5000000000 | bytes 5000000 | tf_op jit(solution)/shard_map/middle/pallas_call | solution.py:1097
  59.9 1.5 collective-permute-start.16
  61.4 1.5 collective-permute-start.17
  62.9 13.8 %mlp.1 = (bf16[128,3072]{1,0:T(8,128)(2,1)}, f32[128,1152]{1,0:T(8,128)}, bf16[128,1152]{1,0:T(8,128)(2,1)}, bf16[8,144,128]{2,1,0:T(8,128)(2,1)}, f32[8,1152]{1,0:T(8,128)}) custom-call(bf16[1152,6144]{1,0:T(8,128)(2,1)} %up_ref.1, bf16[1152,6144]{1,0:T(8,128)(2,1)} %up_ref.1, bf16[1152,1152]{1,0:T(8,128)(2,1)} %outw_ref.1, ...), custom_call_target="tpu_custom_call" | custom-call | flops 12000000000 | bytes 12000000 | tf_op jit(solution)/shard_map/mlp/pallas_call | solution.py:1097
  77.9 6.2 %mlp_out.1 = (f32[128,1152]{1,0:T(8,128)}, f32[8,1152]{1,0:T(8,128)}) custom-call(bf16[128,3072]{1,0:T(8,128)(2,1)} %get-tuple-element.144.act_ref, bf16[3072,1152]{1,0:T(8,128)(2,1)} %refs_19_.1, f32[128,1152]{1,0:T(8,128)} %get-tuple-element.141.mid_ref, f32[128,1152]{1,0:T(8,128)} %bitcast.14, f32[8,1152]{1,0:T(8,128)} %get-tuple-element.138.mod_ref.refs_20_), custom_call_target="tpu_custom_call" | custom-call | flops 5000000000 | bytes 5000000 | tf_op jit(solution)/shard_map/mlp_out/pallas_call | solution.py:1097
  84.2 2.3 %collective-permute-done.21.refs_5_ = bf16[128,1152]{1,0:T(8,128)(2,1)} collective-permute-done((bf16[128,1152]{1,0:T(8,128)(2,1)S(1)}, bf16[128,1152]{1,0:T(8,128)(2,1)}, u32[]{:S(2)}, u32[]{:S(2)}) %collective-permute-start.21) | collective-permute-done | bytes 294944 | tf_op jit(solution)/shard_map/ppermute | solution.py:1126
  88.4 3.6 %all-to-all-start.1 = ((bf16[8,144,128]{2,1,0:T(8,128)(2,1)}), bf16[8,144,128]{2,1,0:T(8,128)(2,1)S(1)}, u32[]{:S(2)}, u32[]{:S(2)}) async-start(bf16[8,144,128]{2,1,0:T(8,128)(2,1)} %get-tuple-element.147), calls=%async_computation.1 | async-start | bytes 589824 | tf_op jit(solution)/shard_map/all_to_all | solution.py:1149
  93.5 13.6 %mlp_weights.1 = (bf16[864,384]{1,0:T(8,128)(2,1)}, bf16[864,384]{1,0:T(8,128)(2,1)}, bf16[864,384]{1,0:T(8,128)(2,1)}, bf16[864,384]{1,0:T(8,128)(2,1)}) custom-call(s32[2]{0:T(128)} %pad_add_fusion.scalars, bf16[128,1152]{1,0:T(8,128)(2,1)} %get-tuple-element.140.hid_ref.refs_0_, bf16[128,1152]{1,0:T(8,128)(2,1)} %copy-done.32, ...), custom_call_target="tpu_custom_call" | custom-call | flops 12000000000 | bytes 12000000 | tf_op jit(solution)/shard_map/mlp_weights/pallas_call | solution.py:1097
  107.9 3.7 %collective-permute-start.26 = (bf16[864,384]{1,0:T(8,128)(2,1)}, bf16[864,384]{1,0:T(8,128)(2,1)S(1)}, u32[]{:S(2)}, u32[]{:S(2)}) collective-permute-start(bf16[864,384]{1,0:T(8,128)(2,1)} %get-tuple-element.174), channel_id=1, source_target_pairs={{0,8},{24,16},{1,9},{25,17},{2,10},{26,18},{3,11},{27,19},{4,12},{... | collective-permute-start | bytes 1990664 | tf_op jit(solution)/shard_map/ppermute | solution.py:1153
  111.6 0.9 collective-permute-start.27
  112.6 2.1 collective-permute-start.28
  115.2 12.7 %attend_back.1 = (bf16[8,432,128]{2,1,0:T(8,128)(2,1)}, f32[8,128]{1,0:T(8,128)}) custom-call(bf16[8,144,128]{2,1,0:T(8,128)(2,1)} %copy-done.5, bf16[6,1024,128]{2,1,0:T(8,128)(2,1)} %get-tuple-element.167.qkv_ref, f32[2,4,256]{2,1,0:T(4,128)} %get-tuple-element.168.log_ref, f32[2,128,1024]{2,1,0:T(8,128)} %get-tuple-element.169.mixed_ref, ...), custom_call_target="tpu_custom_call" | custom-call | flops 15000000512 | bytes 15000000 | tf_op jit(solution)/shard_map/attend_back/pallas_call | solution.py:1097
  128.8 3.6 %all-to-all-start.2 = ((bf16[8,432,128]{2,1,0:T(8,128)(2,1)}), bf16[8,432,128]{2,1,0:T(8,128)(2,1)S(1)}, u32[]{:S(2)}, u32[]{:S(2)}) async-start(bf16[8,432,128]{2,1,0:T(8,128)(2,1)} %get-tuple-element.185.back_ref), calls=%async_computation.2 | async-start | bytes 1769472 | tf_op jit(solution)/shard_map/all_to_all | solution.py:1149
  132.4 2.8 %collective-permute-start.32 = (bf16[864,384]{1,0:T(8,128)(2,1)}, bf16[864,384]{1,0:T(8,128)(2,1)}, u32[]{:S(2)}, u32[]{:S(2)}) collective-permute-start(bf16[864,384]{1,0:T(8,128)(2,1)} %get-tuple-element.201), channel_id=1, source_target_pairs={{0,8},{8,0},{16,24},{24,16},{1,9},{9,1},{17,25},{25,17},{2,10},{10... | collective-permute-start | bytes 1990664 | tf_op jit(solution)/shard_map/ppermute | solution.py:1153
  135.1 3.8 %collective-permute-start.33 = (bf16[864,384]{1,0:T(8,128)(2,1)S(1)}, bf16[864,384]{1,0:T(8,128)(2,1)}, u32[]{:S(2)}, u32[]{:S(2)}) collective-permute-start(bf16[864,384]{1,0:T(8,128)(2,1)S(1)} %copy-done.2), channel_id=1, source_target_pairs={{0,16},{24,8},{1,17},{25,9},{2,18},{26,10},{3,19},{27,11},{4,20},{... | collective-permute-start | bytes 1990664 | tf_op jit(solution)/shard_map/ppermute | solution.py:1153
  139.0 4.5 %qkv_weights.1 = bf16[8,144,512]{2,1,0:T(8,128)(2,1)} custom-call(bf16[1024,1152]{1,0:T(8,128)(2,1)} %get-tuple-element.184.hid_ref, bf16[8,432,128]{2,1,0:T(8,128)(2,1)} %get-tuple-element.185.back_ref), custom_call_target="tpu_custom_call" | custom-call | flops 5000000000 | bytes 5000000 | tf_op jit(solution)/shard_map/qkv_weights/pallas_call | solution.py:1097
  143.6 1.3 collective-permute-start.34
  145.5 3.6 %all-to-all-start.3 = ((bf16[8,144,512]{2,1,0:T(8,128)(2,1)}), bf16[8,144,512]{2,1,0:T(8,128)(2,1)S(1)}, u32[]{:S(2)}, u32[]{:S(2)}) async-start(bf16[8,144,512]{2,1,0:T(8,128)(2,1)} %qkv_weights.1), calls=%async_computation.3 | async-start | bytes 2359296 | tf_op jit(solution)/shard_map/all_to_all | solution.py:1149
  149.1 4.7 %out_weights.1.ograd_ref = bf16[4,144,288]{2,1,0:T(8,128)(2,1)} custom-call(s32[2]{0:T(128)} %pad_add_fusion.scalars, bf16[128,1152]{1,0:T(8,128)(2,1)} %get-tuple-element.148.refs_0_, bf16[128,1152]{1,0:T(8,128)(2,1)} %copy-done.26, bf16[128,1152]{1,0:T(8,128)(2,1)} %copy-done.25, bf16[128,1152]{1,0:T(8,128)(2,1)} %collective-permute-done.29.refs_3_, ...), custom_call_target="tpu_custom_call" | custom-call | flops 5000000000 | bytes 5000000 | tf_op jit(solution)/shard_map/out_weights/pallas_call | solution.py:1097
  153.8 7.1 %input.1 = (f32[128,1152]{1,0:T(8,128)}, f32[32,8,128]{2,1,0:T(8,128)}) custom-call(bf16[8,432,128]{2,1,0:T(8,128)(2,1)} %copy-done.1, bf16[1152,3456]{1,0:T(8,128)(2,1)} %weight_ref.3, f32[128,1152]{1,0:T(8,128)} %bitcast.17, f32[128,1152]{1,0:T(8,128)} %get-tuple-element.188.mgrad_ref, f32[8,1152]{1,0:T(8,128)} %get-tuple-element.138.mod_ref.refs_20_, ...), custom_call_target="tpu_custom_call" | custom-call | flops 7000000000 | bytes 7000000 | tf_op jit(solution)/shard_map/input/pallas_call | solution.py:1097
  160.9 4.6 %all-to-all-done.3.grad_ref = bf16[8,144,512]{2,1,0:T(8,128)(2,1)S(1)} async-done(((bf16[8,144,512]{2,1,0:T(8,128)(2,1)}), bf16[8,144,512]{2,1,0:T(8,128)(2,1)S(1)}, u32[]{:S(2)}, u32[]{:S(2)}) %all-to-all-start.3) | async-done | bytes 1179680 | tf_op jit(solution)/shard_map/all_to_all | solution.py:1149
  165.5 5.2 %all-to-all-start.4 = ((f32[32,8,128]{2,1,0:T(8,128)}), f32[32,8,128]{2,1,0:T(8,128)S(1)}, u32[]{:S(2)}, u32[]{:S(2)}) async-start(f32[32,8,128]{2,1,0:T(8,128)} %get-tuple-element.195), calls=%async_computation.4 | async-start | bytes 262144 | tf_op jit(solution)/shard_map/all_to_all | solution.py:1149
  170.6 3.9 %join.1 = (bf16[144,1152]{1,0:T(8,128)(2,1)}, bf16[144,1152]{1,0:T(8,128)(2,1)}, bf16[144,1152]{1,0:T(8,128)(2,1)}, bf16[144,1152]{1,0:T(8,128)(2,1)}) custom-call(s32[2]{0:T(128)} %pad_add_fusion.scalars, bf16[8,144,512]{2,1,0:T(8,128)(2,1)} %copy-done, bf16[4,144,288]{2,1,0:T(8,128)(2,1)} %out_weights.1.ograd_ref), custom_call_target="tpu_custom_call" | custom-call | flops 5000000000 | bytes 5000000 | tf_op jit(solution)/shard_map/join/pallas_call | solution.py:1097
  174.5 3.7 %collective-permute-start.35 = (bf16[144,1152]{1,0:T(8,128)(2,1)}, bf16[144,1152]{1,0:T(8,128)(2,1)S(1)}, u32[]{:S(2)}, u32[]{:S(2)}) collective-permute-start(bf16[144,1152]{1,0:T(8,128)(2,1)} %get-tuple-element.206), channel_id=1, source_target_pairs={{0,8},{24,16},{1,9},{25,17},{2,10},{26,18},{3,11},{27,19},{4,12},{... | collective-permute-start | bytes 995336 | tf_op jit(solution)/shard_map/ppermute | solution.py:1153
  178.9 2.9 %all-to-all-done.4.got_ref = f32[32,8,128]{2,1,0:T(8,128)S(1)} async-done(((f32[32,8,128]{2,1,0:T(8,128)}), f32[32,8,128]{2,1,0:T(8,128)S(1)}, u32[]{:S(2)}, u32[]{:S(2)}) %all-to-all-start.4) | async-done | bytes 131104 | tf_op jit(solution)/shard_map/all_to_all | solution.py:1149
  182.5 3.5 %tail.1 = (f32[288,864]{1,0:T(8,128)}, f32[864]{0:T(1024)}, f32[72]{0:T(128)}, f32[72]{0:T(128)}, f32[8,8,288]{2,1,0:T(8,128)}, /*index=5*/f32[8,288]{1,0:T(8,128)}, f32[8,128]{1,0:T(8,128)}) custom-call(f32[32,8,128]{2,1,0:T(8,128)} %copy-done.7, f32[32,288]{1,0:T(8,128)} %get-tuple-element.196.table_ref, bf16[864,288]{1,0:T(8,128)(2,1)} %get-tuple-element.197.weight_ref), custom_call_target="tpu_custom_call" | custom-call | flops 5000000000 | bytes 5000000 | tf_op jit(solution)/shard_map/tail/pallas_call | solution.py:1097
  186.1 3.4 %all-to-all-start.5 = ((f32[8,8,288]{2,1,0:T(8,128)}), f32[8,8,288]{2,1,0:T(8,128)S(1)}, u32[]{:S(2)}, u32[]{:S(2)}) async-start(f32[8,8,288]{2,1,0:T(8,128)} %get-tuple-element.198), calls=%async_computation.5 | async-start | bytes 196608 | tf_op jit(solution)/shard_map/all_to_all | solution.py:1149
  190.2 3.1 %collective-permute-start.41 = (bf16[144,1152]{1,0:T(8,128)(2,1)S(1)}, bf16[144,1152]{1,0:T(8,128)(2,1)S(1)}, u32[]{:S(2)}, u32[]{:S(2)}) collective-permute-start(bf16[144,1152]{1,0:T(8,128)(2,1)S(1)} %copy-done.4), channel_id=1, source_target_pairs={{0,16},{24,8},{1,17},{25,9},{2,18},{26,10},{3,19},{27,11},{4,20},{... | collective-permute-start | bytes 995336 | tf_op jit(solution)/shard_map/ppermute | solution.py:1153
  193.4 1.3 collective-permute-start.37
  194.8 4.2 %turn.1 = (bf16[8,144,192]{2,1,0:T(8,128)(2,1)}, bf16[288,192]{1,0:T(8,128)(2,1)}, bf16[288,192]{1,0:T(8,128)(2,1)}) custom-call(s32[2]{0:T(128)} %pad_add_fusion.scalars, bf16[864,384]{1,0:T(8,128)(2,1)} %get-tuple-element.199.refs_0_, bf16[864,384]{1,0:T(8,128)(2,1)} %copy-done.11, bf16[864,384]{1,0:T(8,128)(2,1)} %collective-permute-done.32.refs_2_, ...), custom_call_target="tpu_custom_call" | custom-call | flops 5000000000 | bytes 5000000 | tf_op jit(solution)/shard_map/turn/pallas_call | solution.py:1097
  198.9 4.1 %all-to-all-start.6 = ((bf16[8,144,192]{2,1,0:T(8,128)(2,1)}), bf16[8,144,192]{2,1,0:T(8,128)(2,1)S(1)}, u32[]{:S(2)}, u32[]{:S(2)}) async-start(bf16[8,144,192]{2,1,0:T(8,128)(2,1)} %get-tuple-element.209), calls=%async_computation.6 | async-start | bytes 1179648 | tf_op jit(solution)/shard_map/all_to_all | solution.py:1149
  203.1 1.6 collective-permute-start.38
  204.6 2.5 %collective-permute-start.39 = (bf16[288,192]{1,0:T(8,128)(2,1)}, bf16[288,192]{1,0:T(8,128)(2,1)S(1)}, u32[]{:S(2)}, u32[]{:S(2)}) collective-permute-start(bf16[288,192]{1,0:T(8,128)(2,1)} %get-tuple-element.220), channel_id=1, source_target_pairs={{0,4},{1,0},{2,5},{3,1},{4,6},{5,2},{6,7},{7,3},{8,12},{9,8},{10,1... | collective-permute-start | bytes 331784 | tf_op jit(solution)/shard_map/ppermute | solution.py:1485
  207.2 2.2 %table.1 = f32[4,288]{1,0:T(4,128)} custom-call(s32[2]{0:T(128)} %pad_add_fusion.scalars, f32[8,8,288]{2,1,0:T(8,128)} %copy-done.9, f32[8,288]{1,0:T(8,128)} %get-tuple-element.211.cond_ref, f32[8,128]{1,0:T(8,128)} %get-tuple-element.212.bucket_ref), custom_call_target="tpu_custom_call" | custom-call | flops 5000000000 | bytes 5000000 | tf_op jit(solution)/shard_map/table/pallas_call | solution.py:1097
  209.4 3.6 %collective-permute-done.37.refs_4_ = bf16[144,1152]{1,0:T(8,128)(2,1)} collective-permute-done((bf16[144,1152]{1,0:T(8,128)(2,1)S(1)}, bf16[144,1152]{1,0:T(8,128)(2,1)}, u32[]{:S(2)}, u32[]{:S(2)}) %collective-permute-start.37) | collective-permute-done | bytes 331808 | tf_op jit(solution)/shard_map/ppermute | solution.py:1153
  213.1 2.7 %collective-permute-done.39.second_ref = bf16[288,192]{1,0:T(8,128)(2,1)S(1)} collective-permute-done((bf16[288,192]{1,0:T(8,128)(2,1)}, bf16[288,192]{1,0:T(8,128)(2,1)S(1)}, u32[]{:S(2)}, u32[]{:S(2)}) %collective-permute-start.39) | collective-permute-done | bytes 110624 | tf_op jit(solution)/shard_map/ppermute | solution.py:1485
  216.5 3.9 %lay.1 = (f32[144,1536]{1,0:T(8,128)}, f32[288,384]{1,0:T(8,128)}, f32[144,864]{1,0:T(8,128)}, f32[144,288]{1,0:T(8,128)}) custom-call(s32[2]{0:T(128)} %pad_add_fusion.scalars, bf16[8,144,192]{2,1,0:T(8,128)(2,1)} %copy-done.3, bf16[288,192]{1,0:T(8,128)(2,1)} %copy-done.43, bf16[288,192]{1,0:T(8,128)(2,1)} %copy-done.44, ...), custom_call_target="tpu_custom_call" | custom-call | flops 5000000000 | bytes 5000000 | tf_op jit(solution)/shard_map/lay/pallas_call | solution.py:1097
  (162 shorter events, 16.3 us)
Async XLA Ops:
  4.8 14.0 %collective-permute-start = (bf16[144,1152]{1,0:T(8,128)(2,1)}, bf16[144,1152]{1,0:T(8,128)(2,1)S(1)}, u32[]{:S(2)}, u32[]{:S(2)}) collective-permute-start(bf16[144,1152]{1,0:T(8,128)(2,1)} %get-tuple-element.121.refs_0_), channel_id=1, source_target_pairs={{0,1},{1,0},{2,3},{3,2},{4,5},{5,4},{6,7},{7,6},{8,9},{9,8},{10,11... | collective-permute-start | bytes 995336 | tf_op jit(solution)/shard_map/ppermute | solution.py:1126
  7.7 11.1 %collective-permute-start.1 = (bf16[144,1152]{1,0:T(8,128)(2,1)}, bf16[144,1152]{1,0:T(8,128)(2,1)S(1)}, u32[]{:S(2)}, u32[]{:S(2)}) collective-permute-start(bf16[144,1152]{1,0:T(8,128)(2,1)} %get-tuple-element.121.refs_0_), channel_id=1, source_target_pairs={{0,4},{1,5},{2,6},{3,7},{4,0},{5,1},{6,2},{7,3},{8,12},{9,13},{10,... | collective-permute-start | bytes 995336 | tf_op jit(solution)/shard_map/ppermute | solution.py:1126
  18.8 5.9 %collective-permute-start.5 = (bf16[80,1152]{1,0:T(8,128)(2,1)S(1)}, bf16[80,1152]{1,0:T(8,128)(2,1)S(1)}, u32[]{:S(2)}, u32[]{:S(2)}) collective-permute-start(bf16[80,1152]{1,0:T(8,128)(2,1)S(1)} %slice.7), channel_id=1, source_target_pairs={{0,1},{1,0},{2,3},{3,2},{4,5},{5,4},{6,7},{7,6},{8,9},{9,8},{10,11... | collective-permute-start | bytes 552968 | tf_op jit(solution)/shard_map/ppermute | solution.py:1126
  19.4 6.9 %collective-permute-start.2 = (bf16[144,1152]{1,0:T(8,128)(2,1)S(1)}, bf16[144,1152]{1,0:T(8,128)(2,1)S(1)}, u32[]{:S(2)}, u32[]{:S(2)}) collective-permute-start(bf16[144,1152]{1,0:T(8,128)(2,1)S(1)} %copy-done.12), channel_id=1, source_target_pairs={{0,2},{1,3},{2,0},{3,1},{4,6},{5,7},{6,4},{7,5},{8,10},{9,11},{10,... | collective-permute-start | bytes 995336 | tf_op jit(solution)/shard_map/ppermute | solution.py:1126
  19.5 8.9 %collective-permute-start.3 = (bf16[144,1152]{1,0:T(8,128)(2,1)S(1)}, bf16[144,1152]{1,0:T(8,128)(2,1)S(1)}, u32[]{:S(2)}, u32[]{:S(2)}) collective-permute-start(bf16[144,1152]{1,0:T(8,128)(2,1)S(1)} %collective-permute-done.refs_1_), channel_id=1, source_target_pairs={{0,2},{1,3},{2,0},{3,1},{4,6},{5,7},{6,4},{7,5},{8,10},{9,11},{10,... | collective-permute-start | bytes 995336 | tf_op jit(solution)/shard_map/ppermute | solution.py:1126
  20.0 8.4 %collective-permute-start.6 = (bf16[144,1152]{1,0:T(8,128)(2,1)S(1)}, bf16[144,1152]{1,0:T(8,128)(2,1)S(1)}, u32[]{:S(2)}, u32[]{:S(2)}) collective-permute-start(bf16[144,1152]{1,0:T(8,128)(2,1)S(1)} %collective-permute-done.1.refs_4_), channel_id=1, source_target_pairs={{0,2},{1,3},{2,0},{3,1},{4,6},{5,7},{6,4},{7,5},{8,10},{9,11},{10,... | collective-permute-start | bytes 995336 | tf_op jit(solution)/shard_map/ppermute | solution.py:1126
  20.0 6.3 %collective-permute-start.4 = (bf16[64,1152]{1,0:T(8,128)(2,1)S(1)}, bf16[64,1152]{1,0:T(8,128)(2,1)S(1)}, u32[]{:S(2)}, u32[]{:S(2)}) collective-permute-start(bf16[64,1152]{1,0:T(8,128)(2,1)S(1)} %slice.6), channel_id=1, source_target_pairs={{0,4},{1,5},{2,6},{3,7},{4,0},{5,1},{6,2},{7,3},{8,12},{9,13},{10,... | collective-permute-start | bytes 442376 | tf_op jit(solution)/shard_map/ppermute | solution.py:1126
  24.7 3.7 %collective-permute-start.8 = (bf16[80,1152]{1,0:T(8,128)(2,1)S(1)}, bf16[80,1152]{1,0:T(8,128)(2,1)S(1)}, u32[]{:S(2)}, u32[]{:S(2)}) collective-permute-start(bf16[80,1152]{1,0:T(8,128)(2,1)S(1)} %collective-permute-done.5.refs_6_), channel_id=1, source_target_pairs={{0,2},{1,3},{2,0},{3,1},{4,6},{5,7},{6,4},{7,5},{8,10},{9,11},{10,... | collective-permute-start | bytes 552968 | tf_op jit(solution)/shard_map/ppermute | solution.py:1126
  26.3 16.3 %collective-permute-start.10 = (bf16[128,1152]{1,0:T(8,128)(2,1)S(1)}, bf16[128,1152]{1,0:T(8,128)(2,1)S(1)}, u32[]{:S(2)}, u32[]{:S(2)}) collective-permute-start(bf16[128,1152]{1,0:T(8,128)(2,1)S(1)} %copy-done.20), channel_id=1, source_target_pairs={{0,1},{1,0},{2,3},{3,2},{4,5},{5,4},{6,7},{7,6},{8,9},{9,8},{10,11... | collective-permute-start | bytes 884744 | tf_op jit(solution)/shard_map/ppermute | solution.py:1126
  27.9 14.8 %collective-permute-start.11 = (bf16[128,1152]{1,0:T(8,128)(2,1)S(1)}, bf16[128,1152]{1,0:T(8,128)(2,1)S(1)}, u32[]{:S(2)}, u32[]{:S(2)}) collective-permute-start(bf16[128,1152]{1,0:T(8,128)(2,1)S(1)} %copy-done.20), channel_id=1, source_target_pairs={{0,4},{1,5},{2,6},{3,7},{4,0},{5,1},{6,2},{7,3},{8,12},{9,13},{10,... | collective-permute-start | bytes 884744 | tf_op jit(solution)/shard_map/ppermute | solution.py:1126
  28.4 14.3 %collective-permute-start.9 = (bf16[128,1152]{1,0:T(8,128)(2,1)S(1)}, bf16[128,1152]{1,0:T(8,128)(2,1)S(1)}, u32[]{:S(2)}, u32[]{:S(2)}) collective-permute-start(bf16[128,1152]{1,0:T(8,128)(2,1)S(1)} %copy-done.20), channel_id=1, source_target_pairs={{0,2},{1,3},{2,0},{3,1},{4,6},{5,7},{6,4},{7,5},{8,10},{9,11},{10,... | collective-permute-start | bytes 884744 | tf_op jit(solution)/shard_map/ppermute | solution.py:1126
  42.7 12.6 %collective-permute-start.12 = (bf16[128,1152]{1,0:T(8,128)(2,1)S(1)}, bf16[128,1152]{1,0:T(8,128)(2,1)S(1)}, u32[]{:S(2)}, u32[]{:S(2)}) collective-permute-start(bf16[128,1152]{1,0:T(8,128)(2,1)S(1)} %collective-permute-done.10.refs_9_), channel_id=1, source_target_pairs={{0,4},{1,5},{2,6},{3,7},{4,0},{5,1},{6,2},{7,3},{8,12},{9,13},{10,... | collective-permute-start | bytes 884744 | tf_op jit(solution)/shard_map/ppermute | solution.py:1126
  44.3 11.0 %collective-permute-start.13 = (bf16[128,1152]{1,0:T(8,128)(2,1)S(1)}, bf16[128,1152]{1,0:T(8,128)(2,1)S(1)}, u32[]{:S(2)}, u32[]{:S(2)}) collective-permute-start(bf16[128,1152]{1,0:T(8,128)(2,1)S(1)} %collective-permute-done.10.refs_9_), channel_id=1, source_target_pairs={{0,2},{1,3},{2,0},{3,1},{4,6},{5,7},{6,4},{7,5},{8,10},{9,11},{10,... | collective-permute-start | bytes 884744 | tf_op jit(solution)/shard_map/ppermute | solution.py:1126
  44.5 10.9 %collective-permute-start.14 = (bf16[128,1152]{1,0:T(8,128)(2,1)S(1)}, bf16[128,1152]{1,0:T(8,128)(2,1)S(1)}, u32[]{:S(2)}, u32[]{:S(2)}) collective-permute-start(bf16[128,1152]{1,0:T(8,128)(2,1)S(1)} %collective-permute-done.11.refs_12_), channel_id=1, source_target_pairs={{0,2},{1,3},{2,0},{3,1},{4,6},{5,7},{6,4},{7,5},{8,10},{9,11},{10,... | collective-permute-start | bytes 884744 | tf_op jit(solution)/shard_map/ppermute | solution.py:1126
  44.8 10.5 %all-to-all-start = ((bf16[8,144,128]{2,1,0:T(8,128)(2,1)}), bf16[8,144,128]{2,1,0:T(8,128)(2,1)S(1)}, u32[]{:S(2)}, u32[]{:S(2)}) async-start(bf16[8,144,128]{2,1,0:T(8,128)(2,1)} %get-tuple-element.186.refs_8_), calls=%async_computation | async-start | bytes 589824 | tf_op jit(solution)/shard_map/all_to_all | solution.py:1149
  59.9 16.9 %collective-permute-start.15 = (bf16[128,1152]{1,0:T(8,128)(2,1)}, bf16[128,1152]{1,0:T(8,128)(2,1)S(1)}, u32[]{:S(2)}, u32[]{:S(2)}) collective-permute-start(bf16[128,1152]{1,0:T(8,128)(2,1)} %get-tuple-element.140.hid_ref.refs_0_), channel_id=1, source_target_pairs={{0,2},{1,3},{2,0},{3,1},{4,6},{5,7},{6,4},{7,5},{8,10},{9,11},{10,... | collective-permute-start | bytes 884744 | tf_op jit(solution)/shard_map/ppermute | solution.py:1126
  59.9 16.9 %collective-permute-start.16 = (bf16[128,1152]{1,0:T(8,128)(2,1)}, bf16[128,1152]{1,0:T(8,128)(2,1)S(1)}, u32[]{:S(2)}, u32[]{:S(2)}) collective-permute-start(bf16[128,1152]{1,0:T(8,128)(2,1)} %get-tuple-element.140.hid_ref.refs_0_), channel_id=1, source_target_pairs={{0,1},{1,0},{2,3},{3,2},{4,5},{5,4},{6,7},{7,6},{8,9},{9,8},{10,11... | collective-permute-start | bytes 884744 | tf_op jit(solution)/shard_map/ppermute | solution.py:1126
  61.4 15.4 %collective-permute-start.17 = (bf16[128,1152]{1,0:T(8,128)(2,1)}, bf16[128,1152]{1,0:T(8,128)(2,1)S(1)}, u32[]{:S(2)}, u32[]{:S(2)}) collective-permute-start(bf16[128,1152]{1,0:T(8,128)(2,1)} %get-tuple-element.140.hid_ref.refs_0_), channel_id=1, source_target_pairs={{0,4},{1,5},{2,6},{3,7},{4,0},{5,1},{6,2},{7,3},{8,12},{9,13},{10,... | collective-permute-start | bytes 884744 | tf_op jit(solution)/shard_map/ppermute | solution.py:1126
  62.9 29.1 %collective-permute-start.25 = (bf16[128,1152]{1,0:T(8,128)(2,1)S(1)}, bf16[128,1152]{1,0:T(8,128)(2,1)S(1)}, u32[]{:S(2)}, u32[]{:S(2)}) collective-permute-start(bf16[128,1152]{1,0:T(8,128)(2,1)S(1)} %collective-permute-done.12.refs_13_), channel_id=1, source_target_pairs={{0,2},{1,3},{2,0},{3,1},{4,6},{5,7},{6,4},{7,5},{8,10},{9,11},{10,... | collective-permute-start | bytes 884744 | tf_op jit(solution)/shard_map/ppermute | solution.py:1126
  76.8 9.6 %collective-permute-start.21 = (bf16[128,1152]{1,0:T(8,128)(2,1)S(1)}, bf16[128,1152]{1,0:T(8,128)(2,1)}, u32[]{:S(2)}, u32[]{:S(2)}) collective-permute-start(bf16[128,1152]{1,0:T(8,128)(2,1)S(1)} %collective-permute-done.16.refs_1_), channel_id=1, source_target_pairs={{0,4},{1,5},{2,6},{3,7},{4,0},{5,1},{6,2},{7,3},{8,12},{9,13},{10,... | collective-permute-start | bytes 884744 | tf_op jit(solution)/shard_map/ppermute | solution.py:1126
  77.4 9.0 %collective-permute-start.22 = (bf16[128,1152]{1,0:T(8,128)(2,1)S(1)}, bf16[128,1152]{1,0:T(8,128)(2,1)S(1)}, u32[]{:S(2)}, u32[]{:S(2)}) collective-permute-start(bf16[128,1152]{1,0:T(8,128)(2,1)S(1)} %collective-permute-done.16.refs_1_), channel_id=1, source_target_pairs={{0,2},{1,3},{2,0},{3,1},{4,6},{5,7},{6,4},{7,5},{8,10},{9,11},{10,... | collective-permute-start | bytes 884744 | tf_op jit(solution)/shard_map/ppermute | solution.py:1126
  77.6 8.8 %collective-permute-start.23 = (bf16[128,1152]{1,0:T(8,128)(2,1)S(1)}, bf16[128,1152]{1,0:T(8,128)(2,1)S(1)}, u32[]{:S(2)}, u32[]{:S(2)}) collective-permute-start(bf16[128,1152]{1,0:T(8,128)(2,1)S(1)} %collective-permute-done.17.refs_4_), channel_id=1, source_target_pairs={{0,2},{1,3},{2,0},{3,1},{4,6},{5,7},{6,4},{7,5},{8,10},{9,11},{10,... | collective-permute-start | bytes 884744 | tf_op jit(solution)/shard_map/ppermute | solution.py:1126
  86.4 5.6 %collective-permute-start.24 = (bf16[128,1152]{1,0:T(8,128)(2,1)}, bf16[128,1152]{1,0:T(8,128)(2,1)S(1)}, u32[]{:S(2)}, u32[]{:S(2)}) collective-permute-start(bf16[128,1152]{1,0:T(8,128)(2,1)} %collective-permute-done.21.refs_5_), channel_id=1, source_target_pairs={{0,2},{1,3},{2,0},{3,1},{4,6},{5,7},{6,4},{7,5},{8,10},{9,11},{10,... | collective-permute-start | bytes 884744 | tf_op jit(solution)/shard_map/ppermute | solution.py:1126
  87.1 19.9 %collective-permute-start.18 = (bf16[128,1152]{1,0:T(8,128)(2,1)S(1)}, bf16[128,1152]{1,0:T(8,128)(2,1)S(1)}, u32[]{:S(2)}, u32[]{:S(2)}) collective-permute-start(bf16[128,1152]{1,0:T(8,128)(2,1)S(1)} %copy-done.21), channel_id=1, source_target_pairs={{0,2},{1,3},{2,0},{3,1},{4,6},{5,7},{6,4},{7,5},{8,10},{9,11},{10,... | collective-permute-start | bytes 884744 | tf_op jit(solution)/shard_map/ppermute | solution.py:1126
  87.2 19.8 %collective-permute-start.19 = (bf16[128,1152]{1,0:T(8,128)(2,1)S(1)}, bf16[128,1152]{1,0:T(8,128)(2,1)S(1)}, u32[]{:S(2)}, u32[]{:S(2)}) collective-permute-start(bf16[128,1152]{1,0:T(8,128)(2,1)S(1)} %copy-done.21), channel_id=1, source_target_pairs={{0,1},{1,0},{2,3},{3,2},{4,5},{5,4},{6,7},{7,6},{8,9},{9,8},{10,11... | collective-permute-start | bytes 884744 | tf_op jit(solution)/shard_map/ppermute | solution.py:1126
  87.9 19.2 %collective-permute-start.20 = (bf16[128,1152]{1,0:T(8,128)(2,1)S(1)}, bf16[128,1152]{1,0:T(8,128)(2,1)S(1)}, u32[]{:S(2)}, u32[]{:S(2)}) collective-permute-start(bf16[128,1152]{1,0:T(8,128)(2,1)S(1)} %copy-done.21), channel_id=1, source_target_pairs={{0,4},{1,5},{2,6},{3,7},{4,0},{5,1},{6,2},{7,3},{8,12},{9,13},{10,... | collective-permute-start | bytes 884744 | tf_op jit(solution)/shard_map/ppermute | solution.py:1126
  88.4 18.7 %all-to-all-start.1 = ((bf16[8,144,128]{2,1,0:T(8,128)(2,1)}), bf16[8,144,128]{2,1,0:T(8,128)(2,1)S(1)}, u32[]{:S(2)}, u32[]{:S(2)}) async-start(bf16[8,144,128]{2,1,0:T(8,128)(2,1)} %get-tuple-element.147), calls=%async_computation.1 | async-start | bytes 589824 | tf_op jit(solution)/shard_map/all_to_all | solution.py:1149
  107.9 20.0 %collective-permute-start.26 = (bf16[864,384]{1,0:T(8,128)(2,1)}, bf16[864,384]{1,0:T(8,128)(2,1)S(1)}, u32[]{:S(2)}, u32[]{:S(2)}) collective-permute-start(bf16[864,384]{1,0:T(8,128)(2,1)} %get-tuple-element.174), channel_id=1, source_target_pairs={{0,8},{24,16},{1,9},{25,17},{2,10},{26,18},{3,11},{27,19},{4,12},{... | collective-permute-start | bytes 1990664 | tf_op jit(solution)/shard_map/ppermute | solution.py:1153
  111.6 16.3 %collective-permute-start.27 = (bf16[864,384]{1,0:T(8,128)(2,1)}, bf16[864,384]{1,0:T(8,128)(2,1)S(1)}, u32[]{:S(2)}, u32[]{:S(2)}) collective-permute-start(bf16[864,384]{1,0:T(8,128)(2,1)} %get-tuple-element.174), channel_id=1, source_target_pairs={{8,16},{16,8},{9,17},{17,9},{10,18},{18,10},{11,19},{19,11},{12,20... | collective-permute-start | bytes 1990664 | tf_op jit(solution)/shard_map/ppermute | solution.py:1153
  112.6 15.3 %collective-permute-start.28 = (bf16[128,1152]{1,0:T(8,128)(2,1)S(1)}, bf16[128,1152]{1,0:T(8,128)(2,1)S(1)}, u32[]{:S(2)}, u32[]{:S(2)}) collective-permute-start(bf16[128,1152]{1,0:T(8,128)(2,1)S(1)} %collective-permute-done.19.refs_1_), channel_id=1, source_target_pairs={{0,4},{1,5},{2,6},{3,7},{4,0},{5,1},{6,2},{7,3},{8,12},{9,13},{10,... | collective-permute-start | bytes 884744 | tf_op jit(solution)/shard_map/ppermute | solution.py:1126
  114.7 13.2 %collective-permute-start.29 = (bf16[128,1152]{1,0:T(8,128)(2,1)S(1)}, bf16[128,1152]{1,0:T(8,128)(2,1)}, u32[]{:S(2)}, u32[]{:S(2)}) collective-permute-start(bf16[128,1152]{1,0:T(8,128)(2,1)S(1)} %collective-permute-done.19.refs_1_), channel_id=1, source_target_pairs={{0,2},{1,3},{2,0},{3,1},{4,6},{5,7},{6,4},{7,5},{8,10},{9,11},{10,... | collective-permute-start | bytes 884744 | tf_op jit(solution)/shard_map/ppermute | solution.py:1126
  114.7 13.2 %collective-permute-start.30 = (bf16[128,1152]{1,0:T(8,128)(2,1)S(1)}, bf16[128,1152]{1,0:T(8,128)(2,1)}, u32[]{:S(2)}, u32[]{:S(2)}) collective-permute-start(bf16[128,1152]{1,0:T(8,128)(2,1)S(1)} %collective-permute-done.20.refs_4_), channel_id=1, source_target_pairs={{0,2},{1,3},{2,0},{3,1},{4,6},{5,7},{6,4},{7,5},{8,10},{9,11},{10,... | collective-permute-start | bytes 884744 | tf_op jit(solution)/shard_map/ppermute | solution.py:1126
  127.9 11.0 %collective-permute-start.31 = (bf16[128,1152]{1,0:T(8,128)(2,1)S(1)}, bf16[128,1152]{1,0:T(8,128)(2,1)S(1)}, u32[]{:S(2)}, u32[]{:S(2)}) collective-permute-start(bf16[128,1152]{1,0:T(8,128)(2,1)S(1)} %collective-permute-done.28.refs_5_), channel_id=1, source_target_pairs={{0,2},{1,3},{2,0},{3,1},{4,6},{5,7},{6,4},{7,5},{8,10},{9,11},{10,... | collective-permute-start | bytes 884744 | tf_op jit(solution)/shard_map/ppermute | solution.py:1126
  128.8 16.7 %all-to-all-start.2 = ((bf16[8,432,128]{2,1,0:T(8,128)(2,1)}), bf16[8,432,128]{2,1,0:T(8,128)(2,1)S(1)}, u32[]{:S(2)}, u32[]{:S(2)}) async-start(bf16[8,432,128]{2,1,0:T(8,128)(2,1)} %get-tuple-element.185.back_ref), calls=%async_computation.2 | async-start | bytes 1769472 | tf_op jit(solution)/shard_map/all_to_all | solution.py:1149
  132.4 62.4 %collective-permute-start.32 = (bf16[864,384]{1,0:T(8,128)(2,1)}, bf16[864,384]{1,0:T(8,128)(2,1)}, u32[]{:S(2)}, u32[]{:S(2)}) collective-permute-start(bf16[864,384]{1,0:T(8,128)(2,1)} %get-tuple-element.201), channel_id=1, source_target_pairs={{0,8},{8,0},{16,24},{24,16},{1,9},{9,1},{17,25},{25,17},{2,10},{10... | collective-permute-start | bytes 1990664 | tf_op jit(solution)/shard_map/ppermute | solution.py:1153
  135.1 59.6 %collective-permute-start.33 = (bf16[864,384]{1,0:T(8,128)(2,1)S(1)}, bf16[864,384]{1,0:T(8,128)(2,1)}, u32[]{:S(2)}, u32[]{:S(2)}) collective-permute-start(bf16[864,384]{1,0:T(8,128)(2,1)S(1)} %copy-done.2), channel_id=1, source_target_pairs={{0,16},{24,8},{1,17},{25,9},{2,18},{26,10},{3,19},{27,11},{4,20},{... | collective-permute-start | bytes 1990664 | tf_op jit(solution)/shard_map/ppermute | solution.py:1153
  143.6 45.9 %collective-permute-start.34 = (bf16[864,384]{1,0:T(8,128)(2,1)S(1)}, bf16[864,384]{1,0:T(8,128)(2,1)}, u32[]{:S(2)}, u32[]{:S(2)}) collective-permute-start(bf16[864,384]{1,0:T(8,128)(2,1)S(1)} %add_convert_fusion), channel_id=1, source_target_pairs={{8,24},{16,0},{9,25},{17,1},{10,26},{18,2},{11,27},{19,3},{12,28},... | collective-permute-start | bytes 1990664 | tf_op jit(solution)/shard_map/ppermute | solution.py:1153
  145.5 20.0 %all-to-all-start.3 = ((bf16[8,144,512]{2,1,0:T(8,128)(2,1)}), bf16[8,144,512]{2,1,0:T(8,128)(2,1)S(1)}, u32[]{:S(2)}, u32[]{:S(2)}) async-start(bf16[8,144,512]{2,1,0:T(8,128)(2,1)} %qkv_weights.1), calls=%async_computation.3 | async-start | bytes 2359296 | tf_op jit(solution)/shard_map/all_to_all | solution.py:1149
  165.5 16.4 %all-to-all-start.4 = ((f32[32,8,128]{2,1,0:T(8,128)}), f32[32,8,128]{2,1,0:T(8,128)S(1)}, u32[]{:S(2)}, u32[]{:S(2)}) async-start(f32[32,8,128]{2,1,0:T(8,128)} %get-tuple-element.195), calls=%async_computation.4 | async-start | bytes 262144 | tf_op jit(solution)/shard_map/all_to_all | solution.py:1149
  174.5 15.6 %collective-permute-start.35 = (bf16[144,1152]{1,0:T(8,128)(2,1)}, bf16[144,1152]{1,0:T(8,128)(2,1)S(1)}, u32[]{:S(2)}, u32[]{:S(2)}) collective-permute-start(bf16[144,1152]{1,0:T(8,128)(2,1)} %get-tuple-element.206), channel_id=1, source_target_pairs={{0,8},{24,16},{1,9},{25,17},{2,10},{26,18},{3,11},{27,19},{4,12},{... | collective-permute-start | bytes 995336 | tf_op jit(solution)/shard_map/ppermute | solution.py:1153
  178.2 15.1 %collective-permute-start.36 = (bf16[144,1152]{1,0:T(8,128)(2,1)}, bf16[144,1152]{1,0:T(8,128)(2,1)S(1)}, u32[]{:S(2)}, u32[]{:S(2)}) collective-permute-start(bf16[144,1152]{1,0:T(8,128)(2,1)} %get-tuple-element.206), channel_id=1, source_target_pairs={{8,16},{16,8},{9,17},{17,9},{10,18},{18,10},{11,19},{19,11},{12,20... | collective-permute-start | bytes 995336 | tf_op jit(solution)/shard_map/ppermute | solution.py:1153
  186.1 12.8 %all-to-all-start.5 = ((f32[8,8,288]{2,1,0:T(8,128)}), f32[8,8,288]{2,1,0:T(8,128)S(1)}, u32[]{:S(2)}, u32[]{:S(2)}) async-start(f32[8,8,288]{2,1,0:T(8,128)} %get-tuple-element.198), calls=%async_computation.5 | async-start | bytes 196608 | tf_op jit(solution)/shard_map/all_to_all | solution.py:1149
  189.5 23.6 %collective-permute-start.40 = (bf16[144,1152]{1,0:T(8,128)(2,1)S(1)}, bf16[144,1152]{1,0:T(8,128)(2,1)S(1)}, u32[]{:S(2)}, u32[]{:S(2)}) collective-permute-start(bf16[144,1152]{1,0:T(8,128)(2,1)S(1)} %copy-done.14), channel_id=1, source_target_pairs={{0,8},{8,0},{16,24},{24,16},{1,9},{9,1},{17,25},{25,17},{2,10},{10... | collective-permute-start | bytes 995336 | tf_op jit(solution)/shard_map/ppermute | solution.py:1153
  190.2 22.9 %collective-permute-start.41 = (bf16[144,1152]{1,0:T(8,128)(2,1)S(1)}, bf16[144,1152]{1,0:T(8,128)(2,1)S(1)}, u32[]{:S(2)}, u32[]{:S(2)}) collective-permute-start(bf16[144,1152]{1,0:T(8,128)(2,1)S(1)} %copy-done.4), channel_id=1, source_target_pairs={{0,16},{24,8},{1,17},{25,9},{2,18},{26,10},{3,19},{27,11},{4,20},{... | collective-permute-start | bytes 995336 | tf_op jit(solution)/shard_map/ppermute | solution.py:1153
  193.4 19.6 %collective-permute-start.37 = (bf16[144,1152]{1,0:T(8,128)(2,1)S(1)}, bf16[144,1152]{1,0:T(8,128)(2,1)}, u32[]{:S(2)}, u32[]{:S(2)}) collective-permute-start(bf16[144,1152]{1,0:T(8,128)(2,1)S(1)} %add_convert_fusion.1), channel_id=1, source_target_pairs={{8,24},{16,0},{9,25},{17,1},{10,26},{18,2},{11,27},{19,3},{12,28},... | collective-permute-start | bytes 995336 | tf_op jit(solution)/shard_map/ppermute | solution.py:1153
  198.9 14.1 %all-to-all-start.6 = ((bf16[8,144,192]{2,1,0:T(8,128)(2,1)}), bf16[8,144,192]{2,1,0:T(8,128)(2,1)S(1)}, u32[]{:S(2)}, u32[]{:S(2)}) async-start(bf16[8,144,192]{2,1,0:T(8,128)(2,1)} %get-tuple-element.209), calls=%async_computation.6 | async-start | bytes 1179648 | tf_op jit(solution)/shard_map/all_to_all | solution.py:1149
  203.1 10.0 %collective-permute-start.38 = (bf16[288,192]{1,0:T(8,128)(2,1)}, bf16[288,192]{1,0:T(8,128)(2,1)S(1)}, u32[]{:S(2)}, u32[]{:S(2)}) collective-permute-start(bf16[288,192]{1,0:T(8,128)(2,1)} %get-tuple-element.219), channel_id=1, source_target_pairs={{0,0},{1,4},{2,1},{3,5},{4,2},{5,6},{6,3},{7,7},{8,8},{9,12},{10,9... | collective-permute-start | bytes 331784 | tf_op jit(solution)/shard_map/ppermute | solution.py:1484
  204.6 11.2 %collective-permute-start.39 = (bf16[288,192]{1,0:T(8,128)(2,1)}, bf16[288,192]{1,0:T(8,128)(2,1)S(1)}, u32[]{:S(2)}, u32[]{:S(2)}) collective-permute-start(bf16[288,192]{1,0:T(8,128)(2,1)} %get-tuple-element.220), channel_id=1, source_target_pairs={{0,4},{1,0},{2,5},{3,1},{4,6},{5,2},{6,7},{7,3},{8,12},{9,8},{10,1... | collective-permute-start | bytes 331784 | tf_op jit(solution)/shard_map/ppermute | solution.py:1485
  (46 other events, 271.3 us)

commit v4 on v3

--- a/solution.py
+++ b/solution.py
@@ -392,24 +392,12 @@
     pay_ref[tokens : tokens + EXTRA, :] = extra.astype(jnp.bfloat16)
 
 
-def ready_kernel(
-    blocks, tile_cols, scalars, *refs,
-):
+def ready_kernel(blocks, tile_cols, scalars, *refs):
     qkv_parts, refs = refs[:6], refs[6:]
     (
-        gate_a, gate_b, up_a, up_b, qgain_ref, kgain_ref, table_ref, modw_ref,
-        spread_ref, order_ref, turn_ref, gain_ref, gate_ref, up_ref, tshare_ref, mshare_ref,
-        window_ref, pick_ref,
+        qgain_ref, kgain_ref, spread_ref, order_ref, turn_ref, gain_ref, window_ref, pick_ref,
     ) = refs
     mine = scalars[0]
-    share = tshare_ref.shape[1]
-    for image in range(table_ref.shape[1] // share):
-
-        @pl.when(scalars[1] == image)
-        def _(image=image):
-            tshare_ref[...] = table_ref[:, share * image : share * (image + 1)]
-            mshare_ref[...] = modw_ref[:, share * image : share * (image + 1)]
-
     heads = HEADS // blocks
     span = heads * HD
     wide = 3 * heads * LANES
@@ -441,6 +429,21 @@
     gain_ref[...] = jnp.zeros_like(gain_ref)
     wide_row(qgain_ref[...].reshape(1, HD), gain_ref, 0)
     wide_row(kgain_ref[...].reshape(1, HD), gain_ref, 1)
+
+
+def layout_kernel(
+    scalars, gate_a, gate_b, up_a, up_b, table_ref, modw_ref,
+    gate_ref, up_ref, tshare_ref, mshare_ref,
+):
+    mine = scalars[0]
+    share = tshare_ref.shape[1]
+    for image in range(table_ref.shape[1] // share):
+
+        @pl.when(scalars[1] == image)
+        def _(image=image):
+            tshare_ref[...] = table_ref[:, share * image : share * (image + 1)]
+            mshare_ref[...] = modw_ref[:, share * image : share * (image + 1)]
+
     units = gate_ref.shape[1]
     run = units // 2
     for parity in range(2):
@@ -615,27 +618,42 @@
     out_ref[...] = dot_nt(low_ref[...], down_ref[...])
 
 
-def mlp_kernel(
-    gate_ref, up_ref, outw_ref, hid_ref, mid_ref, attn_ref, cot_ref, agrad_in, mod_ref,
-    act_ref, mgrad_ref, agrad_ref, dgrad_ref, sums_ref, back_ref,
-):
-    step = pl.program_id(0)
-
+def mlp_step(gate_ref, up_ref, hid_ref, agrad_ref, act_ref):
     hidden = hid_ref[...]
     gate = dot_nn(hidden, gate_ref[...])
     up = dot_nn(hidden, up_ref[...])
     sigma = sigmoid(gate)
     silu = gate * sigma
     act_ref[...] = (silu * up).astype(jnp.bfloat16)
-    act_grad = agrad_in[...]
+    act_grad = agrad_ref[...]
     slope = sigma * (1.0 + gate * (1.0 - sigma))
     gate_grad = (act_grad * up * slope).astype(jnp.bfloat16)
     up_grad = (act_grad * silu).astype(jnp.bfloat16)
-    part = dot_nt(gate_grad, gate_ref[...]) + dot_nt(up_grad, up_ref[...])
+    return dot_nt(gate_grad, gate_ref[...]) + dot_nt(up_grad, up_ref[...])
+
+
+def mlp_first_kernel(gate_ref, up_ref, hid_ref, agrad_ref, act_ref, back_ref):
+    part = mlp_step(gate_ref, up_ref, hid_ref, agrad_ref, act_ref)
+
+    @pl.when(pl.program_id(0) == 0)
+    def _():
+        back_ref[...] = part
+
+    @pl.when(pl.program_id(0) > 0)
+    def _():
+        back_ref[...] += part
+
+
+def mlp_kernel(
+    gate_ref, up_ref, outw_ref, hid_ref, mid_ref, attn_ref, cot_ref, agrad_in, mod_ref, start_ref,
+    act_ref, mgrad_ref, agrad_ref, dgrad_ref, sums_ref, back_ref,
+):
+    step = pl.program_id(0)
+    part = mlp_step(gate_ref, up_ref, hid_ref, agrad_in, act_ref)
 
     @pl.when(step == 0)
     def _():
-        back_ref[...] = part
+        back_ref[...] = start_ref[...] + part
 
     @pl.when(step > 0)
     def _():
@@ -663,9 +681,15 @@
         sums_ref[4:5, :] = column_sum(back * unit)
 
 
-def mlp_out_kernel(act_ref, down_ref, mid_ref, cot_ref, mod_ref, output_ref, sum_ref, acc_ref):
+def mlp_out_kernel(
+    first_ref, second_ref, low_ref, high_ref, mid_ref, cot_ref, mod_ref, sums_ref, insum_ref,
+    gsum_ref, bucket_ref, output_ref, send_ref, acc_ref, flat_ref, row_ref,
+):
     step = pl.program_id(0)
-    part = dot_nn(act_ref[...], down_ref[...])
+    blocks = row_ref.shape[0]
+    width = mid_ref.shape[1]
+    columns = 6 * width // blocks
+    part = dot_nn(first_ref[...], low_ref[...]) + dot_nn(second_ref[...], high_ref[...])
 
     @pl.when(step == 0)
     def _():
@@ -678,7 +702,35 @@
     @pl.when(step == pl.num_programs(0) - 1)
     def _():
         output_ref[...] = mid_ref[...] + mod_ref[5:6, :] * acc_ref[...]
-        sum_ref[...] = jnp.broadcast_to(column_sum(cot_ref[...] * acc_ref[...]), sum_ref.shape)
+        for index in range(2):
+            flat_ref[0:1, width * index : width * (index + 1)] = insum_ref[index : index + 1, :]
+        for index in range(2, 5):
+            flat_ref[0:1, width * index : width * (index + 1)] = sums_ref[index : index + 1, :]
+        flat_ref[0:1, width * 5 : width * 6] = column_sum(cot_ref[...] * acc_ref[...])
+        row_ref[...] = jnp.zeros_like(row_ref)
+        for index in range(blocks):
+            row_ref[index : index + 1, 0:columns] = flat_ref[
+                0:1, columns * index : columns * (index + 1)
+            ]
+        row_ref[:, columns : columns + 1] = jnp.broadcast_to(
+            bucket_ref[0].astype(jnp.float32), (blocks, 1)
+        )
+        for line in range(2):
+            for source, target in PLACES:
+                start = columns + 16 + HD * line + source
+                row_ref[:, start : start + QUARTER] = jnp.broadcast_to(
+                    gsum_ref[line : line + 1, target : target + QUARTER], (blocks, QUARTER)
+                )
+        for index in range(blocks):
+            tile = jnp.concatenate(
+                [
+                    row_ref[index : index + 1, LANES * part : LANES * (part + 1)]
+                    for part in range(8)
+                ],
+                axis=0,
+            )
+            for image in range(send_ref.shape[0] // blocks):
+                send_ref[blocks * image + index] = tile
 
 
 def mlp_weights_kernel(scalars, *refs):
@@ -1018,28 +1070,26 @@
 
 
 def input_kernel(
-    back_ref, weight_ref, x_ref, mgrad_ref, mod_ref, sums_ref, gmid_ref, gsum_ref, bucket_ref,
-    grad_ref, send_ref, acc_ref, flat_ref, row_ref,
+    back_ref, weight_ref, x_ref, mgrad_ref, mod_ref, grad_ref, insum_ref, acc_ref,
 ):
     step = pl.program_id(0)
     blocks = back_ref.shape[0]
     span = HD * HEADS // blocks
     width = x_ref.shape[1]
-    columns = 6 * width // blocks
-
-    for side in range(3):
-
-        @pl.when(step == side)
-        def _(side=side):
-            natural = jnp.concatenate(
-                [back_ref[index, span * side : span * (side + 1), :] for index in range(blocks)],
-                axis=0,
-            )
-            part = lax.dot_general(
-                natural, weight_ref[...], (((0,), (1,)), ((), ())),
-                preferred_element_type=jnp.float32,
-            )
-            acc_ref[...] = part if side == 0 else acc_ref[...] + part
+
+    rows = pl.ds(pl.multiple_of(span * step, 16), span)
+    natural = jnp.concatenate([back_ref[index, rows, :] for index in range(blocks)], axis=0)
+    part = lax.dot_general(
+        natural, weight_ref[...], (((0,), (1,)), ((), ())), preferred_element_type=jnp.float32
+    )
+
+    @pl.when(step == 0)
+    def _():
+        acc_ref[...] = part
+
+    @pl.when(step > 0)
+    def _():
+        acc_ref[...] += part
 
     @pl.when(step == 2)
     def _():
@@ -1051,35 +1101,9 @@
         grad_ref[...] = mgrad_ref[...] + inverse * (
             lifted - unit * jnp.mean(lifted * unit, axis=-1, keepdims=True)
         )
-        flat_ref[0:1, 0:width] = column_sum(back)
-        flat_ref[0:1, width : 2 * width] = column_sum(back * unit)
-        for index in range(2, 5):
-            flat_ref[0:1, width * index : width * (index + 1)] = sums_ref[index : index + 1, :]
-        flat_ref[0:1, width * 5 : width * 6] = gmid_ref[0:1, :]
-        row_ref[...] = jnp.zeros_like(row_ref)
-        for index in range(blocks):
-            row_ref[index : index + 1, 0:columns] = flat_ref[
-                0:1, columns * index : columns * (index + 1)
-            ]
-        row_ref[:, columns : columns + 1] = jnp.broadcast_to(
-            bucket_ref[0].astype(jnp.float32), (blocks, 1)
-        )
-        for line in range(2):
-            for source, target in PLACES:
-                start = columns + 16 + HD * line + source
-                row_ref[:, start : start + QUARTER] = jnp.broadcast_to(
-                    gsum_ref[line : line + 1, target : target + QUARTER], (blocks, QUARTER)
-                )
-        for index in range(blocks):
-            tile = jnp.concatenate(
-                [
-                    row_ref[index : index + 1, LANES * part : LANES * (part + 1)]
-                    for part in range(8)
-                ],
-                axis=0,
-            )
-            for image in range(send_ref.shape[0] // blocks):
-                send_ref[blocks * image + index] = tile
+        insum_ref[...] = jnp.zeros_like(insum_ref)
+        insum_ref[0:1, :] = column_sum(back)
+        insum_ref[1:2, :] = column_sum(back * unit)
 
 
 def whole_spec(shape):
@@ -1219,40 +1243,46 @@
         specs={0: SMEM, 1: SMEM},
     )
     core, xn, yn = first_round(pay)
-    spread, order, offsets, gains, own_gate, own_up, table_share, modw_share = call(
+    spread, order, offsets, gains = call(
         functools.partial(ready_kernel, blocks, tile_cols),
-        (*[qkv_weight] * 6, *[gate_up_weight] * 4, query_gain, key_gain, cond_table, mod_weight.T),
+        (*[qkv_weight] * 6, query_gain, key_gain),
         (
             struct((width, wide), bf16),
             struct((3 * span, wide), bf16),
             struct((3, tokens, LANES)),
             struct((8, LANES)),
+        ),
+        [pltpu.VMEM((width, wide), bf16), pltpu.VMEM((wide, wide), bf16)],
+        where,
+        "ready",
+        specs={
+            2 * side + n: pl.BlockSpec(
+                (width, LANES), lambda i, s, c=side * width // LANES + n: (0, c + s[0])
+            )
+            for side in range(3)
+            for n in range(2)
+        },
+    )
+    xn, yn, spread, order, offsets, gains = tie(xn, yn, spread, order, offsets, gains)
+    d1, d2, cx, cy = split_round(xn, yn, half)
+    late_gate, late_table, spread, cx = tie(gate_up_weight, cond_table, spread, cx)
+    own_gate, own_up, table_share, modw_share = call(
+        layout_kernel,
+        (*[late_gate] * 4, late_table, mod_weight.T),
+        (
             struct((width, units), bf16),
             struct((width, units), bf16),
             struct((cond_table.shape[0], share)),
             struct((columns, share), bf16),
         ),
-        [pltpu.VMEM((width, wide), bf16), pltpu.VMEM((wide, wide), bf16)],
-        where,
-        "ready",
+        scalars=where,
+        name="layout",
         specs={
-            **{
-                2 * side + n: pl.BlockSpec(
-                    (width, LANES), lambda i, s, c=side * width // LANES + n: (0, c + s[0])
-                )
-                for side in range(3)
-                for n in range(2)
-            },
-            **{
-                6 + n: pl.BlockSpec((width, units), lambda i, s, n=n: (0, n * 4 + s[0] // 2))
-                for n in range(4)
-            },
+            n: pl.BlockSpec((width, units), lambda i, s, n=n: (0, n * 4 + s[0] // 2))
+            for n in range(4)
         },
     )
-    xn, yn, spread, order, offsets, gains, own_gate, own_up = tie(
-        xn, yn, spread, order, offsets, gains, own_gate, own_up
-    )
-    d1, d2, cx, cy = split_round(xn, yn, half)
+    d1, d2, cy, own_gate = tie(d1, d2, cy, own_gate)
     pieces = (pay, xn, core, cx, yn, d1, d2, cy, swap(d1, 2), swap(d2, 2))
     c_core, c_xn, c_yn = first_round(low_cot)
     att, hid, qkv, unit, turn, mod, logs, mixed = call(
@@ -1313,11 +1343,32 @@
         name="middle",
     )
     h_core, h_xn, h_yn = first_round(hidden_mid)
-    act, middle_grad, attn_grad, attg, sums = call(
+    early = mlp_steps // 2
+    slab = pl.BlockSpec((tokens, step_units), lambda f: (0, f))
+    act_first, back_first = call(
+        mlp_first_kernel,
+        (gate_up_weight, gate_up_weight, hidden_mid, act_grad),
+        (struct((tokens, early * step_units), bf16), struct((tokens, width))),
+        name="mlp_first",
+        micros=7,
+        specs={
+            0: pl.BlockSpec((width, step_units), lambda f: (0, f)),
+            1: pl.BlockSpec((width, step_units), lambda f: (0, mlp_steps + f)),
+            3: slab,
+        },
+        out_specs={0: slab},
+        grid=(early,),
+    )
+    back_first, h_core, h_xn, h_yn = tie(back_first, h_core, h_xn, h_yn)
+    h_dn, h_cx, h_cy = second_round(h_xn, h_yn)
+    act_second, middle_grad, attn_grad, attg, sums = call(
         mlp_kernel,
-        (gate_up_weight, gate_up_weight, out_weight, hidden_mid, middle, attn_out, cot, act_grad, mod),
         (
-            struct((tokens, hidden_units), bf16),
+            gate_up_weight, gate_up_weight, out_weight, hidden_mid, middle, attn_out, cot, act_grad,
+            mod, back_first,
+        ),
+        (
+            struct((tokens, hidden_units - early * step_units), bf16),
             struct((tokens, width)),
             struct((tokens, width), bf16),
             struct((blocks, span, tokens), bf16),
@@ -1325,31 +1376,17 @@
         ),
         [pltpu.VMEM((tokens, width), jnp.float32)],
         name="mlp",
-        micros=12,
+        micros=8,
         specs={
-            0: pl.BlockSpec((width, step_units), lambda f: (0, f)),
-            1: pl.BlockSpec((width, step_units), lambda f: (0, mlp_steps + f)),
-            7: pl.BlockSpec((tokens, step_units), lambda f: (0, f)),
+            0: pl.BlockSpec((width, step_units), lambda f: (0, early + f)),
+            1: pl.BlockSpec((width, step_units), lambda f: (0, mlp_steps + early + f)),
+            7: pl.BlockSpec((tokens, step_units), lambda f: (0, early + f)),
         },
-        out_specs={0: pl.BlockSpec((tokens, step_units), lambda f: (0, f))},
-        grid=(mlp_steps,),
-    )
-    attg, h_core, h_xn, h_yn = tie(attg, h_core, h_xn, h_yn)
+        out_specs={0: slab},
+        grid=(mlp_steps - early,),
+    )
+    attg, h_dn, h_cx, h_cy = tie(attg, h_dn, h_cx, h_cy)
     attg_all = exchange(attg)
-    h_dn, h_cx, h_cy = second_round(h_xn, h_yn)
-    output, gmid = call(
-        mlp_out_kernel,
-        (act, down_weight, middle, cot, mod),
-        (struct((tokens, width)), struct((8, width))),
-        [pltpu.VMEM((tokens, width), jnp.float32)],
-        name="mlp_out",
-        specs={
-            0: pl.BlockSpec((tokens, step_units), lambda f: (0, f)),
-            1: pl.BlockSpec((step_units, width), lambda f: (f, 0)),
-        },
-        grid=(mlp_steps,),
-    )
-    h_dn, h_cx, h_cy, gmid = tie(h_dn, h_cx, h_cy, gmid)
     hid_pieces = (hidden_mid, h_xn, h_core, h_cx, h_yn, h_dn, h_cy, swap(h_dn, 2))
     zrows = run * lanes + width // images
     a_core, a_xn, a_yn = first_round(attn_grad)
@@ -1421,19 +1458,38 @@
         specs={index: ANY for index in range(blocks)},
     )
     back_all, outw_part = tie(back_all, outw_part)
-    in_grad, send = call(
+    in_grad, insum = call(
         input_kernel,
-        (back_all, qkv_weight, x, middle_grad, mod, sums, gmid, gain_sums, bucket),
+        (back_all, qkv_weight, x, middle_grad, mod),
+        (struct((tokens, width)), struct((8, width))),
+        [pltpu.VMEM((tokens, width), jnp.float32)],
+        name="input",
+        micros=7,
+        specs={1: pl.BlockSpec((width, width), lambda s: (0, s))},
+        grid=(3,),
+    )
+    output, send = call(
+        mlp_out_kernel,
+        (
+            act_first, act_second, down_weight, down_weight, middle, cot, mod, sums, insum,
+            gain_sums, bucket,
+        ),
         (struct((tokens, width)), struct((images * blocks, 8, LANES))),
         [
             pltpu.VMEM((tokens, width), jnp.float32),
             pltpu.VMEM((1, 6 * width), jnp.float32),
             pltpu.VMEM((blocks, 1024), jnp.float32),
         ],
-        name="input",
-        micros=7,
-        specs={1: pl.BlockSpec((width, width), lambda s: (0, s)), 8: SMEM},
-        grid=(3,),
+        name="mlp_out",
+        micros=5,
+        specs={
+            0: slab,
+            1: slab,
+            2: pl.BlockSpec((step_units, width), lambda f: (f, 0)),
+            3: pl.BlockSpec((step_units, width), lambda f: (early + f, 0)),
+            10: SMEM,
+        },
+        grid=(early,),
     )
     send, qkv_rows = tie(send, qkv_rows)
     everywhere = exchange(send, ("img", "ty", "tx"))
@@ -1483,6 +1539,7 @@
     gateup_rows = exchange(send_gateup)
     first = lax.ppermute(first, PLANE, [(t, t // 2 + 4 * (t % 2)) for t in range(8)])
     second = lax.ppermute(second, PLANE, [(t, t // 2 + 4 * (1 - t % 2)) for t in range(8)])
+    act_parts, j_other = tie(act_parts, j_other)
     (table_total,) = call(
         table_kernel,
         (act_parts, condition, buckets),
@@ -1490,7 +1547,7 @@
         scalars=where,
         name="table",
     )
-    gateup_rows, table_total, j_other = tie(gateup_rows, table_total, j_other)
+    gateup_rows, table_total = tie(gateup_rows, table_total)
     gateup_total, down_total, qkv_total, outw_total = call(
         lay_kernel,
         (gateup_rows, first, second, joined[0], j_mid, j_near, j_two, j_other),

time: 224 us -> 219 us (0.978)
  waiting for transfers between devices: 23.7 us -> 15.1 us
  Pallas kernels: 115 us -> 120 us
  starting transfers between devices: 71.1 us -> 73.5 us
    ppermute x30, waiting for transfers between devices: 8.47 us -> 2.29 us  [swap(): lax.ppermute(value, PLANE, [(index, index ^ bit) for index in range(8)])]
    pallas_call x17 -> x19, Pallas kernels: 115 us -> 120 us  [call(): pl.pallas_call(kernel, out_shape=outs, grid_spec=pltpu.PrefetchScalarGrid...]
    ppermute x30, starting transfers between devices: 17.9 us -> 20.8 us  [swap(): lax.ppermute(value, PLANE, [(index, index ^ bit) for index in range(8)])]
    all_to_all x7, waiting for transfers between devices: 8.85 us -> 6.45 us  [exchange(): return lax.all_to_all(value, axes, split_axis=0, concat_axis=0, tiled=True)]
    unnamed x90 -> x96, local copies, waits for them, and re-layouts: 7.31 us -> 5.81 us
  transfers between devices with their start and end apart: 49 -> 49, of which waited for: 9 -> 9; matrix products, arithmetic and copies ran while one was open for 0% -> 0% of each run, Pallas kernels for 47% -> 50%
where the time goes in v4:
time: 219 us; the launch traced here: 218 us
  Pallas kernels  120 us (55%)
  starting transfers between devices  73.5 us (34%)
  waiting for transfers between devices  15.1 us (7%)
  local copies, waits for them, and re-layouts  5.84 us (3%)
    pallas_call x19, Pallas kernels, call(): pl.pallas_call(kernel, out_shape=outs, grid_spec=pltpu.PrefetchScalarGrid...  120 us
    all_to_all x7, starting transfers between devices, exchange(): return lax.all_to_all(value, axes, split_axis=0, concat_axis=0, tiled=True)  25.9 us
    ppermute x10, starting transfers between devices, shift(): return lax.ppermute(value, 'img', pairs)  22.7 us
    ppermute x30, starting transfers between devices, swap(): lax.ppermute(value, PLANE, [(index, index ^ bit) for index in range(8)])  20.8 us
    all_to_all x7, waiting for transfers between devices, exchange(): return lax.all_to_all(value, axes, split_axis=0, concat_axis=0, tiled=True)  6.45 us
    unnamed x96, local copies, waits for them, and re-layouts  5.81 us
    ppermute x10, waiting for transfers between devices, shift(): return lax.ppermute(value, 'img', pairs)  5.8 us
  transfers between devices with their start and end apart: 49, of which 9 were waited for; matrix products, arithmetic and copies ran while one was open for 0% of the time, Pallas kernels for 50%

profile of v4, /device:TPU:0, one launch (start us, length us, event | category | flops | bytes accessed | tf_op | source)
XLA Modules:
  0.0 217.6 jit_solution(288356047462739628)
XLA Ops:
  1.3 3.5 %open.1 = (bf16[144,1152]{1,0:T(8,128)(2,1)}, bf16[128,1152]{1,0:T(8,128)(2,1)}) custom-call(s32[1]{0:T(128)S(6)} %copy.24.bucket_ref, s32[2]{0:T(128)} %bitcast.18, f32[128,1152]{1,0:T(8,128)} %bitcast.15, f32[32,1152]{1,0:T(8,128)} %table_ref.2, bf16[864,1152]{1,0:T(8,128)(2,1)} %bitcast.9, f32[864]{0:T(1024)} %bias_ref.1, f32[128,1152]{1,0:T(8,128)} %bitcast.11), custom_call_target="tpu_custom_call" | custom-call | flops 5000000000 | bytes 5000000 | tf_op jit(solution)/shard_map/open/pallas_call | solution.py:1121
  4.8 2.9 %collective-permute-start = (bf16[144,1152]{1,0:T(8,128)(2,1)}, bf16[144,1152]{1,0:T(8,128)(2,1)S(1)}, u32[]{:S(2)}, u32[]{:S(2)}) collective-permute-start(bf16[144,1152]{1,0:T(8,128)(2,1)} %get-tuple-element.130.refs_0_), channel_id=1, source_target_pairs={{0,1},{1,0},{2,3},{3,2},{4,5},{5,4},{6,7},{7,6},{8,9},{9,8},{10,11... | collective-permute-start | bytes 995336 | tf_op jit(solution)/shard_map/ppermute | solution.py:1150
  7.7 1.5 collective-permute-start.1
  9.9 5.7 %ready.1 = (bf16[1152,768]{1,0:T(8,128)(2,1)}, bf16[432,768]{1,0:T(8,128)(2,1)}, f32[3,128,128]{2,1,0:T(8,128)}, f32[8,128]{1,0:T(8,128)}) custom-call(s32[2]{0:T(128)} %pad_add_fusion.scalars, bf16[1152,3456]{1,0:T(8,128)(2,1)} %weight_ref.3, bf16[1152,3456]{1,0:T(8,128)(2,1)} %weight_ref.3, bf16[1152,3456]{1,0:T(8,128)(2,1)} %weight_ref.3, ...), custom_call_target="tpu_custom_call" | custom-call | flops 5000000000 | bytes 5000000 | tf_op jit(solution)/shard_map/ready/pallas_call | solution.py:1121
  15.7 1.5 collective-permute-done.1.refs_4_
  18.3 1.7 collective-permute-start.4
  20.0 5.3 %layout.1 = (bf16[1152,384]{1,0:T(8,128)(2,1)}, bf16[1152,384]{1,0:T(8,128)(2,1)}, f32[32,288]{1,0:T(8,128)}, bf16[864,288]{1,0:T(8,128)(2,1)}) custom-call(s32[2]{0:T(128)} %pad_add_fusion.scalars, bf16[1152,6144]{1,0:T(8,128)(2,1)} %up_ref.3, bf16[1152,6144]{1,0:T(8,128)(2,1)} %up_ref.3, bf16[1152,6144]{1,0:T(8,128)(2,1)} %up_ref.3, ...), custom_call_target="tpu_custom_call" | custom-call | flops 5000000000 | bytes 5000000 | tf_op jit(solution)/shard_map/layout/pallas_call | solution.py:1121
  26.0 1.5 collective-permute-start.10
  29.5 12.7 %attend.1 = (bf16[8,144,128]{2,1,0:T(8,128)(2,1)}, bf16[1024,1152]{1,0:T(8,128)(2,1)}, bf16[6,1024,128]{2,1,0:T(8,128)(2,1)}, f32[4,1024,128]{2,1,0:T(8,128)}, f...) custom-call(s32[2]{0:T(128)} %pad_add_fusion.scalars, ...), custom_call_target="tpu_custom_call" | custom-call | flops 15000000512 | bytes 15000000 | tf_op jit(solution)/shard_map/attend/pallas_call | solution.py:1121
  42.2 1.6 collective-permute-start.12
  44.3 3.6 %all-to-all-start = ((bf16[8,144,128]{2,1,0:T(8,128)(2,1)}), bf16[8,144,128]{2,1,0:T(8,128)(2,1)S(1)}, u32[]{:S(2)}, u32[]{:S(2)}) async-start(bf16[8,144,128]{2,1,0:T(8,128)(2,1)} %get-tuple-element.203.refs_8_), calls=%async_computation | async-start | bytes 589824 | tf_op jit(solution)/shard_map/all_to_all | solution.py:1173
  47.9 6.2 %act_grad.1.agrad_ref.agrad_in = f32[128,3072]{1,0:T(8,128)} custom-call(bf16[3072,1152]{1,0:T(8,128)(2,1)} %high_ref.1, f32[128,1152]{1,0:T(8,128)} %bitcast.12, f32[8,1152]{1,0:T(8,128)} %get-tuple-element.153.mod_ref.refs_20_), custom_call_target="tpu_custom_call" | custom-call | flops 5000000000 | bytes 5000000 | tf_op jit(solution)/shard_map/act_grad/pallas_call | solution.py:1121
  55.6 3.8 %middle.1 = (f32[128,1152]{1,0:T(8,128)}, f32[128,1152]{1,0:T(8,128)}, bf16[128,1152]{1,0:T(8,128)(2,1)}) custom-call(bf16[8,144,128]{2,1,0:T(8,128)(2,1)} %copy-done.6, bf16[1152,1152]{1,0:T(8,128)(2,1)} %outw_ref.1, f32[128,1152]{1,0:T(8,128)} %bitcast.16, f32[8,1152]{1,0:T(8,128)} %get-tuple-element.153.mod_ref.refs_20_), custom_call_target="tpu_custom_call" | custom-call | flops 5000000000 | bytes 5000000 | tf_op jit(solution)/shard_map/middle/pallas_call | solution.py:1121
  60.6 1.5 collective-permute-start.17
  62.1 7.1 %mlp_first.1 = (bf16[128,1536]{1,0:T(8,128)(2,1)}, f32[128,1152]{1,0:T(8,128)}) custom-call(bf16[1152,6144]{1,0:T(8,128)(2,1)} %up_ref.3, bf16[1152,6144]{1,0:T(8,128)(2,1)} %up_ref.3, bf16[128,1152]{1,0:T(8,128)(2,1)} %get-tuple-element.155.hid_ref.refs_0_, f32[128,3072]{1,0:T(8,128)} %act_grad.1.agrad_ref.agrad_in), custom_call_target="tpu_custom_call" | custom-call | flops 7000000000 | bytes 7000000 | tf_op jit(solution)/shard_map/mlp_first/pallas_call | solution.py:1121
  69.8 1.4 collective-permute-start.18
  71.8 10.0 %mlp.1 = (bf16[128,1536]{1,0:T(8,128)(2,1)}, f32[128,1152]{1,0:T(8,128)}, bf16[128,1152]{1,0:T(8,128)(2,1)}, bf16[8,144,128]{2,1,0:T(8,128)(2,1)}, f32[8,1152]{1,0:T(8,128)}) custom-call(bf16[1152,6144]{1,0:T(8,128)(2,1)} %up_ref.3, bf16[1152,6144]{1,0:T(8,128)(2,1)} %up_ref.3, bf16[1152,1152]{1,0:T(8,128)(2,1)} %outw_ref.1, ...), custom_call_target="tpu_custom_call" | custom-call | flops 8000000000 | bytes 8000000 | tf_op jit(solution)/shard_map/mlp/pallas_call | solution.py:1121
  84.2 3.4 %all-to-all-start.1 = ((bf16[8,144,128]{2,1,0:T(8,128)(2,1)}), bf16[8,144,128]{2,1,0:T(8,128)(2,1)S(1)}, u32[]{:S(2)}, u32[]{:S(2)}) async-start(bf16[8,144,128]{2,1,0:T(8,128)(2,1)} %get-tuple-element.167), calls=%async_computation.1 | async-start | bytes 589824 | tf_op jit(solution)/shard_map/all_to_all | solution.py:1173
  88.5 13.6 %mlp_weights.1 = (bf16[864,384]{1,0:T(8,128)(2,1)}, bf16[864,384]{1,0:T(8,128)(2,1)}, bf16[864,384]{1,0:T(8,128)(2,1)}, bf16[864,384]{1,0:T(8,128)(2,1)}) custom-call(s32[2]{0:T(128)} %pad_add_fusion.scalars, bf16[128,1152]{1,0:T(8,128)(2,1)} %get-tuple-element.155.hid_ref.refs_0_, bf16[128,1152]{1,0:T(8,128)(2,1)} %copy-done.32, ...), custom_call_target="tpu_custom_call" | custom-call | flops 12000000000 | bytes 12000000 | tf_op jit(solution)/shard_map/mlp_weights/pallas_call | solution.py:1121
  102.2 3.7 %collective-permute-start.26 = (bf16[864,384]{1,0:T(8,128)(2,1)}, bf16[864,384]{1,0:T(8,128)(2,1)S(1)}, u32[]{:S(2)}, u32[]{:S(2)}) collective-permute-start(bf16[864,384]{1,0:T(8,128)(2,1)} %get-tuple-element.191), channel_id=1, source_target_pairs={{0,8},{24,16},{1,9},{25,17},{2,10},{26,18},{3,11},{27,19},{4,12},{... | collective-permute-start | bytes 1990664 | tf_op jit(solution)/shard_map/ppermute | solution.py:1177
  106.9 2.0 collective-permute-start.28
  109.4 12.7 %attend_back.1 = (bf16[8,432,128]{2,1,0:T(8,128)(2,1)}, f32[8,128]{1,0:T(8,128)}) custom-call(bf16[8,144,128]{2,1,0:T(8,128)(2,1)} %copy-done.5, bf16[6,1024,128]{2,1,0:T(8,128)(2,1)} %get-tuple-element.184.qkv_ref, f32[2,4,256]{2,1,0:T(4,128)} %get-tuple-element.185.log_ref, f32[2,128,1024]{2,1,0:T(8,128)} %get-tuple-element.186.mixed_ref, ...), custom_call_target="tpu_custom_call" | custom-call | flops 15000000512 | bytes 15000000 | tf_op jit(solution)/shard_map/attend_back/pallas_call | solution.py:1121
  122.3 2.3 %collective-permute-start.32 = (bf16[864,384]{1,0:T(8,128)(2,1)}, bf16[864,384]{1,0:T(8,128)(2,1)}, u32[]{:S(2)}, u32[]{:S(2)}) collective-permute-start(bf16[864,384]{1,0:T(8,128)(2,1)} %get-tuple-element.218), channel_id=1, source_target_pairs={{0,8},{8,0},{16,24},{24,16},{1,9},{9,1},{17,25},{25,17},{2,10},{10... | collective-permute-start | bytes 1990664 | tf_op jit(solution)/shard_map/ppermute | solution.py:1177
  124.7 3.8 %collective-permute-start.33 = (bf16[864,384]{1,0:T(8,128)(2,1)S(1)}, bf16[864,384]{1,0:T(8,128)(2,1)}, u32[]{:S(2)}, u32[]{:S(2)}) collective-permute-start(bf16[864,384]{1,0:T(8,128)(2,1)S(1)} %copy-done.2), channel_id=1, source_target_pairs={{0,16},{24,8},{1,17},{25,9},{2,18},{26,10},{3,19},{27,11},{4,20},{... | collective-permute-start | bytes 1990664 | tf_op jit(solution)/shard_map/ppermute | solution.py:1177
  128.5 3.8 %all-to-all-start.2 = ((bf16[8,432,128]{2,1,0:T(8,128)(2,1)}), bf16[8,432,128]{2,1,0:T(8,128)(2,1)S(1)}, u32[]{:S(2)}, u32[]{:S(2)}) async-start(bf16[8,432,128]{2,1,0:T(8,128)(2,1)} %get-tuple-element.202.back_ref), calls=%async_computation.2 | async-start | bytes 1769472 | tf_op jit(solution)/shard_map/all_to_all | solution.py:1173
  133.1 4.3 %qkv_weights.1 = bf16[8,144,512]{2,1,0:T(8,128)(2,1)} custom-call(bf16[1024,1152]{1,0:T(8,128)(2,1)} %get-tuple-element.201.hid_ref, bf16[8,432,128]{2,1,0:T(8,128)(2,1)} %get-tuple-element.202.back_ref), custom_call_target="tpu_custom_call" | custom-call | flops 5000000000 | bytes 5000000 | tf_op jit(solution)/shard_map/qkv_weights/pallas_call | solution.py:1121
  137.5 1.3 collective-permute-start.34
  138.8 4.7 %out_weights.1.ograd_ref = bf16[4,144,288]{2,1,0:T(8,128)(2,1)} custom-call(s32[2]{0:T(128)} %pad_add_fusion.scalars, bf16[128,1152]{1,0:T(8,128)(2,1)} %get-tuple-element.168.refs_0_, bf16[128,1152]{1,0:T(8,128)(2,1)} %copy-done.26, bf16[128,1152]{1,0:T(8,128)(2,1)} %copy-done.25, bf16[128,1152]{1,0:T(8,128)(2,1)} %copy-done.38, ...), custom_call_target="tpu_custom_call" | custom-call | flops 5000000000 | bytes 5000000 | tf_op jit(solution)/shard_map/out_weights/pallas_call | solution.py:1121
  143.5 2.0 all-to-all-done.2.back_ref
  145.5 3.6 %all-to-all-start.3 = ((bf16[8,144,512]{2,1,0:T(8,128)(2,1)}), bf16[8,144,512]{2,1,0:T(8,128)(2,1)S(1)}, u32[]{:S(2)}, u32[]{:S(2)}) async-start(bf16[8,144,512]{2,1,0:T(8,128)(2,1)} %qkv_weights.1), calls=%async_computation.3 | async-start | bytes 2359296 | tf_op jit(solution)/shard_map/all_to_all | solution.py:1173
  149.1 7.2 %input.1 = (f32[128,1152]{1,0:T(8,128)}, f32[8,1152]{1,0:T(8,128)}) custom-call(bf16[8,432,128]{2,1,0:T(8,128)(2,1)} %copy-done.1, bf16[1152,3456]{1,0:T(8,128)(2,1)} %weight_ref.3, f32[128,1152]{1,0:T(8,128)} %bitcast.17, f32[128,1152]{1,0:T(8,128)} %get-tuple-element.205.mgrad_ref, f32[8,1152]{1,0:T(8,128)} %get-tuple-element.153.mod_ref.refs_20_), custom_call_target="tpu_custom_call" | custom-call | flops 7000000000 | bytes 7000000 | tf_op jit(solution)/shard_map/input/pallas_call | solution.py:1121
  156.3 5.6 %mlp_out.1 = (f32[128,1152]{1,0:T(8,128)}, f32[32,8,128]{2,1,0:T(8,128)}) custom-call(bf16[128,1536]{1,0:T(8,128)(2,1)} %get-tuple-element.157.first_ref, bf16[128,1536]{1,0:T(8,128)(2,1)} %get-tuple-element.162.second_ref, bf16[3072,1152]{1,0:T(8,128)(2,1)} %high_ref.1, bf16[3072,1152]{1,0:T(8,128)(2,1)} %high_ref.1, ...), custom_call_target="tpu_custom_call" | custom-call | flops 5000000000 | bytes 5000000 | tf_op jit(solution)/shard_map/mlp_out/pallas_call | solution.py:1121
  161.9 3.4 %all-to-all-done.3.grad_ref = bf16[8,144,512]{2,1,0:T(8,128)(2,1)S(1)} async-done(((bf16[8,144,512]{2,1,0:T(8,128)(2,1)}), bf16[8,144,512]{2,1,0:T(8,128)(2,1)S(1)}, u32[]{:S(2)}, u32[]{:S(2)}) %all-to-all-start.3) | async-done | bytes 1179680 | tf_op jit(solution)/shard_map/all_to_all | solution.py:1173
  165.3 3.9 %all-to-all-start.4 = ((f32[32,8,128]{2,1,0:T(8,128)}), f32[32,8,128]{2,1,0:T(8,128)S(1)}, u32[]{:S(2)}, u32[]{:S(2)}) async-start(f32[32,8,128]{2,1,0:T(8,128)} %get-tuple-element.212), calls=%async_computation.4 | async-start | bytes 262144 | tf_op jit(solution)/shard_map/all_to_all | solution.py:1173
  169.3 3.9 %join.1 = (bf16[144,1152]{1,0:T(8,128)(2,1)}, bf16[144,1152]{1,0:T(8,128)(2,1)}, bf16[144,1152]{1,0:T(8,128)(2,1)}, bf16[144,1152]{1,0:T(8,128)(2,1)}) custom-call(s32[2]{0:T(128)} %pad_add_fusion.scalars, bf16[8,144,512]{2,1,0:T(8,128)(2,1)} %copy-done, bf16[4,144,288]{2,1,0:T(8,128)(2,1)} %out_weights.1.ograd_ref), custom_call_target="tpu_custom_call" | custom-call | flops 5000000000 | bytes 5000000 | tf_op jit(solution)/shard_map/join/pallas_call | solution.py:1121
  173.2 3.7 %collective-permute-start.35 = (bf16[144,1152]{1,0:T(8,128)(2,1)}, bf16[144,1152]{1,0:T(8,128)(2,1)S(1)}, u32[]{:S(2)}, u32[]{:S(2)}) collective-permute-start(bf16[144,1152]{1,0:T(8,128)(2,1)} %get-tuple-element.223), channel_id=1, source_target_pairs={{0,8},{24,16},{1,9},{25,17},{2,10},{26,18},{3,11},{27,19},{4,12},{... | collective-permute-start | bytes 995336 | tf_op jit(solution)/shard_map/ppermute | solution.py:1177
  178.6 3.5 %tail.1 = (f32[288,864]{1,0:T(8,128)}, f32[864]{0:T(1024)}, f32[72]{0:T(128)}, f32[72]{0:T(128)}, f32[8,8,288]{2,1,0:T(8,128)}, /*index=5*/f32[8,288]{1,0:T(8,128)}, f32[8,128]{1,0:T(8,128)}) custom-call(f32[32,8,128]{2,1,0:T(8,128)} %copy-done.7, f32[32,288]{1,0:T(8,128)} %get-tuple-element.213.table_ref, bf16[864,288]{1,0:T(8,128)(2,1)} %get-tuple-element.214.weight_ref), custom_call_target="tpu_custom_call" | custom-call | flops 5000000000 | bytes 5000000 | tf_op jit(solution)/shard_map/tail/pallas_call | solution.py:1121
  182.1 3.4 %all-to-all-start.5 = ((f32[8,8,288]{2,1,0:T(8,128)}), f32[8,8,288]{2,1,0:T(8,128)S(1)}, u32[]{:S(2)}, u32[]{:S(2)}) async-start(f32[8,8,288]{2,1,0:T(8,128)} %get-tuple-element.215), calls=%async_computation.5 | async-start | bytes 196608 | tf_op jit(solution)/shard_map/all_to_all | solution.py:1173
  185.5 2.1 collective-permute-start.40
  187.6 2.8 %collective-permute-start.41 = (bf16[144,1152]{1,0:T(8,128)(2,1)S(1)}, bf16[144,1152]{1,0:T(8,128)(2,1)S(1)}, u32[]{:S(2)}, u32[]{:S(2)}) collective-permute-start(bf16[144,1152]{1,0:T(8,128)(2,1)S(1)} %copy-done.4), channel_id=1, source_target_pairs={{0,16},{24,8},{1,17},{25,9},{2,18},{26,10},{3,19},{27,11},{4,20},{... | collective-permute-start | bytes 995336 | tf_op jit(solution)/shard_map/ppermute | solution.py:1177
  190.5 1.3 collective-permute-start.37
  191.8 4.2 %turn.1 = (bf16[8,144,192]{2,1,0:T(8,128)(2,1)}, bf16[288,192]{1,0:T(8,128)(2,1)}, bf16[288,192]{1,0:T(8,128)(2,1)}) custom-call(s32[2]{0:T(128)} %pad_add_fusion.scalars, bf16[864,384]{1,0:T(8,128)(2,1)} %get-tuple-element.216.refs_0_, bf16[864,384]{1,0:T(8,128)(2,1)} %copy-done.11, bf16[864,384]{1,0:T(8,128)(2,1)} %collective-permute-done.32.refs_2_, ...), custom_call_target="tpu_custom_call" | custom-call | flops 5000000000 | bytes 5000000 | tf_op jit(solution)/shard_map/turn/pallas_call | solution.py:1121
  196.0 4.2 %all-to-all-start.6 = ((bf16[8,144,192]{2,1,0:T(8,128)(2,1)}), bf16[8,144,192]{2,1,0:T(8,128)(2,1)S(1)}, u32[]{:S(2)}, u32[]{:S(2)}) async-start(bf16[8,144,192]{2,1,0:T(8,128)(2,1)} %get-tuple-element.226), calls=%async_computation.6 | async-start | bytes 1179648 | tf_op jit(solution)/shard_map/all_to_all | solution.py:1173
  200.2 1.6 collective-permute-start.38
  201.8 2.5 %collective-permute-start.39 = (bf16[288,192]{1,0:T(8,128)(2,1)}, bf16[288,192]{1,0:T(8,128)(2,1)S(1)}, u32[]{:S(2)}, u32[]{:S(2)}) collective-permute-start(bf16[288,192]{1,0:T(8,128)(2,1)} %get-tuple-element.238), channel_id=1, source_target_pairs={{0,4},{1,0},{2,5},{3,1},{4,6},{5,2},{6,7},{7,3},{8,12},{9,8},{10,1... | collective-permute-start | bytes 331784 | tf_op jit(solution)/shard_map/ppermute | solution.py:1541
  204.3 5.8 %collective-permute-done.37.refs_4_ = bf16[144,1152]{1,0:T(8,128)(2,1)S(1)} collective-permute-done((bf16[144,1152]{1,0:T(8,128)(2,1)S(1)}, bf16[144,1152]{1,0:T(8,128)(2,1)S(1)}, u32[]{:S(2)}, u32[]{:S(2)}) %collective-permute-start.37) | collective-permute-done | bytes 331808 | tf_op jit(solution)/shard_map/ppermute | solution.py:1177
  210.1 2.2 %table.1 = f32[4,288]{1,0:T(4,128)} custom-call(s32[2]{0:T(128)} %pad_add_fusion.scalars, f32[8,8,288]{2,1,0:T(8,128)} %copy-done.9, f32[8,288]{1,0:T(8,128)} %get-tuple-element.231.cond_ref, f32[8,128]{1,0:T(8,128)} %get-tuple-element.232.bucket_ref), custom_call_target="tpu_custom_call" | custom-call | flops 5000000000 | bytes 5000000 | tf_op jit(solution)/shard_map/table/pallas_call | solution.py:1121
  213.6 3.9 %lay.1 = (f32[144,1536]{1,0:T(8,128)}, f32[288,384]{1,0:T(8,128)}, f32[144,864]{1,0:T(8,128)}, f32[144,288]{1,0:T(8,128)}) custom-call(s32[2]{0:T(128)} %pad_add_fusion.scalars, bf16[8,144,192]{2,1,0:T(8,128)(2,1)} %copy-done.3, bf16[288,192]{1,0:T(8,128)(2,1)} %copy-done.45, bf16[288,192]{1,0:T(8,128)(2,1)} %copy-done.46, ...), custom_call_target="tpu_custom_call" | custom-call | flops 5000000000 | bytes 5000000 | tf_op jit(solution)/shard_map/lay/pallas_call | solution.py:1121
  (170 shorter events, 17.5 us)
Async XLA Ops:
  4.8 10.9 %collective-permute-start = (bf16[144,1152]{1,0:T(8,128)(2,1)}, bf16[144,1152]{1,0:T(8,128)(2,1)S(1)}, u32[]{:S(2)}, u32[]{:S(2)}) collective-permute-start(bf16[144,1152]{1,0:T(8,128)(2,1)} %get-tuple-element.130.refs_0_), channel_id=1, source_target_pairs={{0,1},{1,0},{2,3},{3,2},{4,5},{5,4},{6,7},{7,6},{8,9},{9,8},{10,11... | collective-permute-start | bytes 995336 | tf_op jit(solution)/shard_map/ppermute | solution.py:1150
  7.7 9.5 %collective-permute-start.1 = (bf16[144,1152]{1,0:T(8,128)(2,1)}, bf16[144,1152]{1,0:T(8,128)(2,1)S(1)}, u32[]{:S(2)}, u32[]{:S(2)}) collective-permute-start(bf16[144,1152]{1,0:T(8,128)(2,1)} %get-tuple-element.130.refs_0_), channel_id=1, source_target_pairs={{0,4},{1,5},{2,6},{3,7},{4,0},{5,1},{6,2},{7,3},{8,12},{9,13},{10,... | collective-permute-start | bytes 995336 | tf_op jit(solution)/shard_map/ppermute | solution.py:1150
  17.2 2.8 %collective-permute-start.3 = (bf16[144,1152]{1,0:T(8,128)(2,1)S(1)}, bf16[144,1152]{1,0:T(8,128)(2,1)S(1)}, u32[]{:S(2)}, u32[]{:S(2)}) collective-permute-start(bf16[144,1152]{1,0:T(8,128)(2,1)S(1)} %collective-permute-done.refs_1_), channel_id=1, source_target_pairs={{0,2},{1,3},{2,0},{3,1},{4,6},{5,7},{6,4},{7,5},{8,10},{9,11},{10,... | collective-permute-start | bytes 995336 | tf_op jit(solution)/shard_map/ppermute | solution.py:1150
  17.2 10.8 %collective-permute-start.2 = (bf16[144,1152]{1,0:T(8,128)(2,1)S(1)}, bf16[144,1152]{1,0:T(8,128)(2,1)S(1)}, u32[]{:S(2)}, u32[]{:S(2)}) collective-permute-start(bf16[144,1152]{1,0:T(8,128)(2,1)S(1)} %copy-done.12), channel_id=1, source_target_pairs={{0,2},{1,3},{2,0},{3,1},{4,6},{5,7},{6,4},{7,5},{8,10},{9,11},{10,... | collective-permute-start | bytes 995336 | tf_op jit(solution)/shard_map/ppermute | solution.py:1150
  17.7 7.7 %collective-permute-start.6 = (bf16[144,1152]{1,0:T(8,128)(2,1)S(1)}, bf16[144,1152]{1,0:T(8,128)(2,1)S(1)}, u32[]{:S(2)}, u32[]{:S(2)}) collective-permute-start(bf16[144,1152]{1,0:T(8,128)(2,1)S(1)} %collective-permute-done.1.refs_4_), channel_id=1, source_target_pairs={{0,2},{1,3},{2,0},{3,1},{4,6},{5,7},{6,4},{7,5},{8,10},{9,11},{10,... | collective-permute-start | bytes 995336 | tf_op jit(solution)/shard_map/ppermute | solution.py:1150
  17.9 7.5 %collective-permute-start.5 = (bf16[80,1152]{1,0:T(8,128)(2,1)S(1)}, bf16[80,1152]{1,0:T(8,128)(2,1)S(1)}, u32[]{:S(2)}, u32[]{:S(2)}) collective-permute-start(bf16[80,1152]{1,0:T(8,128)(2,1)S(1)} %slice.7), channel_id=1, source_target_pairs={{0,1},{1,0},{2,3},{3,2},{4,5},{5,4},{6,7},{7,6},{8,9},{9,8},{10,11... | collective-permute-start | bytes 552968 | tf_op jit(solution)/shard_map/ppermute | solution.py:1150
  18.3 7.0 %collective-permute-start.4 = (bf16[64,1152]{1,0:T(8,128)(2,1)S(1)}, bf16[64,1152]{1,0:T(8,128)(2,1)S(1)}, u32[]{:S(2)}, u32[]{:S(2)}) collective-permute-start(bf16[64,1152]{1,0:T(8,128)(2,1)S(1)} %slice.6), channel_id=1, source_target_pairs={{0,4},{1,5},{2,6},{3,7},{4,0},{5,1},{6,2},{7,3},{8,12},{9,13},{10,... | collective-permute-start | bytes 442376 | tf_op jit(solution)/shard_map/ppermute | solution.py:1150
  25.4 2.7 %collective-permute-start.8 = (bf16[80,1152]{1,0:T(8,128)(2,1)S(1)}, bf16[80,1152]{1,0:T(8,128)(2,1)S(1)}, u32[]{:S(2)}, u32[]{:S(2)}) collective-permute-start(bf16[80,1152]{1,0:T(8,128)(2,1)S(1)} %collective-permute-done.5.refs_6_), channel_id=1, source_target_pairs={{0,2},{1,3},{2,0},{3,1},{4,6},{5,7},{6,4},{7,5},{8,10},{9,11},{10,... | collective-permute-start | bytes 552968 | tf_op jit(solution)/shard_map/ppermute | solution.py:1150
  26.0 16.2 %collective-permute-start.10 = (bf16[128,1152]{1,0:T(8,128)(2,1)S(1)}, bf16[128,1152]{1,0:T(8,128)(2,1)S(1)}, u32[]{:S(2)}, u32[]{:S(2)}) collective-permute-start(bf16[128,1152]{1,0:T(8,128)(2,1)S(1)} %copy-done.21), channel_id=1, source_target_pairs={{0,1},{1,0},{2,3},{3,2},{4,5},{5,4},{6,7},{7,6},{8,9},{9,8},{10,11... | collective-permute-start | bytes 884744 | tf_op jit(solution)/shard_map/ppermute | solution.py:1150
  27.5 14.7 %collective-permute-start.11 = (bf16[128,1152]{1,0:T(8,128)(2,1)S(1)}, bf16[128,1152]{1,0:T(8,128)(2,1)S(1)}, u32[]{:S(2)}, u32[]{:S(2)}) collective-permute-start(bf16[128,1152]{1,0:T(8,128)(2,1)S(1)} %copy-done.21), channel_id=1, source_target_pairs={{0,4},{1,5},{2,6},{3,7},{4,0},{5,1},{6,2},{7,3},{8,12},{9,13},{10,... | collective-permute-start | bytes 884744 | tf_op jit(solution)/shard_map/ppermute | solution.py:1150
  28.0 14.2 %collective-permute-start.9 = (bf16[128,1152]{1,0:T(8,128)(2,1)S(1)}, bf16[128,1152]{1,0:T(8,128)(2,1)S(1)}, u32[]{:S(2)}, u32[]{:S(2)}) collective-permute-start(bf16[128,1152]{1,0:T(8,128)(2,1)S(1)} %copy-done.21), channel_id=1, source_target_pairs={{0,2},{1,3},{2,0},{3,1},{4,6},{5,7},{6,4},{7,5},{8,10},{9,11},{10,... | collective-permute-start | bytes 884744 | tf_op jit(solution)/shard_map/ppermute | solution.py:1150
  42.2 12.6 %collective-permute-start.12 = (bf16[128,1152]{1,0:T(8,128)(2,1)S(1)}, bf16[128,1152]{1,0:T(8,128)(2,1)S(1)}, u32[]{:S(2)}, u32[]{:S(2)}) collective-permute-start(bf16[128,1152]{1,0:T(8,128)(2,1)S(1)} %collective-permute-done.10.refs_9_), channel_id=1, source_target_pairs={{0,4},{1,5},{2,6},{3,7},{4,0},{5,1},{6,2},{7,3},{8,12},{9,13},{10,... | collective-permute-start | bytes 884744 | tf_op jit(solution)/shard_map/ppermute | solution.py:1150
  43.8 11.0 %collective-permute-start.13 = (bf16[128,1152]{1,0:T(8,128)(2,1)S(1)}, bf16[128,1152]{1,0:T(8,128)(2,1)S(1)}, u32[]{:S(2)}, u32[]{:S(2)}) collective-permute-start(bf16[128,1152]{1,0:T(8,128)(2,1)S(1)} %collective-permute-done.10.refs_9_), channel_id=1, source_target_pairs={{0,2},{1,3},{2,0},{3,1},{4,6},{5,7},{6,4},{7,5},{8,10},{9,11},{10,... | collective-permute-start | bytes 884744 | tf_op jit(solution)/shard_map/ppermute | solution.py:1150
  43.9 10.9 %collective-permute-start.14 = (bf16[128,1152]{1,0:T(8,128)(2,1)S(1)}, bf16[128,1152]{1,0:T(8,128)(2,1)S(1)}, u32[]{:S(2)}, u32[]{:S(2)}) collective-permute-start(bf16[128,1152]{1,0:T(8,128)(2,1)S(1)} %collective-permute-done.11.refs_12_), channel_id=1, source_target_pairs={{0,2},{1,3},{2,0},{3,1},{4,6},{5,7},{6,4},{7,5},{8,10},{9,11},{10,... | collective-permute-start | bytes 884744 | tf_op jit(solution)/shard_map/ppermute | solution.py:1150
  44.3 10.5 %all-to-all-start = ((bf16[8,144,128]{2,1,0:T(8,128)(2,1)}), bf16[8,144,128]{2,1,0:T(8,128)(2,1)S(1)}, u32[]{:S(2)}, u32[]{:S(2)}) async-start(bf16[8,144,128]{2,1,0:T(8,128)(2,1)} %get-tuple-element.203.refs_8_), calls=%async_computation | async-start | bytes 589824 | tf_op jit(solution)/shard_map/all_to_all | solution.py:1173
  59.4 9.8 %collective-permute-start.15 = (bf16[128,1152]{1,0:T(8,128)(2,1)}, bf16[128,1152]{1,0:T(8,128)(2,1)S(1)}, u32[]{:S(2)}, u32[]{:S(2)}) collective-permute-start(bf16[128,1152]{1,0:T(8,128)(2,1)} %get-tuple-element.155.hid_ref.refs_0_), channel_id=1, source_target_pairs={{0,2},{1,3},{2,0},{3,1},{4,6},{5,7},{6,4},{7,5},{8,10},{9,11},{10,... | collective-permute-start | bytes 884744 | tf_op jit(solution)/shard_map/ppermute | solution.py:1150
  59.4 9.8 %collective-permute-start.16 = (bf16[128,1152]{1,0:T(8,128)(2,1)}, bf16[128,1152]{1,0:T(8,128)(2,1)S(1)}, u32[]{:S(2)}, u32[]{:S(2)}) collective-permute-start(bf16[128,1152]{1,0:T(8,128)(2,1)} %get-tuple-element.155.hid_ref.refs_0_), channel_id=1, source_target_pairs={{0,1},{1,0},{2,3},{3,2},{4,5},{5,4},{6,7},{7,6},{8,9},{9,8},{10,11... | collective-permute-start | bytes 884744 | tf_op jit(solution)/shard_map/ppermute | solution.py:1150
  60.6 9.3 %collective-permute-start.17 = (bf16[128,1152]{1,0:T(8,128)(2,1)}, bf16[128,1152]{1,0:T(8,128)(2,1)S(1)}, u32[]{:S(2)}, u32[]{:S(2)}) collective-permute-start(bf16[128,1152]{1,0:T(8,128)(2,1)} %get-tuple-element.155.hid_ref.refs_0_), channel_id=1, source_target_pairs={{0,4},{1,5},{2,6},{3,7},{4,0},{5,1},{6,2},{7,3},{8,12},{9,13},{10,... | collective-permute-start | bytes 884744 | tf_op jit(solution)/shard_map/ppermute | solution.py:1150
  69.1 18.5 %collective-permute-start.25 = (bf16[128,1152]{1,0:T(8,128)(2,1)S(1)}, bf16[128,1152]{1,0:T(8,128)(2,1)S(1)}, u32[]{:S(2)}, u32[]{:S(2)}) collective-permute-start(bf16[128,1152]{1,0:T(8,128)(2,1)S(1)} %collective-permute-done.12.refs_13_), channel_id=1, source_target_pairs={{0,2},{1,3},{2,0},{3,1},{4,6},{5,7},{6,4},{7,5},{8,10},{9,11},{10,... | collective-permute-start | bytes 884744 | tf_op jit(solution)/shard_map/ppermute | solution.py:1150
  69.8 12.0 %collective-permute-start.18 = (bf16[128,1152]{1,0:T(8,128)(2,1)S(1)}, bf16[128,1152]{1,0:T(8,128)(2,1)S(1)}, u32[]{:S(2)}, u32[]{:S(2)}) collective-permute-start(bf16[128,1152]{1,0:T(8,128)(2,1)S(1)} %collective-permute-done.16.refs_1_), channel_id=1, source_target_pairs={{0,4},{1,5},{2,6},{3,7},{4,0},{5,1},{6,2},{7,3},{8,12},{9,13},{10,... | collective-permute-start | bytes 884744 | tf_op jit(solution)/shard_map/ppermute | solution.py:1150
  71.2 10.6 %collective-permute-start.19 = (bf16[128,1152]{1,0:T(8,128)(2,1)S(1)}, bf16[128,1152]{1,0:T(8,128)(2,1)S(1)}, u32[]{:S(2)}, u32[]{:S(2)}) collective-permute-start(bf16[128,1152]{1,0:T(8,128)(2,1)S(1)} %collective-permute-done.16.refs_1_), channel_id=1, source_target_pairs={{0,2},{1,3},{2,0},{3,1},{4,6},{5,7},{6,4},{7,5},{8,10},{9,11},{10,... | collective-permute-start | bytes 884744 | tf_op jit(solution)/shard_map/ppermute | solution.py:1150
  71.3 10.6 %collective-permute-start.20 = (bf16[128,1152]{1,0:T(8,128)(2,1)S(1)}, bf16[128,1152]{1,0:T(8,128)(2,1)S(1)}, u32[]{:S(2)}, u32[]{:S(2)}) collective-permute-start(bf16[128,1152]{1,0:T(8,128)(2,1)S(1)} %collective-permute-done.17.refs_4_), channel_id=1, source_target_pairs={{0,2},{1,3},{2,0},{3,1},{4,6},{5,7},{6,4},{7,5},{8,10},{9,11},{10,... | collective-permute-start | bytes 884744 | tf_op jit(solution)/shard_map/ppermute | solution.py:1150
  81.9 5.8 %collective-permute-start.24 = (bf16[128,1152]{1,0:T(8,128)(2,1)S(1)}, bf16[128,1152]{1,0:T(8,128)(2,1)S(1)}, u32[]{:S(2)}, u32[]{:S(2)}) collective-permute-start(bf16[128,1152]{1,0:T(8,128)(2,1)S(1)} %collective-permute-done.18.refs_5_), channel_id=1, source_target_pairs={{0,2},{1,3},{2,0},{3,1},{4,6},{5,7},{6,4},{7,5},{8,10},{9,11},{10,... | collective-permute-start | bytes 884744 | tf_op jit(solution)/shard_map/ppermute | solution.py:1150
  82.6 19.5 %collective-permute-start.21 = (bf16[128,1152]{1,0:T(8,128)(2,1)}, bf16[128,1152]{1,0:T(8,128)(2,1)S(1)}, u32[]{:S(2)}, u32[]{:S(2)}) collective-permute-start(bf16[128,1152]{1,0:T(8,128)(2,1)} %get-tuple-element.168.refs_0_), channel_id=1, source_target_pairs={{0,2},{1,3},{2,0},{3,1},{4,6},{5,7},{6,4},{7,5},{8,10},{9,11},{10,... | collective-permute-start | bytes 884744 | tf_op jit(solution)/shard_map/ppermute | solution.py:1150
  82.7 19.5 %collective-permute-start.22 = (bf16[128,1152]{1,0:T(8,128)(2,1)}, bf16[128,1152]{1,0:T(8,128)(2,1)S(1)}, u32[]{:S(2)}, u32[]{:S(2)}) collective-permute-start(bf16[128,1152]{1,0:T(8,128)(2,1)} %get-tuple-element.168.refs_0_), channel_id=1, source_target_pairs={{0,1},{1,0},{2,3},{3,2},{4,5},{5,4},{6,7},{7,6},{8,9},{9,8},{10,11... | collective-permute-start | bytes 884744 | tf_op jit(solution)/shard_map/ppermute | solution.py:1150
  83.7 18.5 %collective-permute-start.23 = (bf16[128,1152]{1,0:T(8,128)(2,1)}, bf16[128,1152]{1,0:T(8,128)(2,1)S(1)}, u32[]{:S(2)}, u32[]{:S(2)}) collective-permute-start(bf16[128,1152]{1,0:T(8,128)(2,1)} %get-tuple-element.168.refs_0_), channel_id=1, source_target_pairs={{0,4},{1,5},{2,6},{3,7},{4,0},{5,1},{6,2},{7,3},{8,12},{9,13},{10,... | collective-permute-start | bytes 884744 | tf_op jit(solution)/shard_map/ppermute | solution.py:1150
  84.2 18.0 %all-to-all-start.1 = ((bf16[8,144,128]{2,1,0:T(8,128)(2,1)}), bf16[8,144,128]{2,1,0:T(8,128)(2,1)S(1)}, u32[]{:S(2)}, u32[]{:S(2)}) async-start(bf16[8,144,128]{2,1,0:T(8,128)(2,1)} %get-tuple-element.167), calls=%async_computation.1 | async-start | bytes 589824 | tf_op jit(solution)/shard_map/all_to_all | solution.py:1173
  102.2 20.0 %collective-permute-start.26 = (bf16[864,384]{1,0:T(8,128)(2,1)}, bf16[864,384]{1,0:T(8,128)(2,1)S(1)}, u32[]{:S(2)}, u32[]{:S(2)}) collective-permute-start(bf16[864,384]{1,0:T(8,128)(2,1)} %get-tuple-element.191), channel_id=1, source_target_pairs={{0,8},{24,16},{1,9},{25,17},{2,10},{26,18},{3,11},{27,19},{4,12},{... | collective-permute-start | bytes 1990664 | tf_op jit(solution)/shard_map/ppermute | solution.py:1177
  106.0 16.3 %collective-permute-start.27 = (bf16[864,384]{1,0:T(8,128)(2,1)}, bf16[864,384]{1,0:T(8,128)(2,1)S(1)}, u32[]{:S(2)}, u32[]{:S(2)}) collective-permute-start(bf16[864,384]{1,0:T(8,128)(2,1)} %get-tuple-element.191), channel_id=1, source_target_pairs={{8,16},{16,8},{9,17},{17,9},{10,18},{18,10},{11,19},{19,11},{12,20... | collective-permute-start | bytes 1990664 | tf_op jit(solution)/shard_map/ppermute | solution.py:1177
  106.9 15.3 %collective-permute-start.28 = (bf16[128,1152]{1,0:T(8,128)(2,1)S(1)}, bf16[128,1152]{1,0:T(8,128)(2,1)}, u32[]{:S(2)}, u32[]{:S(2)}) collective-permute-start(bf16[128,1152]{1,0:T(8,128)(2,1)S(1)} %collective-permute-done.22.refs_1_), channel_id=1, source_target_pairs={{0,4},{1,5},{2,6},{3,7},{4,0},{5,1},{6,2},{7,3},{8,12},{9,13},{10,... | collective-permute-start | bytes 884744 | tf_op jit(solution)/shard_map/ppermute | solution.py:1150
  108.9 13.3 %collective-permute-start.29 = (bf16[128,1152]{1,0:T(8,128)(2,1)S(1)}, bf16[128,1152]{1,0:T(8,128)(2,1)S(1)}, u32[]{:S(2)}, u32[]{:S(2)}) collective-permute-start(bf16[128,1152]{1,0:T(8,128)(2,1)S(1)} %collective-permute-done.22.refs_1_), channel_id=1, source_target_pairs={{0,2},{1,3},{2,0},{3,1},{4,6},{5,7},{6,4},{7,5},{8,10},{9,11},{10,... | collective-permute-start | bytes 884744 | tf_op jit(solution)/shard_map/ppermute | solution.py:1150
  108.9 13.3 %collective-permute-start.30 = (bf16[128,1152]{1,0:T(8,128)(2,1)S(1)}, bf16[128,1152]{1,0:T(8,128)(2,1)S(1)}, u32[]{:S(2)}, u32[]{:S(2)}) collective-permute-start(bf16[128,1152]{1,0:T(8,128)(2,1)S(1)} %collective-permute-done.23.refs_4_), channel_id=1, source_target_pairs={{0,2},{1,3},{2,0},{3,1},{4,6},{5,7},{6,4},{7,5},{8,10},{9,11},{10,... | collective-permute-start | bytes 884744 | tf_op jit(solution)/shard_map/ppermute | solution.py:1150
  122.2 10.1 %collective-permute-start.31 = (bf16[128,1152]{1,0:T(8,128)(2,1)}, bf16[128,1152]{1,0:T(8,128)(2,1)S(1)}, u32[]{:S(2)}, u32[]{:S(2)}) collective-permute-start(bf16[128,1152]{1,0:T(8,128)(2,1)} %collective-permute-done.28.refs_5_), channel_id=1, source_target_pairs={{0,2},{1,3},{2,0},{3,1},{4,6},{5,7},{6,4},{7,5},{8,10},{9,11},{10,... | collective-permute-start | bytes 884744 | tf_op jit(solution)/shard_map/ppermute | solution.py:1150
  122.3 69.5 %collective-permute-start.32 = (bf16[864,384]{1,0:T(8,128)(2,1)}, bf16[864,384]{1,0:T(8,128)(2,1)}, u32[]{:S(2)}, u32[]{:S(2)}) collective-permute-start(bf16[864,384]{1,0:T(8,128)(2,1)} %get-tuple-element.218), channel_id=1, source_target_pairs={{0,8},{8,0},{16,24},{24,16},{1,9},{9,1},{17,25},{25,17},{2,10},{10... | collective-permute-start | bytes 1990664 | tf_op jit(solution)/shard_map/ppermute | solution.py:1177
  124.7 67.2 %collective-permute-start.33 = (bf16[864,384]{1,0:T(8,128)(2,1)S(1)}, bf16[864,384]{1,0:T(8,128)(2,1)}, u32[]{:S(2)}, u32[]{:S(2)}) collective-permute-start(bf16[864,384]{1,0:T(8,128)(2,1)S(1)} %copy-done.2), channel_id=1, source_target_pairs={{0,16},{24,8},{1,17},{25,9},{2,18},{26,10},{3,19},{27,11},{4,20},{... | collective-permute-start | bytes 1990664 | tf_op jit(solution)/shard_map/ppermute | solution.py:1177
  128.5 17.0 %all-to-all-start.2 = ((bf16[8,432,128]{2,1,0:T(8,128)(2,1)}), bf16[8,432,128]{2,1,0:T(8,128)(2,1)S(1)}, u32[]{:S(2)}, u32[]{:S(2)}) async-start(bf16[8,432,128]{2,1,0:T(8,128)(2,1)} %get-tuple-element.202.back_ref), calls=%async_computation.2 | async-start | bytes 1769472 | tf_op jit(solution)/shard_map/all_to_all | solution.py:1173
  137.5 47.9 %collective-permute-start.34 = (bf16[864,384]{1,0:T(8,128)(2,1)S(1)}, bf16[864,384]{1,0:T(8,128)(2,1)}, u32[]{:S(2)}, u32[]{:S(2)}) collective-permute-start(bf16[864,384]{1,0:T(8,128)(2,1)S(1)} %add_convert_fusion), channel_id=1, source_target_pairs={{8,24},{16,0},{9,25},{17,1},{10,26},{18,2},{11,27},{19,3},{12,28},... | collective-permute-start | bytes 1990664 | tf_op jit(solution)/shard_map/ppermute | solution.py:1177
  145.5 19.8 %all-to-all-start.3 = ((bf16[8,144,512]{2,1,0:T(8,128)(2,1)}), bf16[8,144,512]{2,1,0:T(8,128)(2,1)S(1)}, u32[]{:S(2)}, u32[]{:S(2)}) async-start(bf16[8,144,512]{2,1,0:T(8,128)(2,1)} %qkv_weights.1), calls=%async_computation.3 | async-start | bytes 2359296 | tf_op jit(solution)/shard_map/all_to_all | solution.py:1173
  165.3 12.5 %all-to-all-start.4 = ((f32[32,8,128]{2,1,0:T(8,128)}), f32[32,8,128]{2,1,0:T(8,128)S(1)}, u32[]{:S(2)}, u32[]{:S(2)}) async-start(f32[32,8,128]{2,1,0:T(8,128)} %get-tuple-element.212), calls=%async_computation.4 | async-start | bytes 262144 | tf_op jit(solution)/shard_map/all_to_all | solution.py:1173
  173.2 14.4 %collective-permute-start.35 = (bf16[144,1152]{1,0:T(8,128)(2,1)}, bf16[144,1152]{1,0:T(8,128)(2,1)S(1)}, u32[]{:S(2)}, u32[]{:S(2)}) collective-permute-start(bf16[144,1152]{1,0:T(8,128)(2,1)} %get-tuple-element.223), channel_id=1, source_target_pairs={{0,8},{24,16},{1,9},{25,17},{2,10},{26,18},{3,11},{27,19},{4,12},{... | collective-permute-start | bytes 995336 | tf_op jit(solution)/shard_map/ppermute | solution.py:1177
  176.9 13.5 %collective-permute-start.36 = (bf16[144,1152]{1,0:T(8,128)(2,1)}, bf16[144,1152]{1,0:T(8,128)(2,1)S(1)}, u32[]{:S(2)}, u32[]{:S(2)}) collective-permute-start(bf16[144,1152]{1,0:T(8,128)(2,1)} %get-tuple-element.223), channel_id=1, source_target_pairs={{8,16},{16,8},{9,17},{17,9},{10,18},{18,10},{11,19},{19,11},{12,20... | collective-permute-start | bytes 995336 | tf_op jit(solution)/shard_map/ppermute | solution.py:1177
  182.1 13.9 %all-to-all-start.5 = ((f32[8,8,288]{2,1,0:T(8,128)}), f32[8,8,288]{2,1,0:T(8,128)S(1)}, u32[]{:S(2)}, u32[]{:S(2)}) async-start(f32[8,8,288]{2,1,0:T(8,128)} %get-tuple-element.215), calls=%async_computation.5 | async-start | bytes 196608 | tf_op jit(solution)/shard_map/all_to_all | solution.py:1173
  185.5 26.9 %collective-permute-start.40 = (bf16[144,1152]{1,0:T(8,128)(2,1)S(1)}, bf16[144,1152]{1,0:T(8,128)(2,1)S(1)}, u32[]{:S(2)}, u32[]{:S(2)}) collective-permute-start(bf16[144,1152]{1,0:T(8,128)(2,1)S(1)} %copy-done.14), channel_id=1, source_target_pairs={{0,8},{8,0},{16,24},{24,16},{1,9},{9,1},{17,25},{25,17},{2,10},{10... | collective-permute-start | bytes 995336 | tf_op jit(solution)/shard_map/ppermute | solution.py:1177
  187.6 24.8 %collective-permute-start.41 = (bf16[144,1152]{1,0:T(8,128)(2,1)S(1)}, bf16[144,1152]{1,0:T(8,128)(2,1)S(1)}, u32[]{:S(2)}, u32[]{:S(2)}) collective-permute-start(bf16[144,1152]{1,0:T(8,128)(2,1)S(1)} %copy-done.4), channel_id=1, source_target_pairs={{0,16},{24,8},{1,17},{25,9},{2,18},{26,10},{3,19},{27,11},{4,20},{... | collective-permute-start | bytes 995336 | tf_op jit(solution)/shard_map/ppermute | solution.py:1177
  190.5 19.6 %collective-permute-start.37 = (bf16[144,1152]{1,0:T(8,128)(2,1)S(1)}, bf16[144,1152]{1,0:T(8,128)(2,1)S(1)}, u32[]{:S(2)}, u32[]{:S(2)}) collective-permute-start(bf16[144,1152]{1,0:T(8,128)(2,1)S(1)} %add_convert_fusion.1), channel_id=1, source_target_pairs={{8,24},{16,0},{9,25},{17,1},{10,26},{18,2},{11,27},{19,3},{12,28},... | collective-permute-start | bytes 995336 | tf_op jit(solution)/shard_map/ppermute | solution.py:1177
  196.0 16.3 %all-to-all-start.6 = ((bf16[8,144,192]{2,1,0:T(8,128)(2,1)}), bf16[8,144,192]{2,1,0:T(8,128)(2,1)S(1)}, u32[]{:S(2)}, u32[]{:S(2)}) async-start(bf16[8,144,192]{2,1,0:T(8,128)(2,1)} %get-tuple-element.226), calls=%async_computation.6 | async-start | bytes 1179648 | tf_op jit(solution)/shard_map/all_to_all | solution.py:1173
  200.2 12.2 %collective-permute-start.38 = (bf16[288,192]{1,0:T(8,128)(2,1)}, bf16[288,192]{1,0:T(8,128)(2,1)S(1)}, u32[]{:S(2)}, u32[]{:S(2)}) collective-permute-start(bf16[288,192]{1,0:T(8,128)(2,1)} %get-tuple-element.237), channel_id=1, source_target_pairs={{0,0},{1,4},{2,1},{3,5},{4,2},{5,6},{6,3},{7,7},{8,8},{9,12},{10,9... | collective-permute-start | bytes 331784 | tf_op jit(solution)/shard_map/ppermute | solution.py:1540
  201.8 11.2 %collective-permute-start.39 = (bf16[288,192]{1,0:T(8,128)(2,1)}, bf16[288,192]{1,0:T(8,128)(2,1)S(1)}, u32[]{:S(2)}, u32[]{:S(2)}) collective-permute-start(bf16[288,192]{1,0:T(8,128)(2,1)} %get-tuple-element.238), channel_id=1, source_target_pairs={{0,4},{1,0},{2,5},{3,1},{4,6},{5,2},{6,7},{7,3},{8,12},{9,8},{10,1... | collective-permute-start | bytes 331784 | tf_op jit(solution)/shard_map/ppermute | solution.py:1541
  (49 other events, 301.2 us)
